TPU v7x, 256 devices: a whole 4x4x8 slice. The times are simulated.
256 devices in a mesh: slab: 16 (over y, z_hi), col: 16 (over x, z_lo, core).
Axes of the slice: x: 4, y: 4, z: 8 (z_hi: 4, z_lo: 2; z = z_hi * 2 + z_lo), core: 2. Of those that a mesh axis runs over, the one named last changes fastest.
Arguments:
- pressure: float32 [256, 1024, 128], P('slab', 'col'), may hold values from -6 to 6
- source: float32 [256, 1024, 128], P('slab', 'col'), may hold values from -12 to 12
- accum: float32 [256, 1024, 128], P('slab', 'col'), may hold values from 0.2 to 2
- trans_z: float32 [256, 1024, 128], P('slab', 'col'), may hold values from 0.1 to 10
- trans_x: float32 [256, 1024, 128], P('slab', 'col'), may hold values from 0.1 to 10
- trans_y: float32 [256, 1024, 128], P('slab', 'col'), may hold values from 0.1 to 10
- nnc_cell: int32 [16, 16, 16, 128], P('slab', 'col'), may hold values from 0 to 1023, as said below
- nnc_trans: float32 [16, 16, 16, 128, 128], P('slab', 'col'), may hold values from 0 to 4, as said below
- fault_cell: int32 [16, 16, 16, 128], P('slab', 'col'), may hold values from -1 to 131071, as said below
- base_stress: float32 [16, 3, 32768], P('slab', None, 'col'), may hold values from -6 to 6
- slip_start: float32 [16, 3, 32768], P('slab', None, 'col'), may hold values from -4 to 4
- stiff_diag: float32 [16, 32768], P('slab', 'col'), may hold values from 1 to 6
- active_set: int32 [2, 16, 32768], P(None, 'slab', 'col'), may hold values 0 or 1
- mortar_blocks: bfloat16 [16, 256, 4, 128, 128], P('slab', 'col'), may hold values from -0.25 to 0.25
- mortar_cols: int32 [16, 256, 4], P('slab', 'col'), may hold values from 0 to 255
Outputs:
- pressure_out: float32 [256, 1024, 128], P('slab', 'col')
- slip: float32 [16, 3, 32768], P('slab', None, 'col')
- traction: float32 [16, 3, 32768], P('slab', None, 'col')
Inputs may be any that keep to these rules, and one draw needn't show every extreme that they name: `nnc_cell`: A slot whose nnc_trans is 0 on its whole line is empty and its line is 0. No slot joins a slab to itself; between slabs 0 and 1 all 128 slots of every column are live. nnc_trans[s, c, q, k, y] equals nnc_trans[q, c, s, k, y]; on live slots every entry lies between 0.1 and 4. `fault_cell`: -1 marks an empty slot; the live slots of each (s, c, o) come first. In each slab one owner gets all 128 slots live from every source column.
All inputs are finite; a program needn't handle non-finite values. No bound on the sum of `active_set` on one device may be relied on, other than what follows from the above.
Results may differ from a plain program's by a relative error of at most 0.0017.
Values may be sent and summed in bfloat16 or wider, within the bound.
No kernel may reach another device: no remote copies, remote signals or barrier semaphores. Data moves between devices by JAX's collectives and lax.ppermute only.
A program may use at most 64 MiB of HBM per device.

v0:
```python
import jax
import jax.numpy as jnp
from jax import lax
from jax.sharding import PartitionSpec as P

ITERS_FLOW = 3
ITERS_C = 2


BIOT = 0.8
HIGHEST = lax.Precision.HIGHEST


def from_behind(block, axis, distance):
    devices = range(lax.axis_size(axis))
    route = [(i - distance, i) for i in devices if i - distance in devices]
    return lax.ppermute(block, axis, route)


def with_halo(cells, sides, width):
    for axis, dim in sides:
        count = lax.axis_size(axis)
        ends = count - 1
        head = lax.slice_in_dim(cells, 0, width, axis=dim)
        tail = lax.slice_in_dim(cells, cells.shape[dim] - width, cells.shape[dim], axis=dim)
        cells = jnp.concatenate(
            [
                lax.ppermute(tail, axis, [(i, (i + 1) % count) for i in range(ends)]),
                cells,
                lax.ppermute(head, axis, [((i + 1) % count, i) for i in range(ends)]),
            ],
            axis=dim,
        )
    return cells


def shifted(field, axis):
    shape = list(field.shape)
    shape[axis] = 1
    zero_layer = jnp.zeros(shape, jnp.float32)
    count = field.shape[axis]
    after = jnp.concatenate([lax.slice_in_dim(field, 1, count, axis=axis), zero_layer], axis)
    before = jnp.concatenate([zero_layer, lax.slice_in_dim(field, 0, count - 1, axis=axis)], axis)
    return (after, before)


def spread_rows(row_hot, values):
    return lax.dot_general(
        row_hot,
        values,
        (((0,), (0,)), ((), ())),
        precision=HIGHEST,
        preferred_element_type=jnp.float32,
    )


def per_device(
    pressure,
    source,
    accum,
    trans_z,
    trans_x,
    trans_y,
    nnc_cell,
    nnc_trans,
    fault_cell,
    base_stress,
    slip_start,
    stiff_diag,
    active_set,
    mortar_blocks,
    mortar_cols,
):
    depth, width, lateral = pressure.shape
    slabs = lax.axis_size("slab")
    columns = lax.axis_size("col")
    line_count = depth * width
    layer = lax.axis_index("slab") * depth + jnp.arange(depth, dtype=jnp.int32)
    across = lax.axis_index("col") * width + jnp.arange(width, dtype=jnp.int32)
    keep_depth = (layer < slabs * depth - 1).astype(jnp.float32)[:, None, None]
    keep_across = (across < columns * width - 1).astype(jnp.float32)[None, :, None]
    keep_along = (jnp.arange(lateral) < lateral - 1).astype(jnp.float32)[None, None, :]
    face_z = trans_z * keep_depth
    face_x = trans_x * keep_across
    face_y = trans_y * keep_along
    from_below = from_behind(face_z[-1:], "slab", 1)
    below_z = jnp.concatenate([from_below, face_z[:-1]], 0)
    from_left = from_behind(face_x[:, -1:], "col", 1)
    below_x = jnp.concatenate([from_left, face_x[:, :-1]], 1)
    below_y = jnp.concatenate([jnp.zeros((depth, width, 1), jnp.float32), face_y[:, :, :-1]], 2)
    line_ids = jnp.arange(line_count, dtype=jnp.int32)
    links = nnc_cell.reshape(-1)
    link_hot = (links[:, None] == line_ids[None, :]).astype(jnp.float32)
    conduct = nnc_trans.reshape(-1, lateral)
    nnc_diagonal = spread_rows(link_hot, conduct).reshape(pressure.shape)
    diagonal = accum + face_z + below_z + face_x + below_x + face_y + below_y + nnc_diagonal
    field = pressure
    for sweep in range(ITERS_FLOW):
        padded = with_halo(field, (("slab", 0), ("col", 1)), 1)
        neighbours = face_z * padded[2:, 1:-1] + below_z * padded[:-2, 1:-1]
        neighbours = neighbours + face_x * padded[1:-1, 2:] + below_x * padded[1:-1, :-2]
        after_y, before_y = shifted(field, 2)
        neighbours = neighbours + face_y * after_y + below_y * before_y
        outgoing = jnp.dot(
            link_hot,
            field.reshape(line_count, lateral),
            precision=HIGHEST,
            preferred_element_type=jnp.float32,
        )
        incoming = lax.all_to_all(
            outgoing.reshape(slabs, -1, lateral), "slab", split_axis=0, concat_axis=0, tiled=True
        )
        linked = spread_rows(link_hot, conduct * incoming.reshape(-1, lateral)).reshape(field.shape)
        field = (source + neighbours + linked) / diagonal
    owners = fault_cell.reshape(-1)
    valid = owners >= 0
    fault_line = jnp.where(valid, owners // lateral, -1)
    fault_lane = owners % lateral
    fault_hot = (fault_line[:, None] == line_ids[None, :]).astype(jnp.float32)
    lane_hot = (fault_lane[:, None] == jnp.arange(lateral, dtype=jnp.int32)[None, :]).astype(
        jnp.float32
    )
    fault_lines = jnp.dot(
        fault_hot,
        field.reshape(line_count, lateral),
        precision=HIGHEST,
        preferred_element_type=jnp.float32,
    )
    press_send = jnp.sum(fault_lines * lane_hot, axis=1).reshape(columns, -1)
    fault_press = lax.all_to_all(
        press_send, "col", split_axis=0, concat_axis=0, tiled=True
    ).reshape(-1)
    stress = base_stress[0]
    load = jnp.concatenate([stress[:1] - BIOT * fault_press[None], stress[1:]], 0)
    slip = slip_start[0]
    blocks = mortar_blocks[0]
    tile_cols = mortar_cols[0]
    stiffness = stiff_diag[0]
    active = active_set[:, 0].astype(jnp.float32)
    tile = blocks.shape[-1]
    traction = load
    for turn in range(ITERS_C):
        slip_half = slip.astype(jnp.bfloat16)
        whole = lax.all_gather(slip_half, "col", axis=1, tiled=True)
        tiles = whole.reshape(3, -1, tile)
        tile_ids = jnp.arange(tiles.shape[1], dtype=jnp.int32)
        chooser = (tile_cols[:, :, None] == tile_ids[None, None, :]).astype(jnp.bfloat16)
        picked = jnp.einsum(
            "rbt,ctj->crbj", chooser, tiles, preferred_element_type=jnp.float32
        ).astype(jnp.bfloat16)
        coupled = jnp.einsum(
            "rbij,crbj->cri", blocks, picked, preferred_element_type=jnp.float32
        ).reshape(3, -1)
        traction = load - coupled
        slip = slip + active[turn][None] * traction / stiffness[None]
    normal = traction[0].reshape(columns, -1)
    normal_back = lax.all_to_all(normal, "col", split_axis=0, concat_axis=0, tiled=True).reshape(-1)
    spread = jnp.where(valid, normal_back, 0.0)[:, None] * lane_hot
    returned = spread_rows(fault_hot, spread)
    pressure_out = field + returned.reshape(field.shape) / diagonal
    return (pressure_out, slip[None], traction[None])


def solution(mesh):
    return jax.shard_map(
        per_device,
        mesh=mesh,
        in_specs=(
            P("slab", "col", None),
            P("slab", "col", None),
            P("slab", "col", None),
            P("slab", "col", None),
            P("slab", "col", None),
            P("slab", "col", None),
            P("slab", "col", None, None),
            P("slab", "col", None, None, None),
            P("slab", "col", None, None),
            P("slab", None, "col"),
            P("slab", None, "col"),
            P("slab", "col"),
            P(None, "slab", "col"),
            P("slab", "col", None, None, None),
            P("slab", "col", None),
        ),
        out_specs=(P("slab", "col", None), P("slab", None, "col"), P("slab", None, "col")),
        check_vma=False,
    )
```

profile of v0, /device:TPU:25, one launch (start us, length us, event | category | flops | bytes accessed | tf_op | source)
XLA Modules:
  0.0 252.0 jit_solution(3762567243004862431)
XLA Ops:
  0.7 1.3 broadcast_multiply_fusion.2
  2.0 0.8 copy-done.10
  2.8 4.9 %collective-permute-start.1 = (f32[1,64,128]{2,1,0:T(8,128)S(1)}, f32[1,64,128]{2,1,0:T(8,128)S(1)}, u32[]{:S(2)}, u32[]{:S(2)}) collective-permute-start(f32[1,64,128]{2,1,0:T(8,128)S(1)} %slice.182), channel_id=1, source_target_pairs={{0,16},{16,32},{32,48},{48,64},{64,80},{80,96},{96,112},{112,128},... | collective-permute-start | bytes 98312 | tf_op jit(solution)/shard_map/ppermute | solution.py:17
  7.7 5.9 %fusion.15 = f32[16,128,128]{2,1,0:T(8,128)} fusion(f32[1024,128,1]{1,0,2:T(8,128)} %bitcast.170, s32[16,128]{1,0:T(8,128)} %bitcast.198), kind=kOutput, calls=%fused_computation.15 | convolution fusion | flops 3223322624 | bytes 1581056 | tf_op jit(solution)/shard_map/dot_general | solution.py:104
  13.5 9.1 %all-to-all-start = ((f32[16,128,128]{2,1,0:T(8,128)}), f32[16,128,128]{2,1,0:T(8,128)}, u32[]{:S(2)}, u32[]{:S(2)}) async-start(f32[16,128,128]{2,1,0:T(8,128)} %fusion.15), calls=%async_computation | async-start | bytes 2097152 | tf_op jit(solution)/shard_map/all_to_all | solution.py:110
  22.8 4.0 %collective-permute-start.4 = (f32[16,1,128]{2,1,0:T(1,128)S(1)}, f32[16,1,128]{2,1,0:T(1,128)S(1)}, u32[]{:S(2)}, u32[]{:S(2)}) collective-permute-start(f32[16,1,128]{2,1,0:T(1,128)S(1)} %slice.185), channel_id=1, source_target_pairs={{0,1},{1,2},{2,3},{3,4},{4,5},{5,6},{6,7},{7,8},{8,9},{9,10},{10,1... | collective-permute-start | bytes 24584 | tf_op jit(solution)/shard_map/ppermute | solution.py:17
  26.9 0.8 fusion.123
  27.7 4.0 %collective-permute-start.2 = (f32[1,64,128]{2,1,0:T(8,128)S(1)}, f32[1,64,128]{2,1,0:T(8,128)S(1)}, u32[]{:S(2)}, u32[]{:S(2)}) collective-permute-start(f32[1,64,128]{2,1,0:T(8,128)S(1)} %get-tuple-element.26), channel_id=1, source_target_pairs={{0,16},{16,32},{32,48},{48,64},{64,80},{80,96},{96,112},{112,128},... | collective-permute-start | bytes 98312 | tf_op jit(solution)/shard_map/ppermute | solution.py:28
  31.7 4.3 %collective-permute-start = (f32[1,64,128]{2,1,0:T(8,128)S(1)}, f32[1,64,128]{2,1,0:T(8,128)S(1)}, u32[]{:S(2)}, u32[]{:S(2)}) collective-permute-start(f32[1,64,128]{2,1,0:T(8,128)S(1)} %get-tuple-element.25), channel_id=1, source_target_pairs={{16,0},{32,16},{48,32},{64,48},{80,64},{96,80},{112,96},{128,112},... | collective-permute-start | bytes 98312 | tf_op jit(solution)/shard_map/ppermute | solution.py:30
  36.1 2.6 %fusion.122 = (f32[16,64,127]{2,1,0:T(8,128)}, f32[16,64,127]{2,1,0:T(8,128)}) fusion(f32[16,64,128]{2,1,0:T(8,128)} %param.15), kind=kLoop, calls=%fused_computation.175 | loop fusion | bytes 2080768 | tf_op jit(solution)/shard_map/slice | solution.py:42
  38.8 8.6 %collective-permute-done.2 = f32[1,64,128]{2,1,0:T(8,128)S(1)} collective-permute-done((f32[1,64,128]{2,1,0:T(8,128)S(1)}, f32[1,64,128]{2,1,0:T(8,128)S(1)}, u32[]{:S(2)}, u32[]{:S(2)}) %collective-permute-start.2) | collective-permute-done | bytes 32800 | tf_op jit(solution)/shard_map/ppermute | solution.py:28
  47.4 1.5 collective-permute-done
  49.0 2.8 %collective-permute-start.3 = (f32[18,1,128]{2,1,0:T(1,128)S(1)}, f32[18,1,128]{2,1,0:T(1,128)S(1)}, u32[]{:S(2)}, u32[]{:S(2)}) collective-permute-start(f32[18,1,128]{2,1,0:T(1,128)S(1)} %get-tuple-element.13), channel_id=1, source_target_pairs={{1,0},{2,1},{3,2},{4,3},{5,4},{6,5},{7,6},{8,7},{9,8},{10,9},{11,1... | collective-permute-start | bytes 27656 | tf_op jit(solution)/shard_map/ppermute | solution.py:30
  51.7 5.0 %collective-permute-start.5 = (f32[18,1,128]{2,1,0:T(1,128)S(1)}, f32[18,1,128]{2,1,0:T(1,128)S(1)}, u32[]{:S(2)}, u32[]{:S(2)}) collective-permute-start(f32[18,1,128]{2,1,0:T(1,128)S(1)} %get-tuple-element.14), channel_id=1, source_target_pairs={{0,1},{1,2},{2,3},{3,4},{4,5},{5,6},{6,7},{7,8},{8,9},{9,10},{10,1... | collective-permute-start | bytes 27656 | tf_op jit(solution)/shard_map/ppermute | solution.py:28
  56.8 4.7 %add_add_fusion = f32[16,64,128]{2,1,0:T(8,128)} fusion(f32[16,64,128]{2,1,0:T(8,128)S(1)} %broadcast_multiply_fusion, f32[16,64,128]{2,1,0:T(8,128)S(1)} %broadcast_multiply_fusion.1, f32[16,64,128]{2,1,0:T(8,128)S(1)} %copy-done.41, f32[16,64,128]{2,1,0:T(8,128)S(1)} %copy-done.11, f32[16,64,127]{2,1,0:T(8,128)S(1)} %bitcast.180, ...), kind=kOutput, calls=%fused_computation.107 | convolution fusion | flops 3224502272 | bytes 5251072 | tf_op jit(solution)/shard_map/dot_general | solution.py:48
  61.6 1.5 bitcast_multiply_fusion.2
  63.4 0.2 copy-done.25
  63.6 0.2 copy-done.29
  63.7 5.9 %fusion.53 = f32[16,64,128]{2,1,0:T(8,128)S(1)} fusion(f32[16,64,128]{2,1,0:T(8,128)S(1)} %copy-done.25, f32[2048,128,1]{1,0,2:T(8,128)S(1)} %bitcast.174, s32[16,64]{1,0:T(8,128)S(1)} %multiply_add_fusion, s32[2048]{0:T(1024)S(1)} %bitcast.201, f32[16,64,128]{2,1,0:T(8,128)} %param.16, f32[18,64,128]{2,1,0:T(8,128)} %copy-done.40, ...), kind=kOutput, calls=%fused_computation.41 | convolution fusion | flops 3225944064 | bytes 8013824 | tf_op jit(solution)/shard_map/dot_general | solution.py:48
  69.6 0.8 copy-done.7
  70.4 4.8 %fusion.13 = f32[16,128,128]{2,1,0:T(8,128)} fusion(f32[1024,128,1]{1,0,2:T(8,128)S(1)} %bitcast.172, s32[16,128]{1,0:T(8,128)S(1)} %bitcast.202), kind=kOutput, calls=%fused_computation.14 | convolution fusion | flops 3223322624 | bytes 1581056 | tf_op jit(solution)/shard_map/dot_general | solution.py:104
  75.2 6.4 %all-to-all-start.1 = ((f32[16,128,128]{2,1,0:T(8,128)}), f32[16,128,128]{2,1,0:T(8,128)}, u32[]{:S(2)}, u32[]{:S(2)}) async-start(f32[16,128,128]{2,1,0:T(8,128)} %fusion.13), calls=%async_computation.1 | async-start | bytes 2097152 | tf_op jit(solution)/shard_map/all_to_all | solution.py:110
  81.6 0.8 fusion.121
  82.5 5.6 %collective-permute-start.6 = (f32[1,64,128]{2,1,0:T(8,128)S(1)}, f32[1,64,128]{2,1,0:T(8,128)S(1)}, u32[]{:S(2)}, u32[]{:S(2)}) collective-permute-start(f32[1,64,128]{2,1,0:T(8,128)S(1)} %get-tuple-element.22), channel_id=1, source_target_pairs={{16,0},{32,16},{48,32},{64,48},{80,64},{96,80},{112,96},{128,112},... | collective-permute-start | bytes 98312 | tf_op jit(solution)/shard_map/ppermute | solution.py:30
  88.1 1.9 collective-permute-start.7
  90.1 2.4 fusion.120
  92.4 13.5 %collective-permute-done.6 = f32[1,64,128]{2,1,0:T(8,128)S(1)} collective-permute-done((f32[1,64,128]{2,1,0:T(8,128)S(1)}, f32[1,64,128]{2,1,0:T(8,128)S(1)}, u32[]{:S(2)}, u32[]{:S(2)}) %collective-permute-start.6) | collective-permute-done | bytes 32800 | tf_op jit(solution)/shard_map/ppermute | solution.py:30
  106.0 2.0 collective-permute-done.7
  108.0 2.1 collective-permute-start.8
  110.1 5.1 %collective-permute-start.9 = (f32[18,1,128]{2,1,0:T(1,128)S(1)}, f32[18,1,128]{2,1,0:T(1,128)S(1)}, u32[]{:S(2)}, u32[]{:S(2)}) collective-permute-start(f32[18,1,128]{2,1,0:T(1,128)S(1)} %get-tuple-element.12), channel_id=1, source_target_pairs={{0,1},{1,2},{2,3},{3,4},{4,5},{5,6},{6,7},{7,8},{8,9},{9,10},{10,1... | collective-permute-start | bytes 27656 | tf_op jit(solution)/shard_map/ppermute | solution.py:28
  115.3 1.5 bitcast_multiply_fusion.1
  116.9 0.2 copy-done.23
  117.1 0.2 copy-done.26
  117.4 5.5 %fusion.50 = f32[16,64,128]{2,1,0:T(8,128)S(1)} fusion(f32[16,64,128]{2,1,0:T(8,128)S(1)} %copy-done.26, f32[2048,128,1]{1,0,2:T(8,128)S(1)} %bitcast.175, s32[16,64]{1,0:T(8,128)S(1)} %multiply_add_fusion, s32[2048]{0:T(1024)S(1)} %bitcast.203, f32[16,64,128]{2,1,0:T(8,128)} %param.16, f32[18,1,128]{2,1,0:T(1,128)S(1)} %collective-permute-done.9, ...), kind=kOutput, calls=%fused_computation.40 | convolution fusion | flops 3226468352 | bytes 7424000 | tf_op jit(solution)/shard_map/dot_general | solution.py:48
  122.9 0.8 copy-done.4
  123.7 4.8 %fusion.11 = f32[16,128,128]{2,1,0:T(8,128)} fusion(f32[1024,128,1]{1,0,2:T(8,128)S(1)} %bitcast.171, s32[16,128]{1,0:T(8,128)S(1)} %bitcast.204), kind=kOutput, calls=%fused_computation.13 | convolution fusion | flops 3223322624 | bytes 1581056 | tf_op jit(solution)/shard_map/dot_general | solution.py:104
  128.5 6.6 %all-to-all-start.2 = ((f32[16,128,128]{2,1,0:T(8,128)}), f32[16,128,128]{2,1,0:T(8,128)}, u32[]{:S(2)}, u32[]{:S(2)}) async-start(f32[16,128,128]{2,1,0:T(8,128)} %fusion.11), calls=%async_computation.2 | async-start | bytes 2097152 | tf_op jit(solution)/shard_map/all_to_all | solution.py:110
  135.2 37.6 %all_gather.6 = bf16[3,32768]{1,0:T(4,128)(2,1)S(1)} all-gather(bf16[3,2048]{1,0:T(4,128)(2,1)S(1)} %bitcast.192), channel_id=1, replica_groups=mesh['slab'=16,'col'=16] {'col'}, dimensions={1}, use_global_device_ids=true | all-gather | bytes 208896 | tf_op jit(solution)/shard_map/all_gather | solution.py:144
  172.8 0.6 add_select_fusion
  173.4 0.8 fusion.119
  174.2 4.6 %collective-permute-start.10 = (f32[1,64,128]{2,1,0:T(8,128)S(1)}, f32[1,64,128]{2,1,0:T(8,128)S(1)}, u32[]{:S(2)}, u32[]{:S(2)}) collective-permute-start(f32[1,64,128]{2,1,0:T(8,128)S(1)} %get-tuple-element.18), channel_id=1, source_target_pairs={{16,0},{32,16},{48,32},{64,48},{80,64},{96,80},{112,96},{128,112},... | collective-permute-start | bytes 98312 | tf_op jit(solution)/shard_map/ppermute | solution.py:30
  178.8 2.5 collective-permute-start.11
  181.3 2.4 fusion.118
  183.7 3.0 %collective-permute-done.11 = f32[1,64,128]{2,1,0:T(8,128)S(1)} collective-permute-done((f32[1,64,128]{2,1,0:T(8,128)S(1)}, f32[1,64,128]{2,1,0:T(8,128)S(1)}, u32[]{:S(2)}, u32[]{:S(2)}) %collective-permute-start.11) | collective-permute-done | bytes 32800 | tf_op jit(solution)/shard_map/ppermute | solution.py:28
  186.7 3.3 %collective-permute-start.12 = (f32[18,1,128]{2,1,0:T(1,128)S(1)}, f32[18,1,128]{2,1,0:T(1,128)}, u32[]{:S(2)}, u32[]{:S(2)}) collective-permute-start(f32[18,1,128]{2,1,0:T(1,128)S(1)} %get-tuple-element.9), channel_id=1, source_target_pairs={{1,0},{2,1},{3,2},{4,3},{5,4},{6,5},{7,6},{8,7},{9,8},{10,9},{11,1... | collective-permute-start | bytes 27656 | tf_op jit(solution)/shard_map/ppermute | solution.py:30
  190.0 3.2 %collective-permute-start.13 = (f32[18,1,128]{2,1,0:T(1,128)S(1)}, f32[18,1,128]{2,1,0:T(1,128)}, u32[]{:S(2)}, u32[]{:S(2)}) collective-permute-start(f32[18,1,128]{2,1,0:T(1,128)S(1)} %get-tuple-element.10), channel_id=1, source_target_pairs={{0,1},{1,2},{2,3},{3,4},{4,5},{5,6},{6,7},{7,8},{8,9},{9,10},{10,1... | collective-permute-start | bytes 27656 | tf_op jit(solution)/shard_map/ppermute | solution.py:28
  193.3 1.5 bitcast_multiply_fusion
  194.9 0.2 copy-done.24
  195.4 5.6 %fusion.47 = f32[16,64,128]{2,1,0:T(8,128)S(1)} fusion(f32[16,64,128]{2,1,0:T(8,128)S(1)} %copy-done.27, f32[2048,128,1]{1,0,2:T(8,128)S(1)} %bitcast.173, s32[16,64]{1,0:T(8,128)} %copy-done.39, s32[2048]{0:T(1024)} %bitcast.199, f32[16,64,128]{2,1,0:T(8,128)} %param.16, f32[18,1,128]{2,1,0:T(1,128)} %collective-permute-done.13, ...), kind=kOutput, calls=%fused_computation.39 | convolution fusion | flops 3226468352 | bytes 7424000 | tf_op jit(solution)/shard_map/dot_general | solution.py:48
  201.1 5.4 %fusion.37 = f32[2048]{0:T(1024)} fusion(f32[1024,128]{1,0:T(8,128)S(1)} %bitcast.184, s32[2048]{0:T(1024)S(1)} %copy-done.38, s32[2048]{0:T(1024)S(1)} %get-tuple-element.33), kind=kOutput, calls=%fused_computation.35 | convolution fusion | flops 3224107008 | bytes 548864 | tf_op jit(solution)/shard_map/dot_general | solution.py:123
  206.5 4.0 %all-to-all-start.3 = ((f32[16,1,128]{2,1,0:T(1,128)}), f32[16,1,128]{2,1,0:T(1,128)S(1)}, u32[]{:S(2)}, u32[]{:S(2)}) async-start(f32[16,1,128]{2,1,0:T(1,128)} %bitcast.23), calls=%async_computation.3 | async-start | bytes 16384 | tf_op jit(solution)/shard_map/all_to_all | solution.py:130
  210.4 0.2 fusion.56
  210.7 5.2 %all-to-all-done.3 = f32[16,1,128]{2,1,0:T(1,128)S(1)} async-done(((f32[16,1,128]{2,1,0:T(1,128)}), f32[16,1,128]{2,1,0:T(1,128)S(1)}, u32[]{:S(2)}, u32[]{:S(2)}) %all-to-all-start.3) | async-done | bytes 8224 | tf_op jit(solution)/shard_map/all_to_all | solution.py:130
  215.9 0.7 fusion.108
  216.6 18.6 %all_gather.7 = bf16[3,32768]{1,0:T(4,128)(2,1)S(1)} all-gather(bf16[3,2048]{1,0:T(4,128)(2,1)S(1)} %get-tuple-element.35), channel_id=1, replica_groups=mesh['slab'=16,'col'=16] {'col'}, dimensions={1}, use_global_device_ids=true | all-gather | bytes 208896 | tf_op jit(solution)/shard_map/all_gather | solution.py:144
  235.2 0.2 fusion.57
  235.4 0.7 bitcast_subtract_fusion
  236.1 0.6 fusion.114
  236.7 3.8 %all-to-all-start.4 = ((f32[16,1,128]{2,1,0:T(1,128)}), f32[16,1,128]{2,1,0:T(1,128)S(1)}, u32[]{:S(2)}, u32[]{:S(2)}) async-start(f32[16,1,128]{2,1,0:T(1,128)} %fusion.114), calls=%async_computation.4 | async-start | bytes 16384 | tf_op jit(solution)/shard_map/all_to_all | solution.py:157
  240.5 0.6 copy.31
  241.1 0.6 copy.32
  241.8 4.2 %all-to-all-done.4 = f32[16,1,128]{2,1,0:T(1,128)S(1)} async-done(((f32[16,1,128]{2,1,0:T(1,128)}), f32[16,1,128]{2,1,0:T(1,128)S(1)}, u32[]{:S(2)}, u32[]{:S(2)}) %all-to-all-start.4) | async-done | bytes 8224 | tf_op jit(solution)/shard_map/all_to_all | solution.py:157
  245.9 4.9 %fusion.17 = f32[1024,128]{1,0:T(8,128)S(1)} fusion(s32[2048]{0:T(1024)S(1)} %copy-done.38, f32[2048]{0:T(1024)S(1)} %broadcast_select_fusion, s32[2048]{0:T(1024)S(1)} %get-tuple-element.33), kind=kOutput, calls=%fused_computation.16 | convolution fusion | flops 3225944064 | bytes 548864 | tf_op jit(solution)/shard_map/dot_general | solution.py:48
  250.9 0.9 divide_add_fusion
  (120 shorter events, 1.5 us)
Async XLA Ops:
  0.6 215.2 %copy-start = (bf16[1,16,4,128,128]{4,3,2,1,0:T(8,128)(2,1)S(1)}, bf16[1,16,4,128,128]{4,3,2,1,0:T(8,128)(2,1)}, u32[]{:S(2)}) copy-start(bf16[1,16,4,128,128]{4,3,2,1,0:T(8,128)(2,1)} %param.28) | copy-start | bytes 6291460
  2.8 54.0 %collective-permute-start.1 = (f32[1,64,128]{2,1,0:T(8,128)S(1)}, f32[1,64,128]{2,1,0:T(8,128)S(1)}, u32[]{:S(2)}, u32[]{:S(2)}) collective-permute-start(f32[1,64,128]{2,1,0:T(8,128)S(1)} %slice.182), channel_id=1, source_target_pairs={{0,16},{16,32},{32,48},{48,64},{64,80},{80,96},{96,112},{112,128},... | collective-permute-start | bytes 98312 | tf_op jit(solution)/shard_map/ppermute | solution.py:17
  7.7 15.0 %copy-start.19 = (f32[16,64,128]{2,1,0:T(8,128)S(1)}, f32[16,64,128]{2,1,0:T(8,128)}, u32[]{:S(2)}) copy-start(f32[16,64,128]{2,1,0:T(8,128)} %param.19) | copy-start | bytes 1572868
  13.5 22.4 %copy-start.20 = (f32[16,64,128]{2,1,0:T(8,128)S(1)}, f32[16,64,128]{2,1,0:T(8,128)}, u32[]{:S(2)}) copy-start(f32[16,64,128]{2,1,0:T(8,128)} %param.20) | copy-start | bytes 1572868
  13.5 48.0 %all-to-all-start = ((f32[16,128,128]{2,1,0:T(8,128)}), f32[16,128,128]{2,1,0:T(8,128)}, u32[]{:S(2)}, u32[]{:S(2)}) async-start(f32[16,128,128]{2,1,0:T(8,128)} %fusion.15), calls=%async_computation | async-start | bytes 2097152 | tf_op jit(solution)/shard_map/all_to_all | solution.py:110
  22.7 16.1 %copy-start.11 = (f32[16,64,128]{2,1,0:T(8,128)S(1)}, f32[16,64,128]{2,1,0:T(8,128)}, u32[]{:S(2)}) copy-start(f32[16,64,128]{2,1,0:T(8,128)} %copy-done.10) | copy-start | bytes 1572868
  22.8 34.0 %copy-start.15 = (f32[16,64,128]{2,1,0:T(8,128)}, f32[16,64,128]{2,1,0:T(8,128)S(1)}, u32[]{:S(2)}) copy-start(f32[16,64,128]{2,1,0:T(8,128)S(1)} %broadcast_multiply_fusion.1) | copy-start | bytes 1572868
  22.8 33.9 %collective-permute-start.4 = (f32[16,1,128]{2,1,0:T(1,128)S(1)}, f32[16,1,128]{2,1,0:T(1,128)S(1)}, u32[]{:S(2)}, u32[]{:S(2)}) collective-permute-start(f32[16,1,128]{2,1,0:T(1,128)S(1)} %slice.185), channel_id=1, source_target_pairs={{0,1},{1,2},{2,3},{3,4},{4,5},{5,6},{6,7},{7,8},{8,9},{9,10},{10,1... | collective-permute-start | bytes 24584 | tf_op jit(solution)/shard_map/ppermute | solution.py:17
  27.7 19.7 %collective-permute-start.2 = (f32[1,64,128]{2,1,0:T(8,128)S(1)}, f32[1,64,128]{2,1,0:T(8,128)S(1)}, u32[]{:S(2)}, u32[]{:S(2)}) collective-permute-start(f32[1,64,128]{2,1,0:T(8,128)S(1)} %get-tuple-element.26), channel_id=1, source_target_pairs={{0,16},{16,32},{32,48},{48,64},{64,80},{80,96},{96,112},{112,128},... | collective-permute-start | bytes 98312 | tf_op jit(solution)/shard_map/ppermute | solution.py:28
  31.7 17.3 %collective-permute-start = (f32[1,64,128]{2,1,0:T(8,128)S(1)}, f32[1,64,128]{2,1,0:T(8,128)S(1)}, u32[]{:S(2)}, u32[]{:S(2)}) collective-permute-start(f32[1,64,128]{2,1,0:T(8,128)S(1)} %get-tuple-element.25), channel_id=1, source_target_pairs={{16,0},{32,16},{48,32},{64,48},{80,64},{96,80},{112,96},{128,112},... | collective-permute-start | bytes 98312 | tf_op jit(solution)/shard_map/ppermute | solution.py:30
  36.0 11.4 %copy-start.2 = (f32[16,64,128]{2,1,0:T(8,128)S(1)}, f32[16,64,128]{2,1,0:T(8,128)}, u32[]{:S(2)}) copy-start(f32[16,64,128]{2,1,0:T(8,128)} %param.15) | copy-start | bytes 1572868
  36.1 20.7 %copy-start.21 = (f32[16,64,128]{2,1,0:T(8,128)}, f32[16,64,128]{2,1,0:T(8,128)S(1)}, u32[]{:S(2)}) copy-start(f32[16,64,128]{2,1,0:T(8,128)S(1)} %broadcast_multiply_fusion) | copy-start | bytes 1572868
  36.1 20.7 %copy-start.1 = (f32[1,1,16,128,128]{4,3,2,1,0:T(8,128)S(1)}, f32[1,1,16,128,128]{4,3,2,1,0:T(8,128)}, u32[]{:S(2)}) copy-start(f32[1,1,16,128,128]{4,3,2,1,0:T(8,128)} %param.22) | copy-start | bytes 3145732
  36.1 20.7 %copy-start.41 = (f32[16,64,128]{2,1,0:T(8,128)S(1)}, f32[16,64,128]{2,1,0:T(8,128)}, u32[]{:S(2)}) copy-start(f32[16,64,128]{2,1,0:T(8,128)} %param.17) | copy-start | bytes 1572868
  36.1 20.7 %copy-start.43 = (s32[1,1,16,128]{3,2,1,0:T(8,128)S(1)}, s32[1,1,16,128]{3,2,1,0:T(8,128)}, u32[]{:S(2)}) copy-start(s32[1,1,16,128]{3,2,1,0:T(8,128)} %param.21) | copy-start | bytes 24580
  38.7 78.1 %copy-start.39 = (s32[16,64]{1,0:T(8,128)}, s32[16,64]{1,0:T(8,128)S(1)}, u32[]{:S(2)}) copy-start(s32[16,64]{1,0:T(8,128)S(1)} %multiply_add_fusion) | copy-start | bytes 12292
  38.8 18.0 %copy-start.32 = (f32[15,64,128]{2,1,0:T(8,128)}, f32[15,64,128]{2,1,0:T(8,128)S(1)}, u32[]{:S(2)}) copy-start(f32[15,64,128]{2,1,0:T(8,128)S(1)} %slice.183) | copy-start | bytes 1474564
  49.0 7.8 %copy-start.40 = (f32[18,64,128]{2,1,0:T(8,128)}, f32[18,64,128]{2,1,0:T(8,128)S(1)}, u32[]{:S(2)}) copy-start(f32[18,64,128]{2,1,0:T(8,128)S(1)} %constant_dynamic-update-slice_fusion) | copy-start | bytes 1769476
  49.0 14.1 %collective-permute-start.3 = (f32[18,1,128]{2,1,0:T(1,128)S(1)}, f32[18,1,128]{2,1,0:T(1,128)S(1)}, u32[]{:S(2)}, u32[]{:S(2)}) collective-permute-start(f32[18,1,128]{2,1,0:T(1,128)S(1)} %get-tuple-element.13), channel_id=1, source_target_pairs={{1,0},{2,1},{3,2},{4,3},{5,4},{6,5},{7,6},{8,7},{9,8},{10,9},{11,1... | collective-permute-start | bytes 27656 | tf_op jit(solution)/shard_map/ppermute | solution.py:30
  51.7 11.4 %collective-permute-start.5 = (f32[18,1,128]{2,1,0:T(1,128)S(1)}, f32[18,1,128]{2,1,0:T(1,128)S(1)}, u32[]{:S(2)}, u32[]{:S(2)}) collective-permute-start(f32[18,1,128]{2,1,0:T(1,128)S(1)} %get-tuple-element.14), channel_id=1, source_target_pairs={{0,1},{1,2},{2,3},{3,4},{4,5},{5,6},{6,7},{7,8},{8,9},{9,10},{10,1... | collective-permute-start | bytes 27656 | tf_op jit(solution)/shard_map/ppermute | solution.py:28
  56.7 60.1 %copy-start.44 = (f32[16,1,128]{2,1,0:T(1,128)}, f32[16,1,128]{2,1,0:T(1,128)S(1)}, u32[]{:S(2)}) copy-start(f32[16,1,128]{2,1,0:T(1,128)S(1)} %collective-permute-done.4) | copy-start | bytes 24580
  56.8 60.1 %copy-start.42 = (f32[1,64,128]{2,1,0:T(8,128)}, f32[1,64,128]{2,1,0:T(8,128)S(1)}, u32[]{:S(2)}) copy-start(f32[1,64,128]{2,1,0:T(8,128)S(1)} %collective-permute-done.1) | copy-start | bytes 98308
  61.6 1.6 copy-start.3
  61.6 1.6 copy-start.12
  61.6 1.7 copy-start.16
  61.6 1.8 copy-start.22
  61.6 2.0 copy-start.25
  61.6 2.1 copy-start.29
  75.2 40.0 %all-to-all-start.1 = ((f32[16,128,128]{2,1,0:T(8,128)}), f32[16,128,128]{2,1,0:T(8,128)}, u32[]{:S(2)}, u32[]{:S(2)}) async-start(f32[16,128,128]{2,1,0:T(8,128)} %fusion.13), calls=%async_computation.1 | async-start | bytes 2097152 | tf_op jit(solution)/shard_map/all_to_all | solution.py:110
  81.6 26.3 %copy-start.8 = (f32[16,64,128]{2,1,0:T(8,128)S(1)}, f32[16,64,128]{2,1,0:T(8,128)}, u32[]{:S(2)}) copy-start(f32[16,64,128]{2,1,0:T(8,128)} %copy-done.7) | copy-start | bytes 1572868
  82.5 23.5 %collective-permute-start.6 = (f32[1,64,128]{2,1,0:T(8,128)S(1)}, f32[1,64,128]{2,1,0:T(8,128)S(1)}, u32[]{:S(2)}, u32[]{:S(2)}) collective-permute-start(f32[1,64,128]{2,1,0:T(8,128)S(1)} %get-tuple-element.22), channel_id=1, source_target_pairs={{16,0},{32,16},{48,32},{64,48},{80,64},{96,80},{112,96},{128,112},... | collective-permute-start | bytes 98312 | tf_op jit(solution)/shard_map/ppermute | solution.py:30
  88.1 19.8 %collective-permute-start.7 = (f32[1,64,128]{2,1,0:T(8,128)S(1)}, f32[1,64,128]{2,1,0:T(8,128)S(1)}, u32[]{:S(2)}, u32[]{:S(2)}) collective-permute-start(f32[1,64,128]{2,1,0:T(8,128)S(1)} %get-tuple-element.21), channel_id=1, source_target_pairs={{0,16},{16,32},{32,48},{48,64},{64,80},{80,96},{96,112},{112,128},... | collective-permute-start | bytes 98312 | tf_op jit(solution)/shard_map/ppermute | solution.py:28
  108.0 8.8 %collective-permute-start.8 = (f32[18,1,128]{2,1,0:T(1,128)S(1)}, f32[18,1,128]{2,1,0:T(1,128)S(1)}, u32[]{:S(2)}, u32[]{:S(2)}) collective-permute-start(f32[18,1,128]{2,1,0:T(1,128)S(1)} %get-tuple-element.11), channel_id=1, source_target_pairs={{1,0},{2,1},{3,2},{4,3},{5,4},{6,5},{7,6},{8,7},{9,8},{10,9},{11,1... | collective-permute-start | bytes 27656 | tf_op jit(solution)/shard_map/ppermute | solution.py:30
  110.1 6.7 %collective-permute-start.9 = (f32[18,1,128]{2,1,0:T(1,128)S(1)}, f32[18,1,128]{2,1,0:T(1,128)S(1)}, u32[]{:S(2)}, u32[]{:S(2)}) collective-permute-start(f32[18,1,128]{2,1,0:T(1,128)S(1)} %get-tuple-element.12), channel_id=1, source_target_pairs={{0,1},{1,2},{2,3},{3,4},{4,5},{5,6},{6,7},{7,8},{8,9},{9,10},{10,1... | collective-permute-start | bytes 27656 | tf_op jit(solution)/shard_map/ppermute | solution.py:28
  115.2 1.6 copy-start.9
  115.2 1.6 copy-start.13
  115.3 1.7 copy-start.17
  115.3 1.8 copy-start.23
  115.3 2.0 copy-start.26
  115.3 2.1 copy-start.31
  122.9 0.8 copy-start.4
  123.7 11.4 %copy-start.37 = (s32[2,1,2048]{2,1,0:T(1,128)S(1)}, s32[2,1,2048]{2,1,0:T(1,128)}, u32[]{:S(2)}) copy-start(s32[2,1,2048]{2,1,0:T(1,128)} %param.27) | copy-start | bytes 49156
  123.7 11.4 %copy-start.33 = (f32[1,3,2048]{2,0,1:T(1,128)S(1)}, f32[1,3,2048]{2,0,1:T(1,128)}, u32[]{:S(2)}) copy-start(f32[1,3,2048]{2,0,1:T(1,128)} %param.25) | copy-start | bytes 73732
  128.5 44.3 %copy-start.36 = (s32[1,1,16,128]{3,2,1,0:T(8,128)S(1)}, s32[1,1,16,128]{3,2,1,0:T(8,128)}, u32[]{:S(2)}) copy-start(s32[1,1,16,128]{3,2,1,0:T(8,128)} %param.23) | copy-start | bytes 24580
  128.5 64.7 %all-to-all-start.2 = ((f32[16,128,128]{2,1,0:T(8,128)}), f32[16,128,128]{2,1,0:T(8,128)}, u32[]{:S(2)}, u32[]{:S(2)}) async-start(f32[16,128,128]{2,1,0:T(8,128)} %fusion.11), calls=%async_computation.2 | async-start | bytes 2097152 | tf_op jit(solution)/shard_map/all_to_all | solution.py:110
  135.1 51.6 %copy-start.5 = (f32[16,64,128]{2,1,0:T(8,128)S(1)}, f32[16,64,128]{2,1,0:T(8,128)}, u32[]{:S(2)}) copy-start(f32[16,64,128]{2,1,0:T(8,128)} %copy-done.4) | copy-start | bytes 1572868
  174.2 9.5 %collective-permute-start.10 = (f32[1,64,128]{2,1,0:T(8,128)S(1)}, f32[1,64,128]{2,1,0:T(8,128)S(1)}, u32[]{:S(2)}, u32[]{:S(2)}) collective-permute-start(f32[1,64,128]{2,1,0:T(8,128)S(1)} %get-tuple-element.18), channel_id=1, source_target_pairs={{16,0},{32,16},{48,32},{64,48},{80,64},{96,80},{112,96},{128,112},... | collective-permute-start | bytes 98312 | tf_op jit(solution)/shard_map/ppermute | solution.py:30
  178.8 7.9 %collective-permute-start.11 = (f32[1,64,128]{2,1,0:T(8,128)S(1)}, f32[1,64,128]{2,1,0:T(8,128)S(1)}, u32[]{:S(2)}, u32[]{:S(2)}) collective-permute-start(f32[1,64,128]{2,1,0:T(8,128)S(1)} %get-tuple-element.17), channel_id=1, source_target_pairs={{0,16},{16,32},{32,48},{48,64},{64,80},{80,96},{96,112},{112,128},... | collective-permute-start | bytes 98312 | tf_op jit(solution)/shard_map/ppermute | solution.py:28
  186.7 8.1 %collective-permute-start.12 = (f32[18,1,128]{2,1,0:T(1,128)S(1)}, f32[18,1,128]{2,1,0:T(1,128)}, u32[]{:S(2)}, u32[]{:S(2)}) collective-permute-start(f32[18,1,128]{2,1,0:T(1,128)S(1)} %get-tuple-element.9), channel_id=1, source_target_pairs={{1,0},{2,1},{3,2},{4,3},{5,4},{6,5},{7,6},{8,7},{9,8},{10,9},{11,1... | collective-permute-start | bytes 27656 | tf_op jit(solution)/shard_map/ppermute | solution.py:30
  190.0 4.8 %collective-permute-start.13 = (f32[18,1,128]{2,1,0:T(1,128)S(1)}, f32[18,1,128]{2,1,0:T(1,128)}, u32[]{:S(2)}, u32[]{:S(2)}) collective-permute-start(f32[18,1,128]{2,1,0:T(1,128)S(1)} %get-tuple-element.10), channel_id=1, source_target_pairs={{0,1},{1,2},{2,3},{3,4},{4,5},{5,6},{6,7},{7,8},{8,9},{9,10},{10,1... | collective-permute-start | bytes 27656 | tf_op jit(solution)/shard_map/ppermute | solution.py:28
  193.2 1.6 copy-start.6
  193.3 1.6 copy-start.14
  193.3 1.7 copy-start.18
  193.3 1.8 copy-start.24
  193.3 2.0 copy-start.27
  193.3 2.1 copy-start.30
  195.4 5.6 %copy-start.38 = (s32[2048]{0:T(1024)S(1)}, s32[2048]{0:T(1024)}, u32[]{:S(2)}) copy-start(s32[2048]{0:T(1024)} %get-tuple-element.34) | copy-start | bytes 24580
  201.0 9.4 %copy-start.45 = (s32[1,16,4]{1,2,0:T(4,128)S(1)}, s32[1,16,4]{1,2,0:T(4,128)}, u32[]{:S(2)}) copy-start(s32[1,16,4]{1,2,0:T(4,128)} %param.29) | copy-start | bytes 772
  201.1 9.6 %slice-start = ((f32[1,3,2048]{2,0,1:T(1,128)}), f32[1,2,2048]{2,0,1:T(1,128)S(1)}, s32[]{:S(2)}) async-start(f32[1,3,2048]{2,0,1:T(1,128)} %param.24), calls=%async_computation.5 | async-start | bytes 32768 | tf_op jit(solution)/shard_map/slice | solution.py:134
  201.1 14.8 %copy-start.34 = (f32[1,3,2048]{2,0,1:T(1,128)S(1)}, f32[1,3,2048]{2,0,1:T(1,128)}, u32[]{:S(2)}) copy-start(f32[1,3,2048]{2,0,1:T(1,128)} %param.24) | copy-start | bytes 73732
  201.1 14.8 %copy-start.35 = (f32[1,2048]{1,0:T(1,128)S(1)}, f32[1,2048]{1,0:T(1,128)}, u32[]{:S(2)}) copy-start(f32[1,2048]{1,0:T(1,128)} %param.26) | copy-start | bytes 24580
  206.5 9.4 %all-to-all-start.3 = ((f32[16,1,128]{2,1,0:T(1,128)}), f32[16,1,128]{2,1,0:T(1,128)S(1)}, u32[]{:S(2)}, u32[]{:S(2)}) async-start(f32[16,1,128]{2,1,0:T(1,128)} %bitcast.23), calls=%async_computation.3 | async-start | bytes 16384 | tf_op jit(solution)/shard_map/all_to_all | solution.py:130
  236.7 9.2 %all-to-all-start.4 = ((f32[16,1,128]{2,1,0:T(1,128)}), f32[16,1,128]{2,1,0:T(1,128)S(1)}, u32[]{:S(2)}, u32[]{:S(2)}) async-start(f32[16,1,128]{2,1,0:T(1,128)} %fusion.114), calls=%async_computation.4 | async-start | bytes 16384 | tf_op jit(solution)/shard_map/all_to_all | solution.py:157
  245.9 4.9 %copy-start.28 = (f32[16,64,128]{2,1,0:T(8,128)S(1)}, f32[16,64,128]{2,1,0:T(8,128)}, u32[]{:S(2)}) copy-start(f32[16,64,128]{2,1,0:T(8,128)} %add_add_fusion) | copy-start | bytes 1572868
  (2 other events, 1.6 us)
where the time goes:
time: 257 us; the launch traced here: 252 us
  starting transfers between devices  83.2 us (32%)
  blocking collectives  56.2 us (22%)
  matrix products  49.2 us (19%)
  waiting for transfers between devices  38.1 us (15%)
  local copies, waits for them, and re-layouts  15.4 us (6%)
  other arithmetic  8.15 us (3%)
    all_gather x2, blocking collectives, per_device(): whole = lax.all_gather(slip_half, 'col', axis=1, tiled=True)  56.2 us
    dot_general x5, matrix products, spread_rows(): lax.dot_general(row_hot, values, (((0,), (0,)), ((), ())), precision=HIGH...  26.7 us
    ppermute x6, starting transfers between devices, with_halo(): lax.ppermute(head, axis, [((i + 1) % count, i) for i in range(ends)])  22.7 us
    all_to_all x3, starting transfers between devices, per_device(): lax.all_to_all(outgoing.reshape(slabs, -1, lateral), 'slab', split_axis=0...  22.2 us
    ppermute x6, starting transfers between devices, with_halo(): lax.ppermute(tail, axis, [(i, (i + 1) % count) for i in range(ends)])  21.7 us
    dot_general x3, matrix products, per_device(): jnp.dot(link_hot, field.reshape(line_count, lateral), precision=HIGHEST,...  15.4 us
    ppermute x6, waiting for transfers between devices, with_halo(): lax.ppermute(head, axis, [((i + 1) % count, i) for i in range(ends)])  15.1 us
    ppermute x6, waiting for transfers between devices, with_halo(): lax.ppermute(tail, axis, [(i, (i + 1) % count) for i in range(ends)])  13.6 us
  transfers between devices with their start and end apart: 19, of which 7 were waited for; matrix products, arithmetic and copies ran while one was open for 11% of the time, Pallas kernels for 0%

commit v1 on v0

v1 whole, which is shorter than its diff:
```python
import functools

import jax
import jax.numpy as jnp
from jax import lax
from jax.experimental import pallas as pl
from jax.experimental.pallas import tpu as pltpu
from jax.sharding import PartitionSpec as P

ITERS_FLOW = 3
BIOT = 0.8
F32 = jnp.float32
BF16 = jnp.bfloat16
NT = (((1,), (1,)), ((), ()))


def call(body, outs, *args, smem=(), scratch=(), mib=40):
    ins = [
        pl.BlockSpec(memory_space=pltpu.SMEM if i in smem else pltpu.VMEM)
        for i in range(len(args))
    ]
    return pl.pallas_call(
        body,
        in_specs=ins,
        out_specs=[pl.BlockSpec(memory_space=pltpu.VMEM) for _ in outs],
        out_shape=[jax.ShapeDtypeStruct(s, d) for s, d in outs],
        scratch_shapes=list(scratch),
        compiler_params=pltpu.CompilerParams(vmem_limit_bytes=mib << 20),
    )(*args)


def iota(shape, dim):
    return lax.broadcasted_iota(jnp.int32, shape, dim)


def halves(x):
    high = x.astype(BF16)
    return high, (x - high.astype(F32)).astype(BF16)


def fill_hot(hot_ref, lines):
    rows = hot_ref.shape[0]
    ids = iota((rows, 128), 0)
    for q in range(lines.shape[0]):
        hit = ids == lines[q : q + 1, :]
        hot_ref[:, q * 128 : (q + 1) * 128] = jnp.where(hit, 1.0, 0.0).astype(BF16)


def gather_lines(hot_ref, field, out_ref):
    turned = field.T.astype(BF16)
    for q in range(0, out_ref.shape[0], 2):
        got = jnp.dot(
            turned, hot_ref[:, q * 128 : (q + 2) * 128], preferred_element_type=F32
        ).astype(BF16)
        out_ref[q] = got[:, :128]
        out_ref[q + 1] = got[:, 128:]


def scatter_lines(hot_ref, values_ref):
    both = lax.dot_general(hot_ref[...], values_ref[...], NT, preferred_element_type=F32)
    return both[:, :128] + both[:, 128:]


def put_halves(values_ref, q, values):
    high, low = halves(values)
    values_ref[:128, q * 128 : (q + 1) * 128] = high
    values_ref[128:, q * 128 : (q + 1) * 128] = low


def first_kernel(field_ref, cell_ref, hot_ref, out_ref):
    depth, width, lateral = field_ref.shape
    fill_hot(hot_ref, cell_ref[...])
    gather_lines(hot_ref, field_ref[...].reshape(depth * width, lateral), out_ref)


def edges_kernel(
    field_ref, face_z_ref, face_x_ref, up_ref, down_ref, right_ref, left_ref
):
    depth, width, _ = field_ref.shape
    up_ref[0] = field_ref[depth - 1]
    up_ref[1] = face_z_ref[depth - 1]
    down_ref[...] = field_ref[0]
    for i in range(depth):
        right_ref[0, i : i + 1, :] = field_ref[i, width - 1 : width, :]
        right_ref[1, i : i + 1, :] = face_x_ref[i, width - 1 : width, :]
        left_ref[i : i + 1, :] = field_ref[i, 0:1, :]


def setup_kernel(
    ends_ref,
    accum_ref,
    face_z_ref,
    face_x_ref,
    face_y_ref,
    hot_ref,
    conduct_ref,
    fault_ref,
    turned_ref,
    partial_ref,
    fault_hot_ref,
    values_ref,
):
    depth, width, lateral = accum_ref.shape
    for q in range(conduct_ref.shape[0]):
        turned = conduct_ref[q].T
        turned_ref[q] = turned
        put_halves(values_ref, q, turned)
    linked = scatter_lines(hot_ref, values_ref)
    last_z = ends_ref[0] != 0
    last_x = ends_ref[1] != 0
    across = iota((width, lateral), 0)
    along = iota((width, lateral), 1)
    for i in range(depth):
        total = accum_ref[i] + linked[i * width : (i + 1) * width]
        own_z = face_z_ref[i]
        if i == depth - 1:
            own_z = jnp.where(last_z, 0.0, own_z)
        total = total + own_z
        if i > 0:
            total = total + face_z_ref[i - 1]
        own_x = face_x_ref[i]
        total = total + jnp.where((across == width - 1) & last_x, 0.0, own_x)
        total = total + jnp.where(across == 0, 0.0, pltpu.roll(own_x, 1, 0))
        own_y = jnp.where(along == lateral - 1, 0.0, face_y_ref[i])
        partial_ref[i] = total + own_y + pltpu.roll(own_y, 1, 1)
    fill_hot(fault_hot_ref, fault_ref[...] >> 7)


def sweep_kernel(
    first,
    last,
    incoming_ref,
    turned_ref,
    hot_ref,
    field_ref,
    source_ref,
    diag_ref,
    face_z_ref,
    face_x_ref,
    face_y_ref,
    below_ref,
    above_ref,
    behind_ref,
    ahead_ref,
    lower_z_ref,
    lower_x_ref,
    *refs,
):
    depth, width, lateral = field_ref.shape
    refs = list(refs)
    values_ref = refs.pop()
    fault_ref, fault_hot_ref = (refs.pop(0), refs.pop(0)) if last else (None, None)
    new_ref = refs.pop(0)
    inverse_ref = refs.pop(0) if first else diag_ref
    for q in range(incoming_ref.shape[0]):
        put_halves(values_ref, q, turned_ref[q] * incoming_ref[q].astype(F32))
    linked = scatter_lines(hot_ref, values_ref)
    across = iota((width, lateral), 0)
    along = iota((width, lateral), 1)
    for i in range(depth):
        field = field_ref[i]
        face_z = face_z_ref[i]
        lower_z = face_z_ref[i - 1] if i > 0 else lower_z_ref[...]
        above = field_ref[i + 1] if i < depth - 1 else above_ref[...]
        below = field_ref[i - 1] if i > 0 else below_ref[...]
        total = source_ref[i] + linked[i * width : (i + 1) * width]
        total = total + face_z * above + lower_z * below
        face_x = face_x_ref[i]
        lower_x = lower_x_ref[i : i + 1, :]
        ahead = jnp.where(
            across == width - 1, ahead_ref[i : i + 1, :], pltpu.roll(field, width - 1, 0)
        )
        flow = jnp.where(
            across == 0,
            lower_x * behind_ref[i : i + 1, :],
            pltpu.roll(face_x * field, 1, 0),
        )
        total = total + face_x * ahead + flow
        face_y = jnp.where(along == lateral - 1, 0.0, face_y_ref[i])
        total = total + face_y * pltpu.roll(field, lateral - 1, 1)
        total = total + pltpu.roll(face_y * field, 1, 1)
        if first:
            whole = diag_ref[i] + jnp.where(across == 0, lower_x, 0.0)
            if i == 0:
                whole = whole + lower_z
            inverse = 1.0 / whole
            inverse_ref[i] = inverse
        else:
            inverse = diag_ref[i]
        new_ref[i] = total * inverse
    lines = new_ref[...].reshape(depth * width, lateral)
    if last:
        (press_ref,) = refs
        high, low = halves(lines.T)
        both = jnp.concatenate([high, low], 0)
        side = iota((lateral, 128), 0)
        for q in range(fault_ref.shape[0]):
            got = jnp.dot(
                both, fault_hot_ref[:, q * 128 : (q + 1) * 128], preferred_element_type=F32
            )
            got = got[:lateral] + got[lateral:]
            lane = fault_ref[q : q + 1, :] & 127
            got = jnp.sum(jnp.where(side == lane, got, 0.0), 0, keepdims=True)
            press_ref[0, q : q + 1, :] = got
        mine = press_ref[0]
        for o in range(1, press_ref.shape[0]):
            press_ref[o] = mine
    else:
        out_ref, up_ref, down_ref, right_ref, left_ref = refs
        gather_lines(hot_ref, lines, out_ref)
        up_ref[...] = new_ref[depth - 1]
        down_ref[...] = new_ref[0]
        for i in range(depth):
            right_ref[i : i + 1, :] = new_ref[i, width - 1 : width, :]
            left_ref[i : i + 1, :] = new_ref[i, 0:1, :]


def couple(select, tiles, blocks_ref):
    rows, per = blocks_ref.shape[:2]
    picked = [jnp.dot(select, t, preferred_element_type=F32) for t in tiles]
    ids = iota((rows, 128), 0)
    total = None
    for r in range(rows):
        for b in range(per):
            n = r * per + b
            left = [jnp.where(ids == r, p[n : n + 1, :], 0.0) for p in picked]
            left = (jnp.concatenate(left, 0) if len(left) > 1 else left[0]).astype(BF16)
            part = lax.dot_general(left, blocks_ref[r, b], NT, preferred_element_type=F32)
            total = part if total is None else total + part
    return total


def contact_one_kernel(
    whole_ref,
    cols_ref,
    blocks_ref,
    base_ref,
    slip_ref,
    stiff_ref,
    active_ref,
    packed_ref,
    own_ref,
):
    owners = whole_ref.shape[0]
    rows = base_ref.shape[1]
    ids = owners * rows
    select = jnp.where(iota((cols_ref.shape[0], ids), 1) == cols_ref[...], 1.0, 0.0)
    tiles = [
        whole_ref[:, p * rows : (p + 1) * rows, :].reshape(ids, 128) for p in range(3)
    ]
    coupled = couple(select.astype(BF16), tiles, blocks_ref)
    gain = active_ref[...].astype(F32) / stiff_ref[...]
    parts = [
        slip_ref[p] + gain * (base_ref[p] - coupled[p * rows : (p + 1) * rows])
        for p in range(3)
    ]
    mine = jnp.concatenate([parts[0], -BIOT * gain, parts[1], parts[2]], 0)
    own_ref[...] = mine
    for o in range(owners):
        packed_ref[o] = mine


def contact_two_kernel(
    whole_ref, cols_ref, blocks_ref, base_ref, own_ref, stiff_ref, active_ref, done_ref
):
    owners = whole_ref.shape[0]
    rows = base_ref.shape[1]
    ids = owners * rows
    select = jnp.where(iota((cols_ref.shape[0], ids), 1) == cols_ref[...], 1.0, 0.0)
    tiles = [
        whole_ref[:, p * rows : (p + 1) * rows, :].reshape(ids, 128).astype(BF16)
        for p in (2, 3)
    ]
    coupled = couple(select.astype(BF16), tiles, blocks_ref)
    gain = active_ref[...].astype(F32) / stiff_ref[...]
    for p in (1, 2):
        traction = base_ref[p] - coupled[(p - 1) * rows : p * rows]
        done_ref[p - 1] = own_ref[(p + 1) * rows : (p + 2) * rows] + gain * traction
        done_ref[p + 1] = traction


def tail_kernel(
    me_ref,
    press_ref,
    slope_ref,
    cols_ref,
    blocks_ref,
    base_ref,
    own_ref,
    stiff_ref,
    active_ref,
    done_ref,
    normal_ref,
    slip_ref,
    traction_ref,
):
    sources, owners, _ = press_ref.shape
    rows = base_ref.shape[1]
    ids = sources * owners
    press = press_ref[...]
    slips = slope_ref[0] + slope_ref[1] * press
    select = jnp.where(iota((cols_ref.shape[0], ids), 1) == cols_ref[...], 1.0, 0.0)
    tiles = [slips.reshape(ids, 128).astype(BF16)]
    coupled = couple(select.astype(BF16), tiles, blocks_ref)
    mine = jnp.where(iota(press.shape, 1) == me_ref[0], press, 0.0)
    mine = jnp.sum(mine, 1)
    slip = own_ref[:rows] + own_ref[rows : 2 * rows] * mine
    traction = base_ref[0] - BIOT * mine - coupled
    normal_ref[...] = traction
    traction_ref[0] = traction
    slip_ref[0] = slip + active_ref[...].astype(F32) / stiff_ref[...] * traction
    for p in (1, 2):
        slip_ref[p] = done_ref[p - 1]
        traction_ref[p] = done_ref[p + 1]


def back_kernel(
    normal_ref, fault_ref, fault_hot_ref, field_ref, inverse_ref, out_ref, values_ref
):
    depth, width, lateral = field_ref.shape
    side = iota((lateral, 128), 0)
    for q in range(normal_ref.shape[0]):
        lane = fault_ref[q : q + 1, :] & 127
        put_halves(values_ref, q, jnp.where(side == lane, normal_ref[q : q + 1, :], 0.0))
    returned = scatter_lines(fault_hot_ref, values_ref).reshape(depth, width, lateral)
    out_ref[...] = field_ref[...] + returned * inverse_ref[...]


def shift(block, axis, step):
    count = lax.axis_size(axis)
    route = [(i, i + step) for i in range(count) if 0 <= i + step < count]
    return lax.ppermute(block, axis, route)


def swap(blocks, axis):
    return lax.all_to_all(blocks, axis, split_axis=0, concat_axis=0, tiled=True)


def per_device(
    pressure,
    source,
    accum,
    trans_z,
    trans_x,
    trans_y,
    nnc_cell,
    nnc_trans,
    fault_cell,
    base_stress,
    slip_start,
    stiff_diag,
    active_set,
    mortar_blocks,
    mortar_cols,
):
    depth, width, lateral = pressure.shape
    slabs = lax.axis_size("slab")
    columns = lax.axis_size("col")
    lines = depth * width
    grid = ((depth, width, lateral), F32)
    slots = slabs * 128
    nodes = columns * 128
    rows = mortar_blocks.shape[1]
    cells = nnc_cell[0, 0]
    faults = fault_cell[0, 0]
    blocks = mortar_blocks[0]
    tile_cols = mortar_cols[0].reshape(-1, 1)
    turned_cols = tile_cols % columns * columns + tile_cols // columns
    base = base_stress[0].reshape(3, rows, 128)
    slip0 = slip_start[0].reshape(3, rows, 128)
    stiff = stiff_diag[0].reshape(rows, 128)
    active = active_set[:, 0].reshape(-1, rows, 128)
    me = lax.axis_index("col")
    last_z = lax.axis_index("slab") == slabs - 1
    ends = jnp.stack([last_z, me == columns - 1]).astype(jnp.int32)
    whole_values = pltpu.VMEM((2 * lateral, slots), BF16)

    layer = ((width, lateral), F32)
    wall = ((depth, lateral), F32)
    hot, outgoing = call(
        first_kernel,
        [((lines, slots), BF16), ((slabs, lateral, 128), BF16)],
        pressure,
        cells,
    )
    incoming = swap(outgoing, "slab")
    up, down, right, left = call(
        edges_kernel,
        [((2, *layer[0]), F32), layer, ((2, *wall[0]), F32), wall],
        pressure,
        trans_z,
        trans_x,
    )
    up = shift(up, "slab", 1)
    right = shift(right, "col", 1)
    below, lower_z = up[0], up[1]
    behind, lower_x = right[0], right[1]
    above = shift(down, "slab", -1)
    ahead = shift(left, "col", -1)
    turned, diag, fault_hot = call(
        setup_kernel,
        [((slabs, lateral, 128), F32), grid, ((lines, nodes), BF16)],
        ends,
        accum,
        trans_z,
        trans_x,
        trans_y,
        hot,
        nnc_trans[0, 0],
        faults,
        smem=(0,),
        scratch=(whole_values,),
    )

    slip_half = slip0.astype(BF16).reshape(1, 3 * rows, 128)
    whole = swap(jnp.broadcast_to(slip_half, (columns, 3 * rows, 128)), "col")
    packed, own = call(
        contact_one_kernel,
        [((columns, 4 * rows, 128), F32), ((4 * rows, 128), F32)],
        whole,
        tile_cols,
        blocks,
        base,
        slip0,
        stiff,
        active[0],
    )
    packed = swap(packed, "col")
    (done,) = call(
        contact_two_kernel,
        [((4, rows, 128), F32)],
        packed,
        tile_cols,
        blocks,
        base,
        own,
        stiff,
        active[1],
    )
    slope = packed[:, : 2 * rows].reshape(columns, 2, rows, 128).transpose(1, 2, 0, 3)

    field = pressure
    for sweep in range(ITERS_FLOW):
        first = sweep == 0
        last = sweep == ITERS_FLOW - 1
        extra = [faults, fault_hot] if last else []
        outs = [grid] + ([grid] if first else [])
        if last:
            outs += [((columns, columns, 128), F32)]
        else:
            outs += [((slabs, lateral, 128), BF16), layer, layer, wall, wall]
        got = list(call(
            functools.partial(sweep_kernel, first, last),
            outs,
            incoming,
            turned,
            hot,
            field,
            source,
            diag,
            trans_z,
            trans_x,
            trans_y,
            below,
            above,
            behind,
            ahead,
            lower_z,
            lower_x,
            *extra,
            scratch=(whole_values,),
        ))
        field = got.pop(0)
        if first:
            diag = got.pop(0)
        if not last:
            incoming = swap(got[0], "slab")
            below = shift(got[1], "slab", 1)
            behind = shift(got[3], "col", 1)
            above = shift(got[2], "slab", -1)
            ahead = shift(got[4], "col", -1)
    press = swap(got[0], "col")
    normal, slip, traction = call(
        tail_kernel,
        [((rows, 128), F32), ((3, rows, 128), F32), ((3, rows, 128), F32)],
        me.reshape(1).astype(jnp.int32),
        press,
        slope,
        turned_cols,
        blocks,
        base,
        own,
        stiff,
        active[1],
        done,
        smem=(0,),
    )
    normal = swap(normal.reshape(columns, -1, 128), "col").reshape(columns, 128)
    (pressure_out,) = call(
        back_kernel,
        [grid],
        normal,
        faults,
        fault_hot,
        field,
        diag,
        scratch=(pltpu.VMEM((2 * lateral, nodes), BF16),),
    )
    return (pressure_out, slip.reshape(1, 3, -1), traction.reshape(1, 3, -1))


def solution(mesh):
    return jax.shard_map(
        per_device,
        mesh=mesh,
        in_specs=(
            P("slab", "col", None),
            P("slab", "col", None),
            P("slab", "col", None),
            P("slab", "col", None),
            P("slab", "col", None),
            P("slab", "col", None),
            P("slab", "col", None, None),
            P("slab", "col", None, None, None),
            P("slab", "col", None, None),
            P("slab", None, "col"),
            P("slab", None, "col"),
            P("slab", "col"),
            P(None, "slab", "col"),
            P("slab", "col", None, None, None),
            P("slab", "col", None),
        ),
        out_specs=(P("slab", "col", None), P("slab", None, "col"), P("slab", None, "col")),
        check_vma=False,
    )
```

time: 257 us -> 222 us (0.86)
  the two profiles are of different devices: /device:TPU:25 before, /device:TPU:9 now
where the time goes in v1:
time: 222 us; the launch traced here: 219 us
  starting transfers between devices  85.1 us (38%)
  local copies, waits for them, and re-layouts  55.7 us (25%)
  waiting for transfers between devices  37.5 us (17%)
  Pallas kernels  31 us (14%)
  blocking collectives  8.6 us (4%)
    unnamed x115, local copies, waits for them, and re-layouts  53 us
    ppermute x12, starting transfers between devices, shift(): return lax.ppermute(block, axis, route)  43.2 us
    all_to_all x6, starting transfers between devices, swap(): return lax.all_to_all(blocks, axis, split_axis=0, concat_axis=0, tiled=True)  42 us
    all_to_all x6, waiting for transfers between devices, swap(): return lax.all_to_all(blocks, axis, split_axis=0, concat_axis=0, tiled=True)  31.4 us
    pallas_call x10, Pallas kernels, call(): pl.pallas_call(body, in_specs=ins, out_specs=[pl.BlockSpec(memory_space=p...  31 us
    all_to_all x1, blocking collectives, swap(): return lax.all_to_all(blocks, axis, split_axis=0, concat_axis=0, tiled=True)  8.6 us
    ppermute x12, waiting for transfers between devices, shift(): return lax.ppermute(block, axis, route)  6.12 us
  transfers between devices with their start and end apart: 18, of which 5 were waited for; matrix products, arithmetic and copies ran while one was open for 1% of the time, Pallas kernels for 9%

profile of v1, /device:TPU:9, one launch (start us, length us, event | category | flops | bytes accessed | tf_op | source)
XLA Modules:
  0.0 219.1 jit_solution(3080076697215973466)
XLA Ops:
  0.6 1.0 copy-done.25
  2.4 2.8 %shard_map.166 = (bf16[1024,2048]{1,0:T(8,128)(2,1)S(1)}, bf16[16,128,128]{2,1,0:T(8,128)(2,1)}) custom-call(f32[16,64,128]{2,1,0:T(8,128)S(1)} %copy-done.25, s32[16,128]{1,0:T(8,128)S(1)} %bitcast.48), custom_call_target="tpu_custom_call" | custom-call | tf_op jit(solution)/shard_map/pallas_call | solution.py:22
  5.2 2.0 copy-done
  7.3 11.1 %all-to-all-start = ((bf16[16,128,128]{2,1,0:T(8,128)(2,1)}), bf16[16,128,128]{2,1,0:T(8,128)(2,1)}, u32[]{:S(2)}, u32[]{:S(2)}) async-start(bf16[16,128,128]{2,1,0:T(8,128)(2,1)} %get-tuple-element.32), calls=%async_computation | async-start | bytes 1048576 | tf_op jit(solution)/shard_map/all_to_all | solution.py:336
  18.4 1.0 copy-done.9
  19.4 1.0 copy-done.12
  20.5 1.0 copy-done.26
  21.5 4.1 %collective-permute-start = (f32[2,64,128]{2,1,0:T(8,128)S(1)}, f32[2,64,128]{2,1,0:T(8,128)S(1)}, u32[]{:S(2)}, u32[]{:S(2)}) collective-permute-start(f32[2,64,128]{2,1,0:T(8,128)S(1)} %get-tuple-element.36), channel_id=1, source_target_pairs={{0,16},{16,32},{32,48},{48,64},{64,80},{80,96},{96,112},{112,128},... | collective-permute-start | bytes 196616 | tf_op jit(solution)/shard_map/ppermute | solution.py:332
  25.7 4.0 %collective-permute-start.2 = (f32[2,16,128]{2,1,0:T(8,128)S(1)}, f32[2,16,128]{2,1,0:T(8,128)S(1)}, u32[]{:S(2)}, u32[]{:S(2)}) collective-permute-start(f32[2,16,128]{2,1,0:T(8,128)S(1)} %get-tuple-element.38), channel_id=1, source_target_pairs={{0,1},{1,2},{2,3},{3,4},{4,5},{5,6},{6,7},{7,8},{8,9},{9,10},{10,1... | collective-permute-start | bytes 49160 | tf_op jit(solution)/shard_map/ppermute | solution.py:332
  29.7 4.3 %collective-permute-start.1 = (f32[64,128]{1,0:T(8,128)S(1)}, f32[64,128]{1,0:T(8,128)S(1)}, u32[]{:S(2)}, u32[]{:S(2)}) collective-permute-start(f32[64,128]{1,0:T(8,128)S(1)} %get-tuple-element.37), channel_id=1, source_target_pairs={{16,0},{32,16},{48,32},{64,48},{80,64},{96,80},{112,96},{128,112},... | collective-permute-start | bytes 98312 | tf_op jit(solution)/shard_map/ppermute | solution.py:332
  34.0 1.9 collective-permute-start.3
  36.1 2.2 copy-done.1
  38.2 1.0 copy-done.10
  39.3 1.0 copy-done.13
  40.3 1.0 copy-done.18
  41.4 1.2 copy-done.34
  42.6 1.0 copy-done.35
  44.3 4.4 %shard_map.167 = (f32[16,128,128]{2,1,0:T(8,128)S(1)}, f32[16,64,128]{2,1,0:T(8,128)S(1)}, bf16[1024,2048]{1,0:T(8,128)(2,1)S(1)}) custom-call(s32[2]{0:T(128)S(1)} %add_convert_fusion.ends_ref, f32[16,64,128]{2,1,0:T(8,128)S(1)} %copy-done.35, f32[16,64,128]{2,1,0:T(8,128)S(1)} %copy-done.10, f32[16,64,128]{2,1,0:T(8,128)S(1)} %copy-done.13, ...), custom_call_target="tpu_custom_call" | custom-call | tf_op jit(solution)/shard_map/pallas_call | solution.py:22
  48.8 2.0 copy-done.6
  51.7 2.5 %copy-done.2 = bf16[1024,2048]{1,0:T(8,128)(2,1)S(1)} copy-done((bf16[1024,2048]{1,0:T(8,128)(2,1)S(1)}, bf16[1024,2048]{1,0:T(8,128)(2,1)}, u32[]{:S(2)}) %copy-start.2) | copy-done | bytes 4194328
  54.2 1.0 copy-done.27
  55.2 1.0 copy-done.41
  56.2 4.4 %shard_map.169 = (f32[16,64,128]{2,1,0:T(8,128)S(1)}, f32[16,64,128]{2,1,0:T(8,128)S(1)}, bf16[16,128,128]{2,1,0:T(8,128)(2,1)S(1)}, f32[64,128]{1,0:T(8,128)S(1...) custom-call(bf16[16,128,128]{2,1,0:T(8,128)(2,1)} %all-to-all-done.incoming_ref, ...), custom_call_target="tpu_custom_call" | custom-call | tf_op jit(solution)/shard_map/pallas_call | solution.py:22
  63.7 8.2 %all-to-all-start.1 = ((bf16[16,128,128]{2,1,0:T(8,128)(2,1)}), bf16[16,128,128]{2,1,0:T(8,128)(2,1)S(1)}, u32[]{:S(2)}, u32[]{:S(2)}) async-start(bf16[16,128,128]{2,1,0:T(8,128)(2,1)} %copy-done.44), calls=%async_computation.1 | async-start | bytes 1048576 | tf_op jit(solution)/shard_map/all_to_all | solution.py:336
  72.0 16.5 %all-to-all-done.1.incoming_ref = bf16[16,128,128]{2,1,0:T(8,128)(2,1)S(1)} async-done(((bf16[16,128,128]{2,1,0:T(8,128)(2,1)}), bf16[16,128,128]{2,1,0:T(8,128)(2,1)S(1)}, u32[]{:S(2)}, u32[]{:S(2)}) %all-to-all-start.1) | async-done | bytes 524320 | tf_op jit(solution)/shard_map/all_to_all | solution.py:336
  89.2 6.0 %all-to-all-start.4 = ((bf16[16,48,128]{2,1,0:T(8,128)(2,1)}), bf16[16,48,128]{2,1,0:T(8,128)(2,1)S(1)}, u32[]{:S(2)}, u32[]{:S(2)}) async-start(bf16[16,48,128]{2,1,0:T(8,128)(2,1)} %broadcast_in_dim.2), calls=%async_computation.4 | async-start | bytes 393216 | tf_op jit(solution)/shard_map/all_to_all | solution.py:336
  95.2 2.3 %collective-permute-start.4 = (f32[64,128]{1,0:T(8,128)}, f32[64,128]{1,0:T(8,128)S(1)}, u32[]{:S(2)}, u32[]{:S(2)}) collective-permute-start(f32[64,128]{1,0:T(8,128)} %copy-done.54), channel_id=1, source_target_pairs={{0,16},{16,32},{32,48},{48,64},{64,80},{80,96},{96,112},{112,128},... | collective-permute-start | bytes 98312 | tf_op jit(solution)/shard_map/ppermute | solution.py:332
  97.5 6.0 %collective-permute-start.5 = (f32[64,128]{1,0:T(8,128)S(1)}, f32[64,128]{1,0:T(8,128)S(1)}, u32[]{:S(2)}, u32[]{:S(2)}) collective-permute-start(f32[64,128]{1,0:T(8,128)S(1)} %get-tuple-element.44), channel_id=1, source_target_pairs={{16,0},{32,16},{48,32},{64,48},{80,64},{96,80},{112,96},{128,112},... | collective-permute-start | bytes 98312 | tf_op jit(solution)/shard_map/ppermute | solution.py:332
  103.5 4.1 %collective-permute-start.6 = (f32[16,128]{1,0:T(8,128)S(1)}, f32[16,128]{1,0:T(8,128)S(1)}, u32[]{:S(2)}, u32[]{:S(2)}) collective-permute-start(f32[16,128]{1,0:T(8,128)S(1)} %get-tuple-element.45), channel_id=1, source_target_pairs={{0,1},{1,2},{2,3},{3,4},{4,5},{5,6},{6,7},{7,8},{8,9},{9,10},{10,1... | collective-permute-start | bytes 24584 | tf_op jit(solution)/shard_map/ppermute | solution.py:332
  107.6 2.1 collective-permute-start.7
  109.8 2.9 %collective-permute-done.7.ahead_ref = f32[16,128]{1,0:T(8,128)S(1)} collective-permute-done((f32[16,128]{1,0:T(8,128)S(1)}, f32[16,128]{1,0:T(8,128)S(1)}, u32[]{:S(2)}, u32[]{:S(2)}) %collective-permute-start.7) | collective-permute-done | bytes 8224 | tf_op jit(solution)/shard_map/ppermute | solution.py:332
  112.6 2.2 copy-done.3
  114.8 1.2 copy-done.16
  116.0 1.0 copy-done.20
  117.1 1.0 copy-done.23
  118.1 1.0 copy-done.29
  119.2 1.0 copy-done.33
  120.2 1.0 copy-done.39
  121.3 3.3 %shard_map.170 = (f32[16,64,128]{2,1,0:T(8,128)S(1)}, bf16[16,128,128]{2,1,0:T(8,128)(2,1)S(1)}, f32[64,128]{1,0:T(8,128)S(1)}, f32[64,128]{1,0:T(8,128)S(1)}, f...) custom-call(bf16[16,128,128]{2,1,0:T(8,128)(2,1)S(1)} %copy-done.33, f32[16,128,128]{2,1,0:T(8,128)S(1)} %copy-done.16, ...), custom_call_target="tpu_custom_call" | custom-call | tf_op jit(solution)/shard_map/pallas_call | solution.py:22
  128.0 4.6 %all-to-all-start.2 = ((bf16[16,128,128]{2,1,0:T(8,128)(2,1)}), bf16[16,128,128]{2,1,0:T(8,128)(2,1)}, u32[]{:S(2)}, u32[]{:S(2)}) async-start(bf16[16,128,128]{2,1,0:T(8,128)(2,1)} %copy-done.43), calls=%async_computation.2 | async-start | bytes 1048576 | tf_op jit(solution)/shard_map/all_to_all | solution.py:336
  134.1 1.7 shard_map.172
  136.7 12.3 %all-to-all-done.2.incoming_ref = bf16[16,128,128]{2,1,0:T(8,128)(2,1)} async-done(((bf16[16,128,128]{2,1,0:T(8,128)(2,1)}), bf16[16,128,128]{2,1,0:T(8,128)(2,1)}, u32[]{:S(2)}, u32[]{:S(2)}) %all-to-all-start.2) | async-done | bytes 524320 | tf_op jit(solution)/shard_map/all_to_all | solution.py:336
  149.0 6.0 %all-to-all-start.5 = ((f32[16,64,128]{2,1,0:T(8,128)}), f32[16,64,128]{2,1,0:T(8,128)}, u32[]{:S(2)}, u32[]{:S(2)}) async-start(f32[16,64,128]{2,1,0:T(8,128)} %copy-done.42), calls=%async_computation.5 | async-start | bytes 1048576 | tf_op jit(solution)/shard_map/all_to_all | solution.py:336
  155.0 2.0 collective-permute-start.8
  157.0 6.3 %collective-permute-start.9 = (f32[64,128]{1,0:T(8,128)S(1)}, f32[64,128]{1,0:T(8,128)S(1)}, u32[]{:S(2)}, u32[]{:S(2)}) collective-permute-start(f32[64,128]{1,0:T(8,128)S(1)} %get-tuple-element.50), channel_id=1, source_target_pairs={{16,0},{32,16},{48,32},{64,48},{80,64},{96,80},{112,96},{128,112},... | collective-permute-start | bytes 98312 | tf_op jit(solution)/shard_map/ppermute | solution.py:332
  163.3 4.1 %collective-permute-start.10 = (f32[16,128]{1,0:T(8,128)}, f32[16,128]{1,0:T(8,128)S(1)}, u32[]{:S(2)}, u32[]{:S(2)}) collective-permute-start(f32[16,128]{1,0:T(8,128)} %copy-done.56), channel_id=1, source_target_pairs={{0,1},{1,2},{2,3},{3,4},{4,5},{5,6},{6,7},{7,8},{8,9},{9,10},{10,1... | collective-permute-start | bytes 24584 | tf_op jit(solution)/shard_map/ppermute | solution.py:332
  167.4 1.9 collective-permute-start.11
  169.4 3.2 %collective-permute-done.11.ahead_ref = f32[16,128]{1,0:T(8,128)S(1)} collective-permute-done((f32[16,128]{1,0:T(8,128)}, f32[16,128]{1,0:T(8,128)S(1)}, u32[]{:S(2)}, u32[]{:S(2)}) %collective-permute-start.11) | collective-permute-done | bytes 8224 | tf_op jit(solution)/shard_map/ppermute | solution.py:332
  172.6 2.2 copy-done.4
  174.8 2.2 copy-done.7
  177.0 1.2 copy-done.17
  178.2 1.0 copy-done.21
  179.3 1.0 copy-done.24
  180.3 1.0 copy-done.30
  181.3 1.0 copy-done.37
  182.4 7.7 %shard_map.171 = (f32[16,64,128]{2,1,0:T(8,128)S(1)}, f32[16,16,128]{2,1,0:T(8,128)}) custom-call(bf16[16,128,128]{2,1,0:T(8,128)(2,1)} %all-to-all-done.2.incoming_ref, f32[16,128,128]{2,1,0:T(8,128)S(1)} %copy-done.17, bf16[1024,2048]{1,0:T(8,128)(2,1)S(1)} %copy-done.4, f32[16,64,128]{2,1,0:T(8,128)S(1)} %copy-done.37, f32[16,64,128]{2,1,0:T(8,128)S(1)} %copy-done.24, ...), custom_call_target="tpu_custom_call" | custom-call | tf_op jit(solution)/shard_map/pallas_call | solution.py:22
  190.9 6.0 %all-to-all-start.3 = ((f32[16,16,128]{2,1,0:T(8,128)}), f32[16,16,128]{2,1,0:T(8,128)S(1)}, u32[]{:S(2)}, u32[]{:S(2)}) async-start(f32[16,16,128]{2,1,0:T(8,128)} %get-tuple-element.54), calls=%async_computation.3 | async-start | bytes 262144 | tf_op jit(solution)/shard_map/all_to_all | solution.py:336
  198.1 2.4 %shard_map.173.done_ref = f32[4,16,128]{2,1,0:T(8,128)S(1)} custom-call(f32[16,64,128]{2,1,0:T(8,128)} %all-to-all-done.5.whole_ref, s32[64,1]{1,0:T(8,128)S(1)} %reshape_squeeze.17.cols_ref, bf16[16,4,128,128]{3,2,1,0:T(8,128)(2,1)S(1)} %bitcast.30, f32[3,16,128]{2,1,0:T(8,128)S(1)} %bitcast.35, f32[64,128]{1,0:T(8,128)S(1)} %get-tuple-element.56.own_ref, ...), custom_call_target="tpu_custom_call" | custom-call | tf_op jit(solution)/shard_map/pallas_call | solution.py:22
  200.5 2.5 %all-to-all-done.3.press_ref = f32[16,16,128]{2,1,0:T(8,128)S(1)} async-done(((f32[16,16,128]{2,1,0:T(8,128)}), f32[16,16,128]{2,1,0:T(8,128)S(1)}, u32[]{:S(2)}, u32[]{:S(2)}) %all-to-all-start.3) | async-done | bytes 131104 | tf_op jit(solution)/shard_map/all_to_all | solution.py:336
  203.0 2.0 shard_map.174
  205.0 8.6 %all_to_all.35 = f32[16,1,128]{2,1,0:T(1,128)S(1)} all-to-all(f32[16,1,128]{2,1,0:T(1,128)S(1)} %bitcast.49), channel_id=1, replica_groups=mesh['slab'=16,'col'=16] {'col'}, dimensions={0} | all-to-all | bytes 16384 | tf_op jit(solution)/shard_map/all_to_all | solution.py:336
  213.6 2.2 copy-done.8
  215.8 1.0 copy-done.46
  216.8 2.2 %shard_map.175 = f32[16,64,128]{2,1,0:T(8,128)} custom-call(f32[16,128]{1,0:T(8,128)S(1)} %bitcast.46, s32[16,128]{1,0:T(8,128)S(1)} %bitcast.43, bf16[1024,2048]{1,0:T(8,128)(2,1)S(1)} %copy-done.8, f32[16,64,128]{2,1,0:T(8,128)S(1)} %copy-done.46, f32[16,64,128]{2,1,0:T(8,128)S(1)} %copy-done.31), custom_call_target="tpu_custom_call" | custom-call | tf_op jit(solution)/shard_map/pallas_call | solution.py:22
  (109 shorter events, 14.0 us)
Async XLA Ops:
  0.6 1.0 copy-start.25
  5.2 2.0 copy-start
  7.3 44.4 %copy-start.22 = (f32[16,64,128]{2,1,0:T(8,128)S(1)}, f32[16,64,128]{2,1,0:T(8,128)}, u32[]{:S(2)}) copy-start(f32[16,64,128]{2,1,0:T(8,128)} %source_ref.5) | copy-start | bytes 1572868
  7.3 44.4 %all-to-all-start = ((bf16[16,128,128]{2,1,0:T(8,128)(2,1)}), bf16[16,128,128]{2,1,0:T(8,128)(2,1)}, u32[]{:S(2)}, u32[]{:S(2)}) async-start(bf16[16,128,128]{2,1,0:T(8,128)(2,1)} %get-tuple-element.32), calls=%async_computation | async-start | bytes 1048576 | tf_op jit(solution)/shard_map/all_to_all | solution.py:336
  18.4 1.0 copy-start.9
  19.4 1.0 copy-start.12
  20.5 1.0 copy-start.26
  21.5 30.1 %copy-start.11 = (f32[16,64,128]{2,1,0:T(8,128)S(1)}, f32[16,64,128]{2,1,0:T(8,128)}, u32[]{:S(2)}) copy-start(f32[16,64,128]{2,1,0:T(8,128)} %face_z_ref.9) | copy-start | bytes 1572868
  21.5 30.1 %copy-start.14 = (f32[16,64,128]{2,1,0:T(8,128)S(1)}, f32[16,64,128]{2,1,0:T(8,128)}, u32[]{:S(2)}) copy-start(f32[16,64,128]{2,1,0:T(8,128)} %face_x_ref.9) | copy-start | bytes 1572868
  21.5 30.2 %copy-start.19 = (f32[16,64,128]{2,1,0:T(8,128)S(1)}, f32[16,64,128]{2,1,0:T(8,128)}, u32[]{:S(2)}) copy-start(f32[16,64,128]{2,1,0:T(8,128)} %face_y_ref.7) | copy-start | bytes 1572868
  21.5 30.0 %collective-permute-start = (f32[2,64,128]{2,1,0:T(8,128)S(1)}, f32[2,64,128]{2,1,0:T(8,128)S(1)}, u32[]{:S(2)}, u32[]{:S(2)}) collective-permute-start(f32[2,64,128]{2,1,0:T(8,128)S(1)} %get-tuple-element.36), channel_id=1, source_target_pairs={{0,16},{16,32},{32,48},{48,64},{64,80},{80,96},{96,112},{112,128},... | collective-permute-start | bytes 196616 | tf_op jit(solution)/shard_map/ppermute | solution.py:332
  25.7 25.9 %collective-permute-start.2 = (f32[2,16,128]{2,1,0:T(8,128)S(1)}, f32[2,16,128]{2,1,0:T(8,128)S(1)}, u32[]{:S(2)}, u32[]{:S(2)}) collective-permute-start(f32[2,16,128]{2,1,0:T(8,128)S(1)} %get-tuple-element.38), channel_id=1, source_target_pairs={{0,1},{1,2},{2,3},{3,4},{4,5},{5,6},{6,7},{7,8},{8,9},{9,10},{10,1... | collective-permute-start | bytes 49160 | tf_op jit(solution)/shard_map/ppermute | solution.py:332
  29.7 21.9 %collective-permute-start.1 = (f32[64,128]{1,0:T(8,128)S(1)}, f32[64,128]{1,0:T(8,128)S(1)}, u32[]{:S(2)}, u32[]{:S(2)}) collective-permute-start(f32[64,128]{1,0:T(8,128)S(1)} %get-tuple-element.37), channel_id=1, source_target_pairs={{16,0},{32,16},{48,32},{64,48},{80,64},{96,80},{112,96},{128,112},... | collective-permute-start | bytes 98312 | tf_op jit(solution)/shard_map/ppermute | solution.py:332
  34.0 17.6 %collective-permute-start.3 = (f32[16,128]{1,0:T(8,128)S(1)}, f32[16,128]{1,0:T(8,128)S(1)}, u32[]{:S(2)}, u32[]{:S(2)}) collective-permute-start(f32[16,128]{1,0:T(8,128)S(1)} %get-tuple-element.39), channel_id=1, source_target_pairs={{1,0},{2,1},{3,2},{4,3},{5,4},{6,5},{7,6},{8,7},{9,8},{10,9},{11,1... | collective-permute-start | bytes 24584 | tf_op jit(solution)/shard_map/ppermute | solution.py:332
  36.0 2.2 copy-start.1
  38.2 1.0 copy-start.10
  39.3 1.0 copy-start.13
  40.3 1.0 copy-start.18
  41.4 1.2 copy-start.34
  42.6 1.0 copy-start.35
  48.7 2.0 copy-start.6
  51.6 9.1 %copy-start.15 = (f32[16,128,128]{2,1,0:T(8,128)}, f32[16,128,128]{2,1,0:T(8,128)S(1)}, u32[]{:S(2)}) copy-start(f32[16,128,128]{2,1,0:T(8,128)S(1)} %get-tuple-element.34.turned_ref) | copy-start | bytes 3145732
  51.7 2.5 %copy-start.2 = (bf16[1024,2048]{1,0:T(8,128)(2,1)S(1)}, bf16[1024,2048]{1,0:T(8,128)(2,1)}, u32[]{:S(2)}) copy-start(bf16[1024,2048]{1,0:T(8,128)(2,1)} %copy-done) | copy-start | bytes 12582916
  54.2 1.0 copy-start.27
  55.2 1.0 copy-start.41
  56.2 15.6 %copy-start.48 = (f32[1,3,2048]{2,0,1:T(1,128)S(1)}, f32[1,3,2048]{2,0,1:T(1,128)}, u32[]{:S(2)}) copy-start(f32[1,3,2048]{2,0,1:T(1,128)} %param.25) | copy-start | bytes 73732
  60.7 0.8 copy-start.28
  63.7 24.8 %all-to-all-start.1 = ((bf16[16,128,128]{2,1,0:T(8,128)(2,1)}), bf16[16,128,128]{2,1,0:T(8,128)(2,1)S(1)}, u32[]{:S(2)}, u32[]{:S(2)}) async-start(bf16[16,128,128]{2,1,0:T(8,128)(2,1)} %copy-done.44), calls=%async_computation.1 | async-start | bytes 1048576 | tf_op jit(solution)/shard_map/all_to_all | solution.py:336
  88.5 24.2 %copy-start.32 = (bf16[16,128,128]{2,1,0:T(8,128)(2,1)}, bf16[16,128,128]{2,1,0:T(8,128)(2,1)S(1)}, u32[]{:S(2)}) copy-start(bf16[16,128,128]{2,1,0:T(8,128)(2,1)S(1)} %all-to-all-done.1.incoming_ref) | copy-start | bytes 1572868
  89.2 38.8 %all-to-all-start.4 = ((bf16[16,48,128]{2,1,0:T(8,128)(2,1)}), bf16[16,48,128]{2,1,0:T(8,128)(2,1)S(1)}, u32[]{:S(2)}, u32[]{:S(2)}) async-start(bf16[16,48,128]{2,1,0:T(8,128)(2,1)} %broadcast_in_dim.2), calls=%async_computation.4 | async-start | bytes 393216 | tf_op jit(solution)/shard_map/all_to_all | solution.py:336
  95.2 17.4 %collective-permute-start.4 = (f32[64,128]{1,0:T(8,128)}, f32[64,128]{1,0:T(8,128)S(1)}, u32[]{:S(2)}, u32[]{:S(2)}) collective-permute-start(f32[64,128]{1,0:T(8,128)} %copy-done.54), channel_id=1, source_target_pairs={{0,16},{16,32},{32,48},{48,64},{64,80},{80,96},{96,112},{112,128},... | collective-permute-start | bytes 98312 | tf_op jit(solution)/shard_map/ppermute | solution.py:332
  97.5 15.1 %collective-permute-start.5 = (f32[64,128]{1,0:T(8,128)S(1)}, f32[64,128]{1,0:T(8,128)S(1)}, u32[]{:S(2)}, u32[]{:S(2)}) collective-permute-start(f32[64,128]{1,0:T(8,128)S(1)} %get-tuple-element.44), channel_id=1, source_target_pairs={{16,0},{32,16},{48,32},{64,48},{80,64},{96,80},{112,96},{128,112},... | collective-permute-start | bytes 98312 | tf_op jit(solution)/shard_map/ppermute | solution.py:332
  103.5 6.2 %collective-permute-start.6 = (f32[16,128]{1,0:T(8,128)S(1)}, f32[16,128]{1,0:T(8,128)S(1)}, u32[]{:S(2)}, u32[]{:S(2)}) collective-permute-start(f32[16,128]{1,0:T(8,128)S(1)} %get-tuple-element.45), channel_id=1, source_target_pairs={{0,1},{1,2},{2,3},{3,4},{4,5},{5,6},{6,7},{7,8},{8,9},{9,10},{10,1... | collective-permute-start | bytes 24584 | tf_op jit(solution)/shard_map/ppermute | solution.py:332
  107.6 5.0 %collective-permute-start.7 = (f32[16,128]{1,0:T(8,128)S(1)}, f32[16,128]{1,0:T(8,128)S(1)}, u32[]{:S(2)}, u32[]{:S(2)}) collective-permute-start(f32[16,128]{1,0:T(8,128)S(1)} %get-tuple-element.46), channel_id=1, source_target_pairs={{1,0},{2,1},{3,2},{4,3},{5,4},{6,5},{7,6},{8,7},{9,8},{10,9},{11,1... | collective-permute-start | bytes 24584 | tf_op jit(solution)/shard_map/ppermute | solution.py:332
  112.6 2.2 copy-start.3
  114.8 1.2 copy-start.16
  116.0 1.0 copy-start.20
  117.1 1.0 copy-start.23
  118.1 1.0 copy-start.29
  119.2 1.0 copy-start.33
  120.2 1.0 copy-start.39
  121.3 12.9 %copy-start.5 = (bf16[1,16,4,128,128]{4,3,2,1,0:T(8,128)(2,1)S(1)}, bf16[1,16,4,128,128]{4,3,2,1,0:T(8,128)(2,1)}, u32[]{:S(2)}) copy-start(bf16[1,16,4,128,128]{4,3,2,1,0:T(8,128)(2,1)} %param.28) | copy-start | bytes 6291460
  121.3 12.9 %copy-start.47 = (f32[1,3,2048]{2,0,1:T(1,128)S(1)}, f32[1,3,2048]{2,0,1:T(1,128)}, u32[]{:S(2)}) copy-start(f32[1,3,2048]{2,0,1:T(1,128)} %param.24) | copy-start | bytes 73732
  121.3 12.9 %copy-start.49 = (f32[1,2048]{1,0:T(1,128)S(1)}, f32[1,2048]{1,0:T(1,128)}, u32[]{:S(2)}) copy-start(f32[1,2048]{1,0:T(1,128)} %param.26) | copy-start | bytes 24580
  124.6 0.8 copy-start.36
  128.0 44.6 %copy-start.51 = (s32[1,1,16,128]{3,2,1,0:T(8,128)S(1)}, s32[1,1,16,128]{3,2,1,0:T(8,128)}, u32[]{:S(2)}) copy-start(s32[1,1,16,128]{3,2,1,0:T(8,128)} %param.23) | copy-start | bytes 24580
  128.0 21.0 %all-to-all-start.2 = ((bf16[16,128,128]{2,1,0:T(8,128)(2,1)}), bf16[16,128,128]{2,1,0:T(8,128)(2,1)}, u32[]{:S(2)}, u32[]{:S(2)}) async-start(bf16[16,128,128]{2,1,0:T(8,128)(2,1)} %copy-done.43), calls=%async_computation.2 | async-start | bytes 1048576 | tf_op jit(solution)/shard_map/all_to_all | solution.py:336
  135.8 0.9 copy-start.42
  149.0 41.9 %all-to-all-start.5 = ((f32[16,64,128]{2,1,0:T(8,128)}), f32[16,64,128]{2,1,0:T(8,128)}, u32[]{:S(2)}, u32[]{:S(2)}) async-start(f32[16,64,128]{2,1,0:T(8,128)} %copy-done.42), calls=%async_computation.5 | async-start | bytes 1048576 | tf_op jit(solution)/shard_map/all_to_all | solution.py:336
  155.0 17.6 %collective-permute-start.8 = (f32[64,128]{1,0:T(8,128)}, f32[64,128]{1,0:T(8,128)S(1)}, u32[]{:S(2)}, u32[]{:S(2)}) collective-permute-start(f32[64,128]{1,0:T(8,128)} %copy-done.53), channel_id=1, source_target_pairs={{0,16},{16,32},{32,48},{48,64},{64,80},{80,96},{96,112},{112,128},... | collective-permute-start | bytes 98312 | tf_op jit(solution)/shard_map/ppermute | solution.py:332
  157.0 15.6 %collective-permute-start.9 = (f32[64,128]{1,0:T(8,128)S(1)}, f32[64,128]{1,0:T(8,128)S(1)}, u32[]{:S(2)}, u32[]{:S(2)}) collective-permute-start(f32[64,128]{1,0:T(8,128)S(1)} %get-tuple-element.50), channel_id=1, source_target_pairs={{16,0},{32,16},{48,32},{64,48},{80,64},{96,80},{112,96},{128,112},... | collective-permute-start | bytes 98312 | tf_op jit(solution)/shard_map/ppermute | solution.py:332
  163.3 6.0 %collective-permute-start.10 = (f32[16,128]{1,0:T(8,128)}, f32[16,128]{1,0:T(8,128)S(1)}, u32[]{:S(2)}, u32[]{:S(2)}) collective-permute-start(f32[16,128]{1,0:T(8,128)} %copy-done.56), channel_id=1, source_target_pairs={{0,1},{1,2},{2,3},{3,4},{4,5},{5,6},{6,7},{7,8},{8,9},{9,10},{10,1... | collective-permute-start | bytes 24584 | tf_op jit(solution)/shard_map/ppermute | solution.py:332
  167.4 5.2 %collective-permute-start.11 = (f32[16,128]{1,0:T(8,128)}, f32[16,128]{1,0:T(8,128)S(1)}, u32[]{:S(2)}, u32[]{:S(2)}) collective-permute-start(f32[16,128]{1,0:T(8,128)} %copy-done.55), channel_id=1, source_target_pairs={{1,0},{2,1},{3,2},{4,3},{5,4},{6,5},{7,6},{8,7},{9,8},{10,9},{11,1... | collective-permute-start | bytes 24584 | tf_op jit(solution)/shard_map/ppermute | solution.py:332
  172.6 2.2 copy-start.4
  174.8 2.2 copy-start.7
  177.0 1.2 copy-start.17
  178.2 1.0 copy-start.21
  179.2 1.0 copy-start.24
  180.3 1.0 copy-start.30
  181.3 1.0 copy-start.37
  190.9 22.7 %copy-start.31 = (f32[16,64,128]{2,1,0:T(8,128)S(1)}, f32[16,64,128]{2,1,0:T(8,128)}, u32[]{:S(2)}) copy-start(f32[16,64,128]{2,1,0:T(8,128)} %copy-done.28) | copy-start | bytes 1572868
  190.9 12.1 %all-to-all-start.3 = ((f32[16,16,128]{2,1,0:T(8,128)}), f32[16,16,128]{2,1,0:T(8,128)S(1)}, u32[]{:S(2)}, u32[]{:S(2)}) async-start(f32[16,16,128]{2,1,0:T(8,128)} %get-tuple-element.54), calls=%async_computation.3 | async-start | bytes 262144 | tf_op jit(solution)/shard_map/all_to_all | solution.py:336
  213.6 2.2 copy-start.8
  215.8 1.0 copy-start.46
  (11 other events, 7.8 us)

commit v2 on v1

v2 whole, which is shorter than its diff:
```python
import functools

import jax
import jax.numpy as jnp
from jax import lax
from jax.experimental import pallas as pl
from jax.experimental.pallas import tpu as pltpu
from jax.sharding import PartitionSpec as P

ITERS_FLOW = 3
BIOT = 0.8
F32 = jnp.float32
BF16 = jnp.bfloat16
NT = (((1,), (1,)), ((), ()))


def call(body, outs, *args, smem=(), hbm=(), scratch=(), mib=14):
    spaces = [
        pltpu.SMEM if i in smem else pltpu.HBM if i in hbm else pltpu.VMEM
        for i in range(len(args))
    ]
    args = [
        pltpu.with_memory_space_constraint(a, pltpu.HBM) if i in hbm else a
        for i, a in enumerate(args)
    ]
    far = [len(o) > 2 for o in outs]
    return pl.pallas_call(
        body,
        in_specs=[pl.BlockSpec(memory_space=space) for space in spaces],
        out_specs=[
            pl.BlockSpec(memory_space=pltpu.HBM if f else pltpu.VMEM) for f in far
        ],
        out_shape=[
            pltpu.HBM(*o[:2]) if f else jax.ShapeDtypeStruct(*o)
            for o, f in zip(outs, far)
        ],
        scratch_shapes=list(scratch),
        compiler_params=pltpu.CompilerParams(vmem_limit_bytes=mib << 20),
    )(*args)


def begin(pairs, sems, at=0):
    copies = [
        pltpu.make_async_copy(source, target, sems.at[at + i])
        for i, (source, target) in enumerate(pairs)
    ]
    for copy in copies:
        copy.start()
    return copies


def finish(copies):
    for copy in copies:
        copy.wait()


def iota(shape, dim):
    return lax.broadcasted_iota(jnp.int32, shape, dim)


def halves(x):
    high = x.astype(BF16)
    return high, (x - high.astype(F32)).astype(BF16)


def fill_hot(hot_ref, lines):
    rows = hot_ref.shape[0]
    ids = iota((rows, 128), 0)
    for q in range(lines.shape[0]):
        hit = ids == lines[q : q + 1, :]
        hot_ref[:, q * 128 : (q + 1) * 128] = jnp.where(hit, 1.0, 0.0).astype(BF16)


def gather_lines(hot_ref, field, out_ref):
    turned = field.T.astype(BF16)
    for q in range(0, out_ref.shape[0], 2):
        got = jnp.dot(
            turned, hot_ref[:, q * 128 : (q + 2) * 128], preferred_element_type=F32
        ).astype(BF16)
        out_ref[q] = got[:, :128]
        out_ref[q + 1] = got[:, 128:]


def scatter_lines(hot_ref, values_ref):
    both = lax.dot_general(hot_ref[...], values_ref[...], NT, preferred_element_type=F32)
    return both[:, :128] + both[:, 128:]


def put_halves(values_ref, q, values):
    high, low = halves(values)
    values_ref[:128, q * 128 : (q + 1) * 128] = high
    values_ref[128:, q * 128 : (q + 1) * 128] = low


def ready_kernel(slip_ref, out_ref):
    parts, rows, _ = slip_ref.shape
    for p in range(parts):
        out_ref[0, p * rows : (p + 1) * rows, :] = slip_ref[p].astype(BF16)
    mine = out_ref[0]
    for o in range(1, out_ref.shape[0]):
        out_ref[o] = mine


def first_kernel(
    field_hbm,
    face_z_hbm,
    face_x_hbm,
    cell_ref,
    out_hbm,
    up_ref,
    down_ref,
    right_ref,
    left_ref,
    hot_ref,
    field_ref,
    wall_ref,
    out_ref,
    sems,
):
    depth, width, lateral = field_ref.shape
    reads = begin(
        [
            (field_hbm, field_ref),
            (face_z_hbm.at[depth - 1], up_ref.at[1]),
            (face_x_hbm.at[:, pl.ds(width - 8, 8), :], wall_ref),
        ],
        sems,
    )
    fill_hot(hot_ref, cell_ref[...])
    finish(reads)
    gather_lines(hot_ref, field_ref[...].reshape(depth * width, lateral), out_ref)
    writes = begin([(out_ref, out_hbm)], sems, 3)
    up_ref[0] = field_ref[depth - 1]
    down_ref[...] = field_ref[0]
    for i in range(depth):
        right_ref[0, i : i + 1, :] = field_ref[i, width - 1 : width, :]
        right_ref[1, i : i + 1, :] = wall_ref[i, 7:8, :]
        left_ref[i : i + 1, :] = field_ref[i, 0:1, :]
    finish(writes)


def sweep_kernel(
    first,
    last,
    incoming_ref,
    turned_hbm,
    field_hbm,
    source_hbm,
    face_z_hbm,
    face_x_hbm,
    face_y_hbm,
    diag_hbm,
    cell_ref,
    below_ref,
    above_ref,
    behind_ref,
    ahead_ref,
    lower_z_ref,
    lower_x_ref,
    *refs,
):
    refs = list(refs)
    sems = refs.pop()
    hot_ref, values_ref, turned_ref = [refs.pop() for _ in range(3)]
    big = [refs.pop() for _ in range(6)]
    field_ref, source_ref, face_z_ref, face_x_ref, face_y_ref, diag_ref = big
    depth, width, lateral = field_ref.shape
    if first:
        link_ref = refs.pop()
    if not last:
        new_ref, out_ref = refs.pop(), refs.pop()
    linked_reads = begin([(turned_hbm, turned_ref)], sems)
    reads = begin(
        list(
            zip(
                (field_hbm, source_hbm, face_z_hbm, face_x_hbm, face_y_hbm, diag_hbm),
                big,
            )
        ),
        sems,
        2,
    )
    fill_hot(hot_ref, cell_ref[...])
    finish(linked_reads)
    for q in range(incoming_ref.shape[0]):
        turned = turned_ref[q]
        if first:
            turned = turned.T
            turned_ref[q] = turned
            put_halves(link_ref, q, turned)
        put_halves(values_ref, q, turned * incoming_ref[q].astype(F32))
    linked = scatter_lines(hot_ref, values_ref)
    if first:
        conduct = scatter_lines(hot_ref, link_ref)
        last_z = lax.axis_index("slab") == lax.axis_size("slab") - 1
        last_x = lax.axis_index("col") == lax.axis_size("col") - 1
    finish(reads)
    writes = []
    if last:
        fault_ref, own_ref, new_ref, fault_hot_ref, press_ref = refs
    elif first:
        new_hbm, out_hbm, turned_out, inverse_out = refs[:4]
        up_ref, down_ref, right_ref, left_ref = refs[4:]
        writes += begin([(turned_ref, turned_out)], sems, 8)
    else:
        new_hbm, out_hbm, up_ref, down_ref, right_ref, left_ref = refs
    across = iota((width, lateral), 0)
    along = iota((width, lateral), 1)
    for i in range(depth):
        field = field_ref[i]
        face_z = face_z_ref[i]
        lower_z = face_z_ref[i - 1] if i > 0 else lower_z_ref[1]
        above = field_ref[i + 1] if i < depth - 1 else above_ref[...]
        below = field_ref[i - 1] if i > 0 else below_ref[0]
        total = source_ref[i] + linked[i * width : (i + 1) * width]
        total = total + face_z * above + lower_z * below
        face_x = face_x_ref[i]
        lower_x = lower_x_ref[1, i : i + 1, :]
        ahead = jnp.where(
            across == width - 1, ahead_ref[i : i + 1, :], pltpu.roll(field, width - 1, 0)
        )
        flow = jnp.where(
            across == 0,
            lower_x * behind_ref[0, i : i + 1, :],
            pltpu.roll(face_x * field, 1, 0),
        )
        total = total + face_x * ahead + flow
        face_y = jnp.where(along == lateral - 1, 0.0, face_y_ref[i])
        total = total + face_y * pltpu.roll(field, lateral - 1, 1)
        total = total + pltpu.roll(face_y * field, 1, 1)
        if first:
            whole = diag_ref[i] + conduct[i * width : (i + 1) * width] + lower_z
            own_z = jnp.where(last_z, 0.0, face_z) if i == depth - 1 else face_z
            whole = whole + own_z + face_y + pltpu.roll(face_y, 1, 1)
            whole = whole + jnp.where((across == width - 1) & last_x, 0.0, face_x)
            whole = whole + jnp.where(across == 0, lower_x, pltpu.roll(face_x, 1, 0))
            inverse = 1.0 / whole
            diag_ref[i] = inverse
        else:
            inverse = diag_ref[i]
        new_ref[i] = total * inverse
    lines = new_ref[...].reshape(depth * width, lateral)
    if last:
        fill_hot(fault_hot_ref, fault_ref[...] >> 7)
        high, low = halves(lines.T)
        both = jnp.concatenate([high, low], 0)
        side = iota((lateral, 128), 0)
        for q in range(fault_ref.shape[0]):
            got = jnp.dot(
                both, fault_hot_ref[:, q * 128 : (q + 1) * 128], preferred_element_type=F32
            )
            got = got[:lateral] + got[lateral:]
            lane = fault_ref[q : q + 1, :] & 127
            got = jnp.sum(jnp.where(side == lane, got, 0.0), 0, keepdims=True)
            press_ref[0, q : q + 1, :] = got
        press_ref[0, fault_ref.shape[0] :, :] = own_ref[...]
        mine = press_ref[0]
        for o in range(1, press_ref.shape[0]):
            press_ref[o] = mine
    else:
        writes += begin([(new_ref, new_hbm)], sems, 9)
        if first:
            writes += begin([(diag_ref, inverse_out)], sems, 10)
        gather_lines(hot_ref, lines, out_ref)
        writes += begin([(out_ref, out_hbm)], sems, 11)
        up_ref[0] = new_ref[depth - 1]
        down_ref[...] = new_ref[0]
        for i in range(depth):
            right_ref[0, i : i + 1, :] = new_ref[i, width - 1 : width, :]
            left_ref[i : i + 1, :] = new_ref[i, 0:1, :]
    finish(writes)


def couple(cols_ref, tiles_ref, blocks_ref):
    rows, per = blocks_ref.shape[:2]
    ids = iota((rows, 128), 0)
    total = None
    for r in range(rows):
        for b in range(per):
            at = pl.ds(cols_ref[r, b], 1)
            left = [
                jnp.where(ids == r, tiles_ref[p, at, :], 0.0)
                for p in range(tiles_ref.shape[0])
            ]
            left = jnp.concatenate(left, 0).astype(BF16)
            part = lax.dot_general(left, blocks_ref[r, b], NT, preferred_element_type=F32)
            total = part if total is None else total + part
    return total


def contact_kernel(
    cols_ref,
    whole_ref,
    blocks_hbm,
    base_ref,
    slip_ref,
    stiff_ref,
    active_ref,
    own_ref,
    tiles_ref,
    blocks_ref,
    sems,
):
    reads = begin([(blocks_hbm, blocks_ref)], sems)
    owners = whole_ref.shape[0]
    rows = base_ref.shape[1]
    for p in range(3):
        part = whole_ref[:, p * rows : (p + 1) * rows, :].astype(F32)
        tiles_ref[p] = part.reshape(owners * rows, 128)
    finish(reads)
    coupled = couple(cols_ref, tiles_ref, blocks_ref)
    gain = active_ref[0].astype(F32) / stiff_ref[...]
    parts = [
        slip_ref[p] + gain * (base_ref[p] - coupled[p * rows : (p + 1) * rows])
        for p in range(3)
    ]
    own_ref[...] = jnp.concatenate([parts[0], -BIOT * gain, parts[1], parts[2]], 0)


def tail_kernel(
    cols_ref,
    whole_ref,
    blocks_ref,
    base_ref,
    own_ref,
    stiff_ref,
    active_ref,
    normal_ref,
    slip_ref,
    traction_ref,
    press_ref,
    tiles_ref,
):
    sources = whole_ref.shape[0]
    rows = base_ref.shape[1]
    ids = sources * rows
    for c in range(sources):
        for o in range(sources):
            n = o * rows + c
            press_ref[n : n + 1, :] = whole_ref[c, o : o + 1, :]

    def part(n):
        return whole_ref[:, (n + 1) * rows : (n + 2) * rows, :].reshape(ids, 128)

    slips = [part(0) + part(1) * press_ref[...], part(2), part(3)]
    for p in range(3):
        tiles_ref[p] = slips[p].astype(BF16).astype(F32)
    coupled = couple(cols_ref, tiles_ref, blocks_ref)
    mine = press_ref[pl.ds(pl.multiple_of(lax.axis_index("col") * rows, rows), rows), :]
    gain = active_ref[1].astype(F32) / stiff_ref[...]
    own = [own_ref[n * rows : (n + 1) * rows] for n in range(4)]
    slips = [own[0] + own[1] * mine, own[2], own[3]]
    loads = [base_ref[0] - BIOT * mine, base_ref[1], base_ref[2]]
    for p in range(3):
        traction = loads[p] - coupled[p * rows : (p + 1) * rows]
        traction_ref[p] = traction
        slip_ref[p] = slips[p] + gain * traction
        if p == 0:
            normal_ref[...] = traction


def back_kernel(
    normal_ref, fault_ref, fault_hot_ref, field_ref, inverse_ref, out_ref, values_ref
):
    depth, width, lateral = field_ref.shape
    side = iota((lateral, 128), 0)
    for q in range(normal_ref.shape[0]):
        lane = fault_ref[q : q + 1, :] & 127
        put_halves(values_ref, q, jnp.where(side == lane, normal_ref[q : q + 1, :], 0.0))
    returned = scatter_lines(fault_hot_ref, values_ref).reshape(depth, width, lateral)
    out_ref[...] = field_ref[...] + returned * inverse_ref[...]


def shift(block, axis, step):
    count = lax.axis_size(axis)
    route = [(i, i + step) for i in range(count) if 0 <= i + step < count]
    return lax.ppermute(block, axis, route)


def swap(blocks, axis):
    return lax.all_to_all(blocks, axis, split_axis=0, concat_axis=0, tiled=True)


def per_device(
    pressure,
    source,
    accum,
    trans_z,
    trans_x,
    trans_y,
    nnc_cell,
    nnc_trans,
    fault_cell,
    base_stress,
    slip_start,
    stiff_diag,
    active_set,
    mortar_blocks,
    mortar_cols,
):
    depth, width, lateral = pressure.shape
    slabs = lax.axis_size("slab")
    columns = lax.axis_size("col")
    lines = depth * width
    grid = ((depth, width, lateral), F32)
    slots = slabs * 128
    nodes = columns * 128
    rows = mortar_blocks.shape[1]
    cells = nnc_cell[0, 0]
    faults = fault_cell[0, 0]
    blocks = mortar_blocks[0]
    tile_cols = mortar_cols[0]
    base = base_stress[0].reshape(3, rows, 128)
    slip0 = slip_start[0].reshape(3, rows, 128)
    stiff = stiff_diag[0].reshape(rows, 128)
    active = active_set[:, 0].reshape(-1, rows, 128)
    tiles = pltpu.VMEM((3, columns * rows, 128), F32)
    layer, wall = (width, lateral), (depth, lateral)
    table = pltpu.VMEM((lines, slots), BF16)
    block = pltpu.VMEM((depth, width, lateral), F32)
    packet = pltpu.VMEM((slabs, lateral, 128), BF16)
    values = pltpu.VMEM((2 * lateral, slots), BF16)
    edges = [((1, *layer), F32), (layer, F32), ((1, *wall), F32), (wall, F32)]

    (ready,) = call(ready_kernel, [((columns, 3 * rows, 128), BF16)], slip0)
    whole = swap(ready, "col")
    outgoing, up, down, right, left = call(
        first_kernel,
        [
            ((slabs, lateral, 128), BF16, 0),
            ((2, *layer), F32),
            (layer, F32),
            ((2, *wall), F32),
            (wall, F32),
        ],
        pressure,
        trans_z,
        trans_x,
        cells,
        hbm=(0, 1, 2),
        scratch=(
            table,
            block,
            pltpu.VMEM((depth, 8, lateral), F32),
            packet,
            pltpu.SemaphoreType.DMA((4,)),
        ),
    )
    whole, outgoing = lax.optimization_barrier((whole, outgoing))
    incoming = swap(outgoing, "slab")
    below = lower_z = shift(up, "slab", 1)
    behind = lower_x = shift(right, "col", 1)
    above = shift(down, "slab", -1)
    ahead = shift(left, "col", -1)
    turned, diag = nnc_trans[0, 0], accum
    field = pressure
    for sweep in range(ITERS_FLOW):
        first = sweep == 0
        last = sweep == ITERS_FLOW - 1
        extra = [faults, own] if last else []
        if last:
            outs = [
                (grid[0], F32),
                ((lines, nodes), BF16),
                ((columns, columns + 4 * rows, 128), F32),
            ]
        else:
            outs = [(*grid, 0), ((slabs, lateral, 128), BF16, 0)]
            if first:
                outs += [((slabs, lateral, 128), F32, 0), (*grid, 0)]
            outs += edges
        got = call(
            functools.partial(sweep_kernel, first, last),
            outs,
            incoming,
            turned,
            field,
            source,
            trans_z,
            trans_x,
            trans_y,
            diag,
            cells,
            below,
            above,
            behind,
            ahead,
            lower_z,
            lower_x,
            *extra,
            hbm=range(1, 8),
            scratch=[
                *([] if last else [packet, block]),
                *([values] if first else []),
                *[block] * 6,
                pltpu.VMEM((slabs, lateral, 128), F32),
                values,
                table,
                pltpu.SemaphoreType.DMA((12,)),
            ],
        )
        if last:
            field, fault_hot, whole = got
            break
        if first:
            turned, diag = got[2:4]
            whole, _ = lax.optimization_barrier((whole, got[-1]))
        field, outgoing = got[:2]
        up, down, right, left = got[-4:]
        incoming = swap(outgoing, "slab")
        below = shift(up, "slab", 1)
        behind = shift(right, "col", 1)
        above = shift(down, "slab", -1)
        ahead = shift(left, "col", -1)
        if first:
            (own,) = call(
                contact_kernel,
                [((4 * rows, 128), F32)],
                tile_cols,
                whole,
                blocks,
                base,
                slip0,
                stiff,
                active,
                smem=(0,),
                hbm=(2,),
                scratch=(
                    tiles,
                    pltpu.VMEM(blocks.shape, BF16),
                    pltpu.SemaphoreType.DMA((1,)),
                ),
            )
    whole = swap(whole, "col")
    normal, slip, traction = call(
        tail_kernel,
        [((rows, 128), F32), ((3, rows, 128), F32), ((3, rows, 128), F32)],
        tile_cols,
        whole,
        blocks,
        base,
        own,
        stiff,
        active,
        smem=(0,),
        scratch=(pltpu.VMEM((columns * rows, 128), F32), tiles),
    )
    normal = swap(normal.reshape(columns, -1, 128), "col").reshape(columns, 128)
    (pressure_out,) = call(
        back_kernel,
        [grid],
        normal,
        faults,
        fault_hot,
        field,
        diag,
        scratch=(pltpu.VMEM((2 * lateral, nodes), BF16),),
    )
    return (pressure_out, slip.reshape(1, 3, -1), traction.reshape(1, 3, -1))


def solution(mesh):
    return jax.shard_map(
        per_device,
        mesh=mesh,
        in_specs=(
            P("slab", "col", None),
            P("slab", "col", None),
            P("slab", "col", None),
            P("slab", "col", None),
            P("slab", "col", None),
            P("slab", "col", None),
            P("slab", "col", None, None),
            P("slab", "col", None, None, None),
            P("slab", "col", None, None),
            P("slab", None, "col"),
            P("slab", None, "col"),
            P("slab", "col"),
            P(None, "slab", "col"),
            P("slab", "col", None, None, None),
            P("slab", "col", None),
        ),
        out_specs=(P("slab", "col", None), P("slab", None, "col"), P("slab", None, "col")),
        check_vma=False,
    )
```

time: 222 us -> 147 us (0.66)
  the two profiles are of different devices: /device:TPU:9 before, /device:TPU:1 now
where the time goes in v2:
time: 147 us; the launch traced here: 145 us
  starting transfers between devices  64.6 us (44%)
  Pallas kernels  32.5 us (22%)
  blocking collectives  25.7 us (17%)
  waiting for transfers between devices  19.5 us (13%)
  local copies, waits for them, and re-layouts  2.26 us (2%)
    all_to_all x4, starting transfers between devices, swap(): return lax.all_to_all(blocks, axis, split_axis=0, concat_axis=0, tiled=True)  33 us
    pallas_call x8, Pallas kernels, call(): pl.pallas_call(body, in_specs=[pl.BlockSpec(memory_space=space) for space...  32.5 us
    ppermute x12, starting transfers between devices, shift(): return lax.ppermute(block, axis, route)  31.6 us
    all_to_all x2, blocking collectives, swap(): return lax.all_to_all(blocks, axis, split_axis=0, concat_axis=0, tiled=True)  25.7 us
    all_to_all x4, waiting for transfers between devices, swap(): return lax.all_to_all(blocks, axis, split_axis=0, concat_axis=0, tiled=True)  11.6 us
    ppermute x12, waiting for transfers between devices, shift(): return lax.ppermute(block, axis, route)  7.97 us
  transfers between devices with their start and end apart: 16, of which 7 were waited for; matrix products, arithmetic and copies ran while one was open for 0% of the time, Pallas kernels for 5%

profile of v2, /device:TPU:1, one launch (start us, length us, event | category | flops | bytes accessed | tf_op | source)
XLA Modules:
  0.0 145.5 jit_solution(17010403789210832220)
XLA Ops:
  0.6 0.0 copy-start.6
  0.6 0.7 copy-done.6
  1.4 0.7 shard_map.166
  2.1 7.2 %all-to-all-start = ((bf16[16,48,128]{2,1,0:T(8,128)(2,1)}), bf16[16,48,128]{2,1,0:T(8,128)(2,1)S(1)}, u32[]{:S(2)}, u32[]{:S(2)}) async-start(bf16[16,48,128]{2,1,0:T(8,128)(2,1)} %shard_map.166), calls=%async_computation | async-start | bytes 393216 | tf_op jit(solution)/shard_map/all_to_all | solution.py:381
  9.2 0.0 copy-start.2
  9.2 0.7 copy-done.2
  9.9 2.9 %shard_map.167 = (bf16[16,128,128]{2,1,0:T(8,128)(2,1)}, f32[2,64,128]{2,1,0:T(8,128)S(1)}, f32[64,128]{1,0:T(8,128)S(1)}, f32[2,16,128]{2,1,0:T(8,128)S(1)}, f32[16,128]{1,0:T(8,128)S(1)}) custom-call(f32[16,64,128]{2,1,0:T(8,128)} %field_hbm.3, f32[16,64,128]{2,1,0:T(8,128)} %face_z_hbm.7, f32[16,64,128]{2,1,0:T(8,128)} %face_x_hbm.7, s32[16,128]{1,0:T(8,128)S(1)} %bitcast.17), custom_call_target="tpu_custom_call" | custom-call | tf_op jit(solution)/shard_map/pallas_call | solution.py:27
  12.8 3.1 %all-to-all-done.whole_ref = bf16[16,48,128]{2,1,0:T(8,128)(2,1)S(1)} async-done(((bf16[16,48,128]{2,1,0:T(8,128)(2,1)}), bf16[16,48,128]{2,1,0:T(8,128)(2,1)S(1)}, u32[]{:S(2)}, u32[]{:S(2)}) %all-to-all-start) | async-done | bytes 196640 | tf_op jit(solution)/shard_map/all_to_all | solution.py:381
  15.9 10.0 %all-to-all-start.1 = ((bf16[16,128,128]{2,1,0:T(8,128)(2,1)}), bf16[16,128,128]{2,1,0:T(8,128)(2,1)S(1)}, u32[]{:S(2)}, u32[]{:S(2)}) async-start(bf16[16,128,128]{2,1,0:T(8,128)(2,1)} %get-tuple-element.32), calls=%async_computation.1 | async-start | bytes 1048576 | tf_op jit(solution)/shard_map/all_to_all | solution.py:381
  25.9 4.2 %collective-permute-start = (f32[2,64,128]{2,1,0:T(8,128)S(1)}, f32[2,64,128]{2,1,0:T(8,128)S(1)}, u32[]{:S(2)}, u32[]{:S(2)}) collective-permute-start(f32[2,64,128]{2,1,0:T(8,128)S(1)} %get-tuple-element.33), channel_id=1, source_target_pairs={{0,16},{16,32},{32,48},{48,64},{64,80},{80,96},{96,112},{112,128},... | collective-permute-start | bytes 196616 | tf_op jit(solution)/shard_map/ppermute | solution.py:377
  30.1 1.3 collective-permute-start.1
  31.4 3.5 %collective-permute-start.2 = (f32[2,16,128]{2,1,0:T(8,128)S(1)}, f32[2,16,128]{2,1,0:T(8,128)S(1)}, u32[]{:S(2)}, u32[]{:S(2)}) collective-permute-start(f32[2,16,128]{2,1,0:T(8,128)S(1)} %get-tuple-element.35), channel_id=1, source_target_pairs={{0,1},{1,2},{2,3},{3,4},{4,5},{5,6},{6,7},{7,8},{8,9},{9,10},{10,1... | collective-permute-start | bytes 49160 | tf_op jit(solution)/shard_map/ppermute | solution.py:377
  34.9 1.9 %collective-permute-start.3 = (f32[16,128]{1,0:T(8,128)S(1)}, f32[16,128]{1,0:T(8,128)S(1)}, u32[]{:S(2)}, u32[]{:S(2)}) collective-permute-start(f32[16,128]{1,0:T(8,128)S(1)} %get-tuple-element.36), channel_id=1, source_target_pairs={{1,0},{2,1},{3,2},{4,3},{5,4},{6,5},{7,6},{8,7},{9,8},{10,9},{11,1... | collective-permute-start | bytes 24584 | tf_op jit(solution)/shard_map/ppermute | solution.py:377
  36.9 3.5 %collective-permute-done.3.ahead_ref = f32[16,128]{1,0:T(8,128)S(1)} collective-permute-done((f32[16,128]{1,0:T(8,128)S(1)}, f32[16,128]{1,0:T(8,128)S(1)}, u32[]{:S(2)}, u32[]{:S(2)}) %collective-permute-start.3) | collective-permute-done | bytes 8224 | tf_op jit(solution)/shard_map/ppermute | solution.py:377
  40.4 0.0 collective-permute-done.2.behind_ref.lower_x_ref
  40.4 1.1 collective-permute-done.1.above_ref
  41.5 0.0 collective-permute-done.below_ref.lower_z_ref
  41.5 1.6 %all-to-all-done.1.incoming_ref = bf16[16,128,128]{2,1,0:T(8,128)(2,1)S(1)} async-done(((bf16[16,128,128]{2,1,0:T(8,128)(2,1)}), bf16[16,128,128]{2,1,0:T(8,128)(2,1)S(1)}, u32[]{:S(2)}, u32[]{:S(2)}) %all-to-all-start.1) | async-done | bytes 524320 | tf_op jit(solution)/shard_map/all_to_all | solution.py:381
  43.1 0.7 copy-done.3
  43.8 6.1 %shard_map.168 = (f32[16,64,128]{2,1,0:T(8,128)}, bf16[16,128,128]{2,1,0:T(8,128)(2,1)}, f32[16,128,128]{2,1,0:T(8,128)}, f32[16,64,128]{2,1,0:T(8,128)}, f32[1,...) custom-call(bf16[16,128,128]{2,1,0:T(8,128)(2,1)S(1)} %all-to-all-done.1.incomin, ...), custom_call_target="tpu_custom_call" | custom-call | tf_op jit(solution)/shard_map/pallas_call | solution.py:27
  49.9 0.0 copy-start.11
  49.9 0.0 copy-start.5
  49.9 0.0 copy-start.7
  50.0 0.0 copy-start.8
  50.0 0.0 copy-start.9
  50.0 8.2 %all-to-all-start.2 = ((bf16[16,128,128]{2,1,0:T(8,128)(2,1)}), bf16[16,128,128]{2,1,0:T(8,128)(2,1)S(1)}, u32[]{:S(2)}, u32[]{:S(2)}) async-start(bf16[16,128,128]{2,1,0:T(8,128)(2,1)} %get-tuple-element.37), calls=%async_computation.2 | async-start | bytes 1048576 | tf_op jit(solution)/shard_map/all_to_all | solution.py:381
  58.2 4.2 %collective-permute-start.4 = (f32[1,64,128]{2,1,0:T(8,128)S(1)}, f32[1,64,128]{2,1,0:T(8,128)S(1)}, u32[]{:S(2)}, u32[]{:S(2)}) collective-permute-start(f32[1,64,128]{2,1,0:T(8,128)S(1)} %get-tuple-element.41), channel_id=1, source_target_pairs={{0,16},{16,32},{32,48},{48,64},{64,80},{80,96},{96,112},{112,128},... | collective-permute-start | bytes 98312 | tf_op jit(solution)/shard_map/ppermute | solution.py:377
  62.4 1.3 collective-permute-start.5
  63.7 0.0 copy-start.10
  63.7 2.9 %collective-permute-start.6 = (f32[1,16,128]{2,1,0:T(8,128)S(1)}, f32[1,16,128]{2,1,0:T(8,128)S(1)}, u32[]{:S(2)}, u32[]{:S(2)}) collective-permute-start(f32[1,16,128]{2,1,0:T(8,128)S(1)} %get-tuple-element.43), channel_id=1, source_target_pairs={{0,1},{1,2},{2,3},{3,4},{4,5},{5,6},{6,7},{7,8},{8,9},{9,10},{10,1... | collective-permute-start | bytes 24584 | tf_op jit(solution)/shard_map/ppermute | solution.py:377
  66.7 1.9 %collective-permute-start.7 = (f32[16,128]{1,0:T(8,128)S(1)}, f32[16,128]{1,0:T(8,128)S(1)}, u32[]{:S(2)}, u32[]{:S(2)}) collective-permute-start(f32[16,128]{1,0:T(8,128)S(1)} %get-tuple-element.44), channel_id=1, source_target_pairs={{1,0},{2,1},{3,2},{4,3},{5,4},{6,5},{7,6},{8,7},{9,8},{10,9},{11,1... | collective-permute-start | bytes 24584 | tf_op jit(solution)/shard_map/ppermute | solution.py:377
  68.6 0.0 collective-permute-done.6.behind_ref
  68.6 3.3 %collective-permute-done.7.ahead_ref = f32[16,128]{1,0:T(8,128)S(1)} collective-permute-done((f32[16,128]{1,0:T(8,128)S(1)}, f32[16,128]{1,0:T(8,128)S(1)}, u32[]{:S(2)}, u32[]{:S(2)}) %collective-permute-start.7) | collective-permute-done | bytes 8224 | tf_op jit(solution)/shard_map/ppermute | solution.py:377
  71.9 0.0 collective-permute-done.4.below_ref
  71.9 0.0 collective-permute-done.5.above_ref
  71.9 3.4 %all-to-all-done.2.incoming_ref = bf16[16,128,128]{2,1,0:T(8,128)(2,1)S(1)} async-done(((bf16[16,128,128]{2,1,0:T(8,128)(2,1)}), bf16[16,128,128]{2,1,0:T(8,128)(2,1)S(1)}, u32[]{:S(2)}, u32[]{:S(2)}) %all-to-all-start.2) | async-done | bytes 524320 | tf_op jit(solution)/shard_map/all_to_all | solution.py:381
  75.4 0.0 copy-done.4
  75.4 5.8 %shard_map.169 = (f32[16,64,128]{2,1,0:T(8,128)}, bf16[16,128,128]{2,1,0:T(8,128)(2,1)}, f32[1,64,128]{2,1,0:T(8,128)S(1)}, f32[64,128]{1,0:T(8,128)S(1)}, f32[1...) custom-call(bf16[16,128,128]{2,1,0:T(8,128)(2,1)S(1)} %all-to-all-done.2.incoming_ref, ...), custom_call_target="tpu_custom_call" | custom-call | tf_op jit(solution)/shard_map/pallas_call | solution.py:27
  81.2 7.6 %all-to-all-start.3 = ((bf16[16,128,128]{2,1,0:T(8,128)(2,1)}), bf16[16,128,128]{2,1,0:T(8,128)(2,1)S(1)}, u32[]{:S(2)}, u32[]{:S(2)}) async-start(bf16[16,128,128]{2,1,0:T(8,128)(2,1)} %get-tuple-element.45), calls=%async_computation.3 | async-start | bytes 1048576 | tf_op jit(solution)/shard_map/all_to_all | solution.py:381
  88.8 4.2 %collective-permute-start.8 = (f32[1,64,128]{2,1,0:T(8,128)S(1)}, f32[1,64,128]{2,1,0:T(8,128)S(1)}, u32[]{:S(2)}, u32[]{:S(2)}) collective-permute-start(f32[1,64,128]{2,1,0:T(8,128)S(1)} %get-tuple-element.47), channel_id=1, source_target_pairs={{0,16},{16,32},{32,48},{48,64},{64,80},{80,96},{96,112},{112,128},... | collective-permute-start | bytes 98312 | tf_op jit(solution)/shard_map/ppermute | solution.py:377
  92.9 1.3 collective-permute-start.9
  94.2 2.8 %collective-permute-start.10 = (f32[1,16,128]{2,1,0:T(8,128)S(1)}, f32[1,16,128]{2,1,0:T(8,128)S(1)}, u32[]{:S(2)}, u32[]{:S(2)}) collective-permute-start(f32[1,16,128]{2,1,0:T(8,128)S(1)} %get-tuple-element.49), channel_id=1, source_target_pairs={{0,1},{1,2},{2,3},{3,4},{4,5},{5,6},{6,7},{7,8},{8,9},{9,10},{10,1... | collective-permute-start | bytes 24584 | tf_op jit(solution)/shard_map/ppermute | solution.py:377
  97.0 2.1 %collective-permute-start.11 = (f32[16,128]{1,0:T(8,128)S(1)}, f32[16,128]{1,0:T(8,128)S(1)}, u32[]{:S(2)}, u32[]{:S(2)}) collective-permute-start(f32[16,128]{1,0:T(8,128)S(1)} %get-tuple-element.50), channel_id=1, source_target_pairs={{1,0},{2,1},{3,2},{4,3},{5,4},{6,5},{7,6},{8,7},{9,8},{10,9},{11,1... | collective-permute-start | bytes 24584 | tf_op jit(solution)/shard_map/ppermute | solution.py:377
  99.1 0.0 copy-done.11
  99.1 0.1 copy.27.cols_ref
  99.2 0.0 copy-done.5
  99.2 0.0 copy-done.7
  99.2 0.0 copy-done.8
  99.2 0.0 copy-done.9
  99.2 0.0 copy-start
  99.2 3.7 %shard_map.170.refs_1_.own_ref = f32[64,128]{1,0:T(8,128)S(1)} custom-call(s32[16,4]{1,0:T(8,128)S(1)} %copy.27.cols_ref, bf16[16,48,128]{2,1,0:T(8,128)(2,1)S(1)} %all-to-all-done.whole_ref, bf16[16,4,128,128]{3,2,1,0:T(8,128)(2,1)} %bitcast.15, f32[3,16,128]{2,1,0:T(8,128)S(1)} %bitcast.21, f32[3,16,128]{2,1,0:T(8,128)S(1)} %bitcast.24, ...), custom_call_target="tpu_custom_call" | custom-call | tf_op jit(solution)/shard_map/pallas_call | solution.py:27
  102.9 0.0 collective-permute-done.10.behind_ref
  103.0 0.0 collective-permute-done.11.ahead_ref
  103.0 0.0 collective-permute-done.8.below_ref
  103.0 0.0 collective-permute-done.9.above_ref
  103.0 3.5 %all-to-all-done.3.incoming_ref = bf16[16,128,128]{2,1,0:T(8,128)(2,1)S(1)} async-done(((bf16[16,128,128]{2,1,0:T(8,128)(2,1)}), bf16[16,128,128]{2,1,0:T(8,128)(2,1)S(1)}, u32[]{:S(2)}, u32[]{:S(2)}) %all-to-all-start.3) | async-done | bytes 524320 | tf_op jit(solution)/shard_map/all_to_all | solution.py:381
  106.4 0.0 copy-done.10
  106.5 8.2 %shard_map.171 = (f32[16,64,128]{2,1,0:T(8,128)S(1)}, bf16[1024,2048]{1,0:T(8,128)(2,1)S(1)}, f32[16,80,128]{2,1,0:T(8,128)S(1)}) custom-call(bf16[16,128,128]{2,1,0:T(8,128)(2,1)S(1)} %all-to-all-done.3.incoming_ref, f32[16,128,128]{2,1,0:T(8,128)} %get-tuple-element.38.turned_hbm, f32[16,64,128]{2,1,0:T(8,128)} %get-tuple-element.46.field_hbm, ...), custom_call_target="tpu_custom_call" | custom-call | tf_op jit(solution)/shard_map/pallas_call | solution.py:27
  114.7 17.1 %all_to_all.30.whole_ref = f32[16,80,128]{2,1,0:T(8,128)S(1)} all-to-all(f32[16,80,128]{2,1,0:T(8,128)S(1)} %get-tuple-element.53), channel_id=1, replica_groups=mesh['slab'=16,'col'=16] {'col'}, dimensions={0} | all-to-all | bytes 1310720 | tf_op jit(solution)/shard_map/all_to_all | solution.py:381
  131.8 0.0 copy-done
  131.8 2.9 %shard_map.172 = (f32[16,128]{1,0:T(8,128)S(1)}, f32[3,16,128]{2,1,0:T(8,128)}, f32[3,16,128]{2,1,0:T(8,128)}) custom-call(s32[16,4]{1,0:T(8,128)S(1)} %copy.27.cols_ref, f32[16,80,128]{2,1,0:T(8,128)S(1)} %all_to_all.30.whole_ref, bf16[16,4,128,128]{3,2,1,0:T(8,128)(2,1)S(1)} %bitcast.16, f32[3,16,128]{2,1,0:T(8,128)S(1)} %bitcast.22, ...), custom_call_target="tpu_custom_call" | custom-call | tf_op jit(solution)/shard_map/pallas_call | solution.py:27
  134.6 8.6 %all_to_all.31 = f32[16,1,128]{2,1,0:T(1,128)S(1)} all-to-all(f32[16,1,128]{2,1,0:T(1,128)S(1)} %bitcast.32), channel_id=1, replica_groups=mesh['slab'=16,'col'=16] {'col'}, dimensions={0} | all-to-all | bytes 16384 | tf_op jit(solution)/shard_map/all_to_all | solution.py:381
  143.2 0.0 copy-done.1
  143.2 2.2 %shard_map.173 = f32[16,64,128]{2,1,0:T(8,128)} custom-call(f32[16,128]{1,0:T(8,128)S(1)} %bitcast.31, s32[16,128]{1,0:T(8,128)S(1)} %bitcast.30, bf16[1024,2048]{1,0:T(8,128)(2,1)S(1)} %get-tuple-element.55.fault_hot_ref, f32[16,64,128]{2,1,0:T(8,128)S(1)} %get-tuple-element.56.field_ref, f32[16,64,128]{2,1,0:T(8,128)S(1)} %copy-done.1), custom_call_target="tpu_custom_call" | custom-call | tf_op jit(solution)/shard_map/pallas_call | solution.py:27
  (3 shorter events, 0.0 us)
Async XLA Ops:
  0.6 0.7 copy-start.6
  2.1 13.8 %all-to-all-start = ((bf16[16,48,128]{2,1,0:T(8,128)(2,1)}), bf16[16,48,128]{2,1,0:T(8,128)(2,1)S(1)}, u32[]{:S(2)}, u32[]{:S(2)}) async-start(bf16[16,48,128]{2,1,0:T(8,128)(2,1)} %shard_map.166), calls=%async_computation | async-start | bytes 393216 | tf_op jit(solution)/shard_map/all_to_all | solution.py:381
  9.2 0.7 copy-start.2
  9.9 65.5 %copy-start.4 = (s32[1,1,16,128]{3,2,1,0:T(8,128)S(1)}, s32[1,1,16,128]{3,2,1,0:T(8,128)}, u32[]{:S(2)}) copy-start(s32[1,1,16,128]{3,2,1,0:T(8,128)} %param.21) | copy-start | bytes 24580
  15.9 27.2 %all-to-all-start.1 = ((bf16[16,128,128]{2,1,0:T(8,128)(2,1)}), bf16[16,128,128]{2,1,0:T(8,128)(2,1)S(1)}, u32[]{:S(2)}, u32[]{:S(2)}) async-start(bf16[16,128,128]{2,1,0:T(8,128)(2,1)} %get-tuple-element.32), calls=%async_computation.1 | async-start | bytes 1048576 | tf_op jit(solution)/shard_map/all_to_all | solution.py:381
  25.9 15.6 %collective-permute-start = (f32[2,64,128]{2,1,0:T(8,128)S(1)}, f32[2,64,128]{2,1,0:T(8,128)S(1)}, u32[]{:S(2)}, u32[]{:S(2)}) collective-permute-start(f32[2,64,128]{2,1,0:T(8,128)S(1)} %get-tuple-element.33), channel_id=1, source_target_pairs={{0,16},{16,32},{32,48},{48,64},{64,80},{80,96},{96,112},{112,128},... | collective-permute-start | bytes 196616 | tf_op jit(solution)/shard_map/ppermute | solution.py:377
  30.1 11.4 %collective-permute-start.1 = (f32[64,128]{1,0:T(8,128)S(1)}, f32[64,128]{1,0:T(8,128)S(1)}, u32[]{:S(2)}, u32[]{:S(2)}) collective-permute-start(f32[64,128]{1,0:T(8,128)S(1)} %get-tuple-element.34), channel_id=1, source_target_pairs={{16,0},{32,16},{48,32},{64,48},{80,64},{96,80},{112,96},{128,112},... | collective-permute-start | bytes 98312 | tf_op jit(solution)/shard_map/ppermute | solution.py:377
  31.4 9.0 %collective-permute-start.2 = (f32[2,16,128]{2,1,0:T(8,128)S(1)}, f32[2,16,128]{2,1,0:T(8,128)S(1)}, u32[]{:S(2)}, u32[]{:S(2)}) collective-permute-start(f32[2,16,128]{2,1,0:T(8,128)S(1)} %get-tuple-element.35), channel_id=1, source_target_pairs={{0,1},{1,2},{2,3},{3,4},{4,5},{5,6},{6,7},{7,8},{8,9},{9,10},{10,1... | collective-permute-start | bytes 49160 | tf_op jit(solution)/shard_map/ppermute | solution.py:377
  34.9 5.5 %collective-permute-start.3 = (f32[16,128]{1,0:T(8,128)S(1)}, f32[16,128]{1,0:T(8,128)S(1)}, u32[]{:S(2)}, u32[]{:S(2)}) collective-permute-start(f32[16,128]{1,0:T(8,128)S(1)} %get-tuple-element.36), channel_id=1, source_target_pairs={{1,0},{2,1},{3,2},{4,3},{5,4},{6,5},{7,6},{8,7},{9,8},{10,9},{11,1... | collective-permute-start | bytes 24584 | tf_op jit(solution)/shard_map/ppermute | solution.py:377
  43.1 0.7 copy-start.3
  49.9 49.2 %copy-start.11 = (s32[1,16,4]{1,2,0:T(4,128)S(1)}, s32[1,16,4]{1,2,0:T(4,128)}, u32[]{:S(2)}) copy-start(s32[1,16,4]{1,2,0:T(4,128)} %param.29) | copy-start | bytes 772
  49.9 49.3 %copy-start.5 = (f32[1,3,2048]{2,0,1:T(1,128)S(1)}, f32[1,3,2048]{2,0,1:T(1,128)}, u32[]{:S(2)}) copy-start(f32[1,3,2048]{2,0,1:T(1,128)} %param.24) | copy-start | bytes 73732
  49.9 49.3 %copy-start.7 = (f32[1,3,2048]{2,0,1:T(1,128)S(1)}, f32[1,3,2048]{2,0,1:T(1,128)}, u32[]{:S(2)}) copy-start(f32[1,3,2048]{2,0,1:T(1,128)} %param.25) | copy-start | bytes 73732
  50.0 49.3 %copy-start.8 = (s32[2,1,2048]{2,1,0:T(1,128)S(1)}, s32[2,1,2048]{2,1,0:T(1,128)}, u32[]{:S(2)}) copy-start(s32[2,1,2048]{2,1,0:T(1,128)} %param.27) | copy-start | bytes 49156
  50.0 49.3 %copy-start.9 = (f32[1,2048]{1,0:T(1,128)S(1)}, f32[1,2048]{1,0:T(1,128)}, u32[]{:S(2)}) copy-start(f32[1,2048]{1,0:T(1,128)} %param.26) | copy-start | bytes 24580
  50.0 25.4 %all-to-all-start.2 = ((bf16[16,128,128]{2,1,0:T(8,128)(2,1)}), bf16[16,128,128]{2,1,0:T(8,128)(2,1)S(1)}, u32[]{:S(2)}, u32[]{:S(2)}) async-start(bf16[16,128,128]{2,1,0:T(8,128)(2,1)} %get-tuple-element.37), calls=%async_computation.2 | async-start | bytes 1048576 | tf_op jit(solution)/shard_map/all_to_all | solution.py:381
  58.2 13.7 %collective-permute-start.4 = (f32[1,64,128]{2,1,0:T(8,128)S(1)}, f32[1,64,128]{2,1,0:T(8,128)S(1)}, u32[]{:S(2)}, u32[]{:S(2)}) collective-permute-start(f32[1,64,128]{2,1,0:T(8,128)S(1)} %get-tuple-element.41), channel_id=1, source_target_pairs={{0,16},{16,32},{32,48},{48,64},{64,80},{80,96},{96,112},{112,128},... | collective-permute-start | bytes 98312 | tf_op jit(solution)/shard_map/ppermute | solution.py:377
  62.4 9.5 %collective-permute-start.5 = (f32[64,128]{1,0:T(8,128)S(1)}, f32[64,128]{1,0:T(8,128)S(1)}, u32[]{:S(2)}, u32[]{:S(2)}) collective-permute-start(f32[64,128]{1,0:T(8,128)S(1)} %get-tuple-element.42), channel_id=1, source_target_pairs={{16,0},{32,16},{48,32},{64,48},{80,64},{96,80},{112,96},{128,112},... | collective-permute-start | bytes 98312 | tf_op jit(solution)/shard_map/ppermute | solution.py:377
  63.7 42.7 %copy-start.10 = (s32[1,1,16,128]{3,2,1,0:T(8,128)S(1)}, s32[1,1,16,128]{3,2,1,0:T(8,128)}, u32[]{:S(2)}) copy-start(s32[1,1,16,128]{3,2,1,0:T(8,128)} %param.23) | copy-start | bytes 24580
  63.7 4.9 %collective-permute-start.6 = (f32[1,16,128]{2,1,0:T(8,128)S(1)}, f32[1,16,128]{2,1,0:T(8,128)S(1)}, u32[]{:S(2)}, u32[]{:S(2)}) collective-permute-start(f32[1,16,128]{2,1,0:T(8,128)S(1)} %get-tuple-element.43), channel_id=1, source_target_pairs={{0,1},{1,2},{2,3},{3,4},{4,5},{5,6},{6,7},{7,8},{8,9},{9,10},{10,1... | collective-permute-start | bytes 24584 | tf_op jit(solution)/shard_map/ppermute | solution.py:377
  66.7 5.3 %collective-permute-start.7 = (f32[16,128]{1,0:T(8,128)S(1)}, f32[16,128]{1,0:T(8,128)S(1)}, u32[]{:S(2)}, u32[]{:S(2)}) collective-permute-start(f32[16,128]{1,0:T(8,128)S(1)} %get-tuple-element.44), channel_id=1, source_target_pairs={{1,0},{2,1},{3,2},{4,3},{5,4},{6,5},{7,6},{8,7},{9,8},{10,9},{11,1... | collective-permute-start | bytes 24584 | tf_op jit(solution)/shard_map/ppermute | solution.py:377
  81.2 25.3 %all-to-all-start.3 = ((bf16[16,128,128]{2,1,0:T(8,128)(2,1)}), bf16[16,128,128]{2,1,0:T(8,128)(2,1)S(1)}, u32[]{:S(2)}, u32[]{:S(2)}) async-start(bf16[16,128,128]{2,1,0:T(8,128)(2,1)} %get-tuple-element.45), calls=%async_computation.3 | async-start | bytes 1048576 | tf_op jit(solution)/shard_map/all_to_all | solution.py:381
  88.8 14.2 %collective-permute-start.8 = (f32[1,64,128]{2,1,0:T(8,128)S(1)}, f32[1,64,128]{2,1,0:T(8,128)S(1)}, u32[]{:S(2)}, u32[]{:S(2)}) collective-permute-start(f32[1,64,128]{2,1,0:T(8,128)S(1)} %get-tuple-element.47), channel_id=1, source_target_pairs={{0,16},{16,32},{32,48},{48,64},{64,80},{80,96},{96,112},{112,128},... | collective-permute-start | bytes 98312 | tf_op jit(solution)/shard_map/ppermute | solution.py:377
  92.9 10.1 %collective-permute-start.9 = (f32[64,128]{1,0:T(8,128)S(1)}, f32[64,128]{1,0:T(8,128)S(1)}, u32[]{:S(2)}, u32[]{:S(2)}) collective-permute-start(f32[64,128]{1,0:T(8,128)S(1)} %get-tuple-element.48), channel_id=1, source_target_pairs={{16,0},{32,16},{48,32},{64,48},{80,64},{96,80},{112,96},{128,112},... | collective-permute-start | bytes 98312 | tf_op jit(solution)/shard_map/ppermute | solution.py:377
  94.2 8.7 %collective-permute-start.10 = (f32[1,16,128]{2,1,0:T(8,128)S(1)}, f32[1,16,128]{2,1,0:T(8,128)S(1)}, u32[]{:S(2)}, u32[]{:S(2)}) collective-permute-start(f32[1,16,128]{2,1,0:T(8,128)S(1)} %get-tuple-element.49), channel_id=1, source_target_pairs={{0,1},{1,2},{2,3},{3,4},{4,5},{5,6},{6,7},{7,8},{8,9},{9,10},{10,1... | collective-permute-start | bytes 24584 | tf_op jit(solution)/shard_map/ppermute | solution.py:377
  97.0 5.9 %collective-permute-start.11 = (f32[16,128]{1,0:T(8,128)S(1)}, f32[16,128]{1,0:T(8,128)S(1)}, u32[]{:S(2)}, u32[]{:S(2)}) collective-permute-start(f32[16,128]{1,0:T(8,128)S(1)} %get-tuple-element.50), channel_id=1, source_target_pairs={{1,0},{2,1},{3,2},{4,3},{5,4},{6,5},{7,6},{8,7},{9,8},{10,9},{11,1... | collective-permute-start | bytes 24584 | tf_op jit(solution)/shard_map/ppermute | solution.py:377
  99.2 32.5 %copy-start = (bf16[1,16,4,128,128]{4,3,2,1,0:T(8,128)(2,1)S(1)}, bf16[1,16,4,128,128]{4,3,2,1,0:T(8,128)(2,1)}, u32[]{:S(2)}) copy-start(bf16[1,16,4,128,128]{4,3,2,1,0:T(8,128)(2,1)} %param.28) | copy-start | bytes 6291460
  106.5 36.8 %copy-start.1 = (f32[16,64,128]{2,1,0:T(8,128)S(1)}, f32[16,64,128]{2,1,0:T(8,128)}, u32[]{:S(2)}) copy-start(f32[16,64,128]{2,1,0:T(8,128)} %get-tuple-element.40.diag_hbm.inverse_ref) | copy-start | bytes 1572868

commit v3 on v2

--- a/solution.py
+++ b/solution.py
@@ -92,50 +92,71 @@
     values_ref[128:, q * 128 : (q + 1) * 128] = low
 
 
-def ready_kernel(slip_ref, out_ref):
-    parts, rows, _ = slip_ref.shape
-    for p in range(parts):
-        out_ref[0, p * rows : (p + 1) * rows, :] = slip_ref[p].astype(BF16)
-    mine = out_ref[0]
-    for o in range(1, out_ref.shape[0]):
-        out_ref[o] = mine
+def odd(axis):
+    return lax.axis_index(axis) % 2 == 1
+
+
+def put_edges(field_ref, edge_refs):
+    z_one, z_two, x_one, x_two = edge_refs
+    depth, width, _ = field_ref.shape
+    swap_z, swap_x = odd("slab"), odd("col")
+    head, tail = field_ref[0], field_ref[depth - 1]
+    z_one[0] = jnp.where(swap_z, head, tail)
+    z_two[0] = jnp.where(swap_z, tail, head)
+    for i in range(depth):
+        head, tail = field_ref[i, 0:1, :], field_ref[i, width - 1 : width, :]
+        x_one[0, i : i + 1, :] = jnp.where(swap_x, head, tail)
+        x_two[0, i : i + 1, :] = jnp.where(swap_x, tail, head)
 
 
 def first_kernel(
     field_hbm,
     face_z_hbm,
     face_x_hbm,
+    slip_hbm,
     cell_ref,
     out_hbm,
-    up_ref,
-    down_ref,
-    right_ref,
-    left_ref,
+    ready_hbm,
+    kept_ref,
+    z_one,
+    z_two,
+    x_one,
+    x_two,
     hot_ref,
     field_ref,
     wall_ref,
+    slip_ref,
     out_ref,
+    ready_ref,
     sems,
 ):
     depth, width, lateral = field_ref.shape
     reads = begin(
         [
             (field_hbm, field_ref),
-            (face_z_hbm.at[depth - 1], up_ref.at[1]),
             (face_x_hbm.at[:, pl.ds(width - 8, 8), :], wall_ref),
+            (face_z_hbm.at[depth - 1], z_one.at[1]),
+            (face_z_hbm.at[depth - 1], z_two.at[1]),
+            (slip_hbm, slip_ref),
         ],
         sems,
     )
+    kept_ref[...] = cell_ref[...]
     fill_hot(hot_ref, cell_ref[...])
     finish(reads)
     gather_lines(hot_ref, field_ref[...].reshape(depth * width, lateral), out_ref)
-    writes = begin([(out_ref, out_hbm)], sems, 3)
-    up_ref[0] = field_ref[depth - 1]
-    down_ref[...] = field_ref[0]
+    writes = begin([(out_ref, out_hbm)], sems, 5)
+    parts, rows, _ = slip_ref.shape
+    for p in range(parts):
+        ready_ref[0, p * rows : (p + 1) * rows, :] = slip_ref[p].astype(BF16)
+    mine = ready_ref[0]
+    for o in range(1, ready_ref.shape[0]):
+        ready_ref[o] = mine
+    writes += begin([(ready_ref, ready_hbm)], sems, 6)
+    put_edges(field_ref, (z_one, z_two, x_one, x_two))
     for i in range(depth):
-        right_ref[0, i : i + 1, :] = field_ref[i, width - 1 : width, :]
-        right_ref[1, i : i + 1, :] = wall_ref[i, 7:8, :]
-        left_ref[i : i + 1, :] = field_ref[i, 0:1, :]
+        x_one[1, i : i + 1, :] = wall_ref[i, 7:8, :]
+        x_two[1, i : i + 1, :] = wall_ref[i, 7:8, :]
     finish(writes)
 
 
@@ -151,12 +172,10 @@
     face_y_hbm,
     diag_hbm,
     cell_ref,
-    below_ref,
-    above_ref,
-    behind_ref,
-    ahead_ref,
-    lower_z_ref,
-    lower_x_ref,
+    z_one,
+    z_two,
+    x_one,
+    x_two,
     *refs,
 ):
     refs = list(refs)
@@ -169,6 +188,7 @@
         link_ref = refs.pop()
     if not last:
         new_ref, out_ref = refs.pop(), refs.pop()
+    faces = [z_one, z_two, x_one, x_two] if first else [refs.pop(0) for _ in range(4)]
     linked_reads = begin([(turned_hbm, turned_ref)], sems)
     reads = begin(
         list(
@@ -200,28 +220,36 @@
         fault_ref, own_ref, new_ref, fault_hot_ref, press_ref = refs
     elif first:
         new_hbm, out_hbm, turned_out, inverse_out = refs[:4]
-        up_ref, down_ref, right_ref, left_ref = refs[4:]
+        edge_refs = refs[4:]
         writes += begin([(turned_ref, turned_out)], sems, 8)
     else:
-        new_hbm, out_hbm, up_ref, down_ref, right_ref, left_ref = refs
+        new_hbm, out_hbm = refs[:2]
+        edge_refs = refs[2:]
+    swap_z, swap_x = odd("slab"), odd("col")
+    below_z = jnp.where(swap_z, z_one[0], z_two[0])
+    above_z = jnp.where(swap_z, z_two[0], z_one[0])
+    edge_z = jnp.where(swap_z, faces[0][1], faces[1][1])
+    behind_x = jnp.where(swap_x, x_one[0], x_two[0])
+    ahead_x = jnp.where(swap_x, x_two[0], x_one[0])
+    edge_x = jnp.where(swap_x, faces[2][1], faces[3][1])
     across = iota((width, lateral), 0)
     along = iota((width, lateral), 1)
     for i in range(depth):
         field = field_ref[i]
         face_z = face_z_ref[i]
-        lower_z = face_z_ref[i - 1] if i > 0 else lower_z_ref[1]
-        above = field_ref[i + 1] if i < depth - 1 else above_ref[...]
-        below = field_ref[i - 1] if i > 0 else below_ref[0]
+        lower_z = face_z_ref[i - 1] if i > 0 else edge_z
+        above = field_ref[i + 1] if i < depth - 1 else above_z
+        below = field_ref[i - 1] if i > 0 else below_z
         total = source_ref[i] + linked[i * width : (i + 1) * width]
         total = total + face_z * above + lower_z * below
         face_x = face_x_ref[i]
-        lower_x = lower_x_ref[1, i : i + 1, :]
+        lower_x = edge_x[i : i + 1, :]
         ahead = jnp.where(
-            across == width - 1, ahead_ref[i : i + 1, :], pltpu.roll(field, width - 1, 0)
+            across == width - 1, ahead_x[i : i + 1, :], pltpu.roll(field, width - 1, 0)
         )
         flow = jnp.where(
             across == 0,
-            lower_x * behind_ref[0, i : i + 1, :],
+            lower_x * behind_x[i : i + 1, :],
             pltpu.roll(face_x * field, 1, 0),
         )
         total = total + face_x * ahead + flow
@@ -252,8 +280,15 @@
             got = got[:lateral] + got[lateral:]
             lane = fault_ref[q : q + 1, :] & 127
             got = jnp.sum(jnp.where(side == lane, got, 0.0), 0, keepdims=True)
-            press_ref[0, q : q + 1, :] = got
-        press_ref[0, fault_ref.shape[0] :, :] = own_ref[...]
+            face_x_ref[0, q : q + 1, :] = got
+        rows = fault_ref.shape[0]
+        planes = [
+            *halves(face_x_ref[0, :rows, :]),
+            *halves(own_ref[:rows]),
+            *[own_ref[n * rows : (n + 1) * rows].astype(BF16) for n in (1, 2, 3)],
+        ]
+        for n, plane in enumerate(planes):
+            press_ref[0, n * rows : (n + 1) * rows, :] = plane
         mine = press_ref[0]
         for o in range(1, press_ref.shape[0]):
             press_ref[o] = mine
@@ -263,11 +298,7 @@
             writes += begin([(diag_ref, inverse_out)], sems, 10)
         gather_lines(hot_ref, lines, out_ref)
         writes += begin([(out_ref, out_hbm)], sems, 11)
-        up_ref[0] = new_ref[depth - 1]
-        down_ref[...] = new_ref[0]
-        for i in range(depth):
-            right_ref[0, i : i + 1, :] = new_ref[i, width - 1 : width, :]
-            left_ref[i : i + 1, :] = new_ref[i, 0:1, :]
+        put_edges(new_ref, edge_refs)
     finish(writes)
 
 
@@ -334,15 +365,14 @@
     sources = whole_ref.shape[0]
     rows = base_ref.shape[1]
     ids = sources * rows
+    def part(n):
+        plane = whole_ref[:, n * rows : (n + 1) * rows, :].astype(F32)
+        return plane.reshape(ids, 128)
+
     for c in range(sources):
-        for o in range(sources):
-            n = o * rows + c
-            press_ref[n : n + 1, :] = whole_ref[c, o : o + 1, :]
-
-    def part(n):
-        return whole_ref[:, (n + 1) * rows : (n + 2) * rows, :].reshape(ids, 128)
-
-    slips = [part(0) + part(1) * press_ref[...], part(2), part(3)]
+        press = whole_ref[c, :rows, :].astype(F32) + whole_ref[c, rows : 2 * rows, :]
+        press_ref[pl.ds(c, sources, stride=rows), :] = press
+    slips = [part(2) + part(3) + part(4) * press_ref[...], part(5), part(6)]
     for p in range(3):
         tiles_ref[p] = slips[p].astype(BF16).astype(F32)
     coupled = couple(cols_ref, tiles_ref, blocks_ref)
@@ -371,10 +401,13 @@
     out_ref[...] = field_ref[...] + returned * inverse_ref[...]
 
 
-def shift(block, axis, step):
-    count = lax.axis_size(axis)
-    route = [(i, i + step) for i in range(count) if 0 <= i + step < count]
-    return lax.ppermute(block, axis, route)
+def exchange(edges):
+    got = []
+    for edge, (axis, start) in zip(edges, (("slab", 0), ("slab", 1), ("col", 0), ("col", 1))):
+        count = lax.axis_size(axis)
+        pairs = [(i, i + 1) for i in range(start, count - 1, 2)]
+        got.append(lax.ppermute(edge, axis, pairs + [(j, i) for i, j in pairs]))
+    return got
 
 
 def swap(blocks, axis):
@@ -420,49 +453,51 @@
     block = pltpu.VMEM((depth, width, lateral), F32)
     packet = pltpu.VMEM((slabs, lateral, 128), BF16)
     values = pltpu.VMEM((2 * lateral, slots), BF16)
-    edges = [((1, *layer), F32), (layer, F32), ((1, *wall), F32), (wall, F32)]
-
-    (ready,) = call(ready_kernel, [((columns, 3 * rows, 128), BF16)], slip0)
-    whole = swap(ready, "col")
-    outgoing, up, down, right, left = call(
+    edges = [((1, *layer), F32)] * 2 + [((1, *wall), F32)] * 2
+    doubled = [((2, *layer), F32)] * 2 + [((2, *wall), F32)] * 2
+    planes = 7 * rows
+
+    outgoing, ready, cells, *sides = call(
         first_kernel,
         [
             ((slabs, lateral, 128), BF16, 0),
-            ((2, *layer), F32),
-            (layer, F32),
-            ((2, *wall), F32),
-            (wall, F32),
+            ((columns, 3 * rows, 128), BF16, 0),
+            (cells.shape, jnp.int32),
+            *doubled,
         ],
         pressure,
         trans_z,
         trans_x,
+        slip0,
         cells,
-        hbm=(0, 1, 2),
+        hbm=(0, 1, 2, 3),
         scratch=(
             table,
             block,
             pltpu.VMEM((depth, 8, lateral), F32),
+            pltpu.VMEM(slip0.shape, F32),
             packet,
-            pltpu.SemaphoreType.DMA((4,)),
+            pltpu.VMEM((columns, 3 * rows, 128), BF16),
+            pltpu.SemaphoreType.DMA((7,)),
         ),
     )
-    whole, outgoing = lax.optimization_barrier((whole, outgoing))
     incoming = swap(outgoing, "slab")
-    below = lower_z = shift(up, "slab", 1)
-    behind = lower_x = shift(right, "col", 1)
-    above = shift(down, "slab", -1)
-    ahead = shift(left, "col", -1)
+    sides = exchange(sides)
+    ready, incoming, sides = lax.optimization_barrier((ready, incoming, sides))
+    faces = sides
+    whole = swap(ready, "col")
     turned, diag = nnc_trans[0, 0], accum
     field = pressure
     for sweep in range(ITERS_FLOW):
         first = sweep == 0
         last = sweep == ITERS_FLOW - 1
-        extra = [faults, own] if last else []
+        extra = [] if first else list(faces)
         if last:
+            extra += [faults, own]
             outs = [
                 (grid[0], F32),
                 ((lines, nodes), BF16),
-                ((columns, columns + 4 * rows, 128), F32),
+                ((columns, planes, 128), BF16),
             ]
         else:
             outs = [(*grid, 0), ((slabs, lateral, 128), BF16, 0)]
@@ -481,12 +516,7 @@
             trans_y,
             diag,
             cells,
-            below,
-            above,
-            behind,
-            ahead,
-            lower_z,
-            lower_x,
+            *sides,
             *extra,
             hbm=range(1, 8),
             scratch=[
@@ -502,16 +532,12 @@
         if last:
             field, fault_hot, whole = got
             break
+        field, outgoing = got[:2]
         if first:
             turned, diag = got[2:4]
-            whole, _ = lax.optimization_barrier((whole, got[-1]))
-        field, outgoing = got[:2]
-        up, down, right, left = got[-4:]
+            whole, outgoing = lax.optimization_barrier((whole, outgoing))
         incoming = swap(outgoing, "slab")
-        below = shift(up, "slab", 1)
-        behind = shift(right, "col", 1)
-        above = shift(down, "slab", -1)
-        ahead = shift(left, "col", -1)
+        sides = exchange(got[-4:])
         if first:
             (own,) = call(
                 contact_kernel,

time: 147 us -> 140 us (0.952)
  starting transfers between devices: 64.6 us -> 54.4 us
  waiting for transfers between devices: 19.5 us -> 23 us
  blocking collectives: 25.7 us -> 28.4 us
    ppermute x12, waiting for transfers between devices: 7.97 us -> 19.3 us  [exchange(): got.append(lax.ppermute(edge, axis, pairs + [(j, i) for i, j in pairs]))]
    ppermute x12, starting transfers between devices: 31.6 us -> 21.7 us  [exchange(): got.append(lax.ppermute(edge, axis, pairs + [(j, i) for i, j in pairs]))]
    all_to_all x4, waiting for transfers between devices: 11.6 us -> 3.74 us  [swap(): return lax.all_to_all(blocks, axis, split_axis=0, concat_axis=0, tiled=True)]
    all_to_all x2, blocking collectives: 25.7 us -> 28.4 us  [swap(): return lax.all_to_all(blocks, axis, split_axis=0, concat_axis=0, tiled=True)]
    pallas_call x8 -> x7, Pallas kernels: 32.5 us -> 32 us  [call(): pl.pallas_call(body, in_specs=[pl.BlockSpec(memory_space=space) for space...]
  transfers between devices with their start and end apart: 16 -> 16, of which waited for: 7 -> 7; matrix products, arithmetic and copies ran while one was open for 0% -> 0% of each run, Pallas kernels for 5% -> 7%
where the time goes in v3:
time: 140 us; the launch traced here: 139 us
  starting transfers between devices  54.4 us (39%)
  Pallas kernels  32 us (23%)
  blocking collectives  28.4 us (20%)
  waiting for transfers between devices  23 us (16%)
    all_to_all x4, starting transfers between devices, swap(): return lax.all_to_all(blocks, axis, split_axis=0, concat_axis=0, tiled=True)  32.7 us
    pallas_call x7, Pallas kernels, call(): pl.pallas_call(body, in_specs=[pl.BlockSpec(memory_space=space) for space...  32 us
    all_to_all x2, blocking collectives, swap(): return lax.all_to_all(blocks, axis, split_axis=0, concat_axis=0, tiled=True)  28.4 us
    ppermute x12, starting transfers between devices, exchange(): got.append(lax.ppermute(edge, axis, pairs + [(j, i) for i, j in pairs]))  21.7 us
    ppermute x12, waiting for transfers between devices, exchange(): got.append(lax.ppermute(edge, axis, pairs + [(j, i) for i, j in pairs]))  19.3 us
    all_to_all x4, waiting for transfers between devices, swap(): return lax.all_to_all(blocks, axis, split_axis=0, concat_axis=0, tiled=True)  3.74 us
  transfers between devices with their start and end apart: 16, of which 7 were waited for; matrix products, arithmetic and copies ran while one was open for 0% of the time, Pallas kernels for 7%

profile of v3, /device:TPU:1, one launch (start us, length us, event | category | flops | bytes accessed | tf_op | source)
XLA Modules:
  0.0 139.4 jit_solution(2543483141991558788)
XLA Ops:
  0.6 0.0 copy-start.7
  0.6 0.7 copy-done.7
  1.3 3.0 %shard_map.166 = (bf16[16,128,128]{2,1,0:T(8,128)(2,1)}, bf16[16,48,128]{2,1,0:T(8,128)(2,1)}, s32[16,128]{1,0:T(8,128)S(1)}, f32[2,64,128]{2,1,0:T(8,128)S(1)},...) custom-call(f32[16,64,128]{2,1,0:T(8,128)} %field_hbm.3, ...), custom_call_target="tpu_custom_call" | custom-call | tf_op jit(solution)/shard_map/pallas_call | solution.py:27
  4.3 11.7 %all-to-all-start = ((bf16[16,128,128]{2,1,0:T(8,128)(2,1)}), bf16[16,128,128]{2,1,0:T(8,128)(2,1)S(1)}, u32[]{:S(2)}, u32[]{:S(2)}) async-start(bf16[16,128,128]{2,1,0:T(8,128)(2,1)} %get-tuple-element.39), calls=%async_computation | async-start | bytes 1048576 | tf_op jit(solution)/shard_map/all_to_all | solution.py:414
  16.1 2.3 %collective-permute-start = (f32[2,64,128]{2,1,0:T(8,128)S(1)}, f32[2,64,128]{2,1,0:T(8,128)S(1)}, u32[]{:S(2)}, u32[]{:S(2)}) collective-permute-start(f32[2,64,128]{2,1,0:T(8,128)S(1)} %get-tuple-element.40), channel_id=1, source_target_pairs={{0,16},{32,48},{64,80},{96,112},{128,144},{160,176},{192,208},{224... | collective-permute-start | bytes 196616 | tf_op jit(solution)/shard_map/ppermute | solution.py:409
  18.3 0.7 collective-permute-start.1
  19.0 1.6 %collective-permute-start.2 = (f32[2,16,128]{2,1,0:T(8,128)S(1)}, f32[2,16,128]{2,1,0:T(8,128)S(1)}, u32[]{:S(2)}, u32[]{:S(2)}) collective-permute-start(f32[2,16,128]{2,1,0:T(8,128)S(1)} %get-tuple-element.42), channel_id=1, source_target_pairs={{0,1},{2,3},{4,5},{6,7},{8,9},{10,11},{12,13},{14,15},{1,0},{3,2},... | collective-permute-start | bytes 49160 | tf_op jit(solution)/shard_map/ppermute | solution.py:409
  20.6 2.6 %collective-permute-start.3 = (f32[2,16,128]{2,1,0:T(8,128)S(1)}, f32[2,16,128]{2,1,0:T(8,128)S(1)}, u32[]{:S(2)}, u32[]{:S(2)}) collective-permute-start(f32[2,16,128]{2,1,0:T(8,128)S(1)} %get-tuple-element.43), channel_id=1, source_target_pairs={{1,2},{3,4},{5,6},{7,8},{9,10},{11,12},{13,14},{2,1},{4,3},{6,5},{... | collective-permute-start | bytes 49160 | tf_op jit(solution)/shard_map/ppermute | solution.py:409
  23.2 0.0 collective-permute-done.2.x_one.refs_2_
  23.2 4.9 %collective-permute-done.3.x_two.refs_3_ = f32[2,16,128]{2,1,0:T(8,128)S(1)} collective-permute-done((f32[2,16,128]{2,1,0:T(8,128)S(1)}, f32[2,16,128]{2,1,0:T(8,128)S(1)}, u32[]{:S(2)}, u32[]{:S(2)}) %collective-permute-start.3) | collective-permute-done | bytes 16416 | tf_op jit(solution)/shard_map/ppermute | solution.py:409
  28.1 4.9 %collective-permute-done.z_one.refs_0_ = f32[2,64,128]{2,1,0:T(8,128)S(1)} collective-permute-done((f32[2,64,128]{2,1,0:T(8,128)S(1)}, f32[2,64,128]{2,1,0:T(8,128)S(1)}, u32[]{:S(2)}, u32[]{:S(2)}) %collective-permute-start) | collective-permute-done | bytes 65568 | tf_op jit(solution)/shard_map/ppermute | solution.py:409
  33.0 0.0 collective-permute-done.1.z_two.refs_1_
  33.0 0.0 all-to-all-done.incoming_ref
  33.0 8.7 %all-to-all-start.1 = ((bf16[16,48,128]{2,1,0:T(8,128)(2,1)}), bf16[16,48,128]{2,1,0:T(8,128)(2,1)S(1)}, u32[]{:S(2)}, u32[]{:S(2)}) async-start(bf16[16,48,128]{2,1,0:T(8,128)(2,1)} %get-tuple-element.44), calls=%async_computation.1 | async-start | bytes 393216 | tf_op jit(solution)/shard_map/all_to_all | solution.py:414
  41.7 6.1 %shard_map.167 = (f32[16,64,128]{2,1,0:T(8,128)}, bf16[16,128,128]{2,1,0:T(8,128)(2,1)}, f32[16,128,128]{2,1,0:T(8,128)}, f32[16,64,128]{2,1,0:T(8,128)}, f32[1,...) custom-call(bf16[16,128,128]{2,1,0:T(8,128)(2,1)S(1)} %all-to-all-done.i, ...), custom_call_target="tpu_custom_call" | custom-call | tf_op jit(solution)/shard_map/pallas_call | solution.py:27
  47.8 0.0 copy-start.8
  47.8 0.0 copy-start.2
  47.8 0.0 copy-start.3
  47.8 0.0 copy-start.4
  47.8 0.0 copy-start.5
  47.9 0.4 all-to-all-done.1.whole_ref
  48.3 4.8 %all-to-all-start.2 = ((bf16[16,128,128]{2,1,0:T(8,128)(2,1)}), bf16[16,128,128]{2,1,0:T(8,128)(2,1)S(1)}, u32[]{:S(2)}, u32[]{:S(2)}) async-start(bf16[16,128,128]{2,1,0:T(8,128)(2,1)} %get-tuple-element.52), calls=%async_computation.2 | async-start | bytes 1048576 | tf_op jit(solution)/shard_map/all_to_all | solution.py:414
  53.2 2.3 %collective-permute-start.4 = (f32[1,64,128]{2,1,0:T(8,128)S(1)}, f32[1,64,128]{2,1,0:T(8,128)S(1)}, u32[]{:S(2)}, u32[]{:S(2)}) collective-permute-start(f32[1,64,128]{2,1,0:T(8,128)S(1)} %get-tuple-element.56), channel_id=1, source_target_pairs={{0,16},{32,48},{64,80},{96,112},{128,144},{160,176},{192,208},{224... | collective-permute-start | bytes 98312 | tf_op jit(solution)/shard_map/ppermute | solution.py:409
  55.4 0.7 collective-permute-start.5
  56.1 1.7 %collective-permute-start.6 = (f32[1,16,128]{2,1,0:T(8,128)S(1)}, f32[1,16,128]{2,1,0:T(8,128)S(1)}, u32[]{:S(2)}, u32[]{:S(2)}) collective-permute-start(f32[1,16,128]{2,1,0:T(8,128)S(1)} %get-tuple-element.58), channel_id=1, source_target_pairs={{0,1},{2,3},{4,5},{6,7},{8,9},{10,11},{12,13},{14,15},{1,0},{3,2},... | collective-permute-start | bytes 24584 | tf_op jit(solution)/shard_map/ppermute | solution.py:409
  57.8 2.5 %collective-permute-start.7 = (f32[1,16,128]{2,1,0:T(8,128)S(1)}, f32[1,16,128]{2,1,0:T(8,128)S(1)}, u32[]{:S(2)}, u32[]{:S(2)}) collective-permute-start(f32[1,16,128]{2,1,0:T(8,128)S(1)} %get-tuple-element.59), channel_id=1, source_target_pairs={{1,2},{3,4},{5,6},{7,8},{9,10},{11,12},{13,14},{2,1},{4,3},{6,5},{... | collective-permute-start | bytes 24584 | tf_op jit(solution)/shard_map/ppermute | solution.py:409
  60.3 0.0 collective-permute-done.6.x_one
  60.3 6.3 %collective-permute-done.7.x_two = f32[1,16,128]{2,1,0:T(8,128)S(1)} collective-permute-done((f32[1,16,128]{2,1,0:T(8,128)S(1)}, f32[1,16,128]{2,1,0:T(8,128)S(1)}, u32[]{:S(2)}, u32[]{:S(2)}) %collective-permute-start.7) | collective-permute-done | bytes 8224 | tf_op jit(solution)/shard_map/ppermute | solution.py:409
  66.6 0.0 collective-permute-done.4.z_one
  66.6 0.0 collective-permute-done.5.z_two
  66.6 2.5 %all-to-all-done.2.incoming_ref = bf16[16,128,128]{2,1,0:T(8,128)(2,1)S(1)} async-done(((bf16[16,128,128]{2,1,0:T(8,128)(2,1)}), bf16[16,128,128]{2,1,0:T(8,128)(2,1)S(1)}, u32[]{:S(2)}, u32[]{:S(2)}) %all-to-all-start.2) | async-done | bytes 524320 | tf_op jit(solution)/shard_map/all_to_all | solution.py:414
  69.1 0.0 copy-start.6
  69.1 5.8 %shard_map.168 = (f32[16,64,128]{2,1,0:T(8,128)}, bf16[16,128,128]{2,1,0:T(8,128)(2,1)}, f32[1,64,128]{2,1,0:T(8,128)S(1)}, f32[1,64,128]{2,1,0:T(8,128)S(1)}, f...) custom-call(bf16[16,128,128]{2,1,0:T(8,128)(2,1)S(1)} %all-to-all-done.2.incoming_ref, ...), custom_call_target="tpu_custom_call" | custom-call | tf_op jit(solution)/shard_map/pallas_call | solution.py:27
  74.9 7.4 %all-to-all-start.3 = ((bf16[16,128,128]{2,1,0:T(8,128)(2,1)}), bf16[16,128,128]{2,1,0:T(8,128)(2,1)S(1)}, u32[]{:S(2)}, u32[]{:S(2)}) async-start(bf16[16,128,128]{2,1,0:T(8,128)(2,1)} %get-tuple-element.60), calls=%async_computation.3 | async-start | bytes 1048576 | tf_op jit(solution)/shard_map/all_to_all | solution.py:414
  82.3 0.0 copy-start
  82.3 2.3 %collective-permute-start.8 = (f32[1,64,128]{2,1,0:T(8,128)S(1)}, f32[1,64,128]{2,1,0:T(8,128)S(1)}, u32[]{:S(2)}, u32[]{:S(2)}) collective-permute-start(f32[1,64,128]{2,1,0:T(8,128)S(1)} %get-tuple-element.62), channel_id=1, source_target_pairs={{0,16},{32,48},{64,80},{96,112},{128,144},{160,176},{192,208},{224... | collective-permute-start | bytes 98312 | tf_op jit(solution)/shard_map/ppermute | solution.py:409
  84.7 0.7 collective-permute-start.9
  85.3 1.8 %collective-permute-start.10 = (f32[1,16,128]{2,1,0:T(8,128)S(1)}, f32[1,16,128]{2,1,0:T(8,128)S(1)}, u32[]{:S(2)}, u32[]{:S(2)}) collective-permute-start(f32[1,16,128]{2,1,0:T(8,128)S(1)} %get-tuple-element.64), channel_id=1, source_target_pairs={{0,1},{2,3},{4,5},{6,7},{8,9},{10,11},{12,13},{14,15},{1,0},{3,2},... | collective-permute-start | bytes 24584 | tf_op jit(solution)/shard_map/ppermute | solution.py:409
  87.1 2.6 %collective-permute-start.11 = (f32[1,16,128]{2,1,0:T(8,128)S(1)}, f32[1,16,128]{2,1,0:T(8,128)S(1)}, u32[]{:S(2)}, u32[]{:S(2)}) collective-permute-start(f32[1,16,128]{2,1,0:T(8,128)S(1)} %get-tuple-element.65), channel_id=1, source_target_pairs={{1,2},{3,4},{5,6},{7,8},{9,10},{11,12},{13,14},{2,1},{4,3},{6,5},{... | collective-permute-start | bytes 24584 | tf_op jit(solution)/shard_map/ppermute | solution.py:409
  89.8 0.0 copy-done.8
  89.8 0.1 copy.27.cols_ref
  89.9 0.0 copy-done.2
  89.9 0.0 copy-done.3
  89.9 0.0 copy-done.4
  89.9 0.0 copy-done.5
  89.9 3.7 %shard_map.169.refs_5_.own_ref = f32[64,128]{1,0:T(8,128)S(1)} custom-call(s32[16,4]{1,0:T(8,128)S(1)} %copy.27.cols_ref, bf16[16,48,128]{2,1,0:T(8,128)(2,1)S(1)} %all-to-all-done.1.whole_ref, bf16[16,4,128,128]{3,2,1,0:T(8,128)(2,1)} %bitcast.15, f32[3,16,128]{2,1,0:T(8,128)S(1)} %bitcast.17, f32[3,16,128]{2,1,0:T(8,128)S(1)} %bitcast.20, ...), custom_call_target="tpu_custom_call" | custom-call | tf_op jit(solution)/shard_map/pallas_call | solution.py:27
  93.6 0.0 collective-permute-done.10.x_one
  93.6 3.2 %collective-permute-done.11.x_two = f32[1,16,128]{2,1,0:T(8,128)S(1)} collective-permute-done((f32[1,16,128]{2,1,0:T(8,128)S(1)}, f32[1,16,128]{2,1,0:T(8,128)S(1)}, u32[]{:S(2)}, u32[]{:S(2)}) %collective-permute-start.11) | collective-permute-done | bytes 8224 | tf_op jit(solution)/shard_map/ppermute | solution.py:409
  96.8 0.0 collective-permute-done.8.z_one
  96.8 0.0 collective-permute-done.9.z_two
  96.8 0.8 all-to-all-done.3.incoming_ref
  97.6 0.0 copy-done.6
  97.6 0.0 copy-start.1
  97.6 8.3 %shard_map.170 = (f32[16,64,128]{2,1,0:T(8,128)S(1)}, bf16[1024,2048]{1,0:T(8,128)(2,1)S(1)}, bf16[16,112,128]{2,1,0:T(8,128)(2,1)S(1)}) custom-call(bf16[16,128,128]{2,1,0:T(8,128)(2,1)S(1)} %all-to-all-done.3.incoming_ref, f32[16,128,128]{2,1,0:T(8,128)} %get-tuple-element.53.turned_hbm, f32[16,64,128]{2,1,0:T(8,128)} %get-tuple-element.61.field_hbm, ...), custom_call_target="tpu_custom_call" | custom-call | tf_op jit(solution)/shard_map/pallas_call | solution.py:27
  105.9 19.1 %all_to_all.30.whole_ref = bf16[16,112,128]{2,1,0:T(8,128)(2,1)S(1)} all-to-all(bf16[16,112,128]{2,1,0:T(8,128)(2,1)S(1)} %get-tuple-element.67), channel_id=1, replica_groups=mesh['slab'=16,'col'=16] {'col'}, dimensions={0} | all-to-all | bytes 917504 | tf_op jit(solution)/shard_map/all_to_all | solution.py:414
  125.1 0.0 copy-done
  125.1 2.8 %shard_map.171 = (f32[16,128]{1,0:T(8,128)S(1)}, f32[3,16,128]{2,1,0:T(8,128)}, f32[3,16,128]{2,1,0:T(8,128)}) custom-call(s32[16,4]{1,0:T(8,128)S(1)} %copy.27.cols_ref, bf16[16,112,128]{2,1,0:T(8,128)(2,1)S(1)} %all_to_all.30.whole_ref, bf16[16,4,128,128]{3,2,1,0:T(8,128)(2,1)S(1)} %bitcast.16, f32[3,16,128]{2,1,0:T(8,128)S(1)} %bitcast.18, ...), custom_call_target="tpu_custom_call" | custom-call | tf_op jit(solution)/shard_map/pallas_call | solution.py:27
  127.9 9.2 %all_to_all.31 = f32[16,1,128]{2,1,0:T(1,128)S(1)} all-to-all(f32[16,1,128]{2,1,0:T(1,128)S(1)} %bitcast.29), channel_id=1, replica_groups=mesh['slab'=16,'col'=16] {'col'}, dimensions={0} | all-to-all | bytes 16384 | tf_op jit(solution)/shard_map/all_to_all | solution.py:414
  137.1 0.0 copy-done.1
  137.1 2.2 %shard_map.172 = f32[16,64,128]{2,1,0:T(8,128)} custom-call(f32[16,128]{1,0:T(8,128)S(1)} %bitcast.27, s32[16,128]{1,0:T(8,128)S(1)} %bitcast.26, bf16[1024,2048]{1,0:T(8,128)(2,1)S(1)} %get-tuple-element.69.fault_hot_ref, f32[16,64,128]{2,1,0:T(8,128)S(1)} %get-tuple-element.70.field_ref, f32[16,64,128]{2,1,0:T(8,128)S(1)} %copy-done.1), custom_call_target="tpu_custom_call" | custom-call | tf_op jit(solution)/shard_map/pallas_call | solution.py:27
Async XLA Ops:
  0.6 0.7 copy-start.7
  4.3 28.7 %all-to-all-start = ((bf16[16,128,128]{2,1,0:T(8,128)(2,1)}), bf16[16,128,128]{2,1,0:T(8,128)(2,1)S(1)}, u32[]{:S(2)}, u32[]{:S(2)}) async-start(bf16[16,128,128]{2,1,0:T(8,128)(2,1)} %get-tuple-element.39), calls=%async_computation | async-start | bytes 1048576 | tf_op jit(solution)/shard_map/all_to_all | solution.py:414
  16.1 16.9 %collective-permute-start = (f32[2,64,128]{2,1,0:T(8,128)S(1)}, f32[2,64,128]{2,1,0:T(8,128)S(1)}, u32[]{:S(2)}, u32[]{:S(2)}) collective-permute-start(f32[2,64,128]{2,1,0:T(8,128)S(1)} %get-tuple-element.40), channel_id=1, source_target_pairs={{0,16},{32,48},{64,80},{96,112},{128,144},{160,176},{192,208},{224... | collective-permute-start | bytes 196616 | tf_op jit(solution)/shard_map/ppermute | solution.py:409
  18.3 14.6 %collective-permute-start.1 = (f32[2,64,128]{2,1,0:T(8,128)S(1)}, f32[2,64,128]{2,1,0:T(8,128)S(1)}, u32[]{:S(2)}, u32[]{:S(2)}) collective-permute-start(f32[2,64,128]{2,1,0:T(8,128)S(1)} %get-tuple-element.41), channel_id=1, source_target_pairs={{16,32},{48,64},{80,96},{112,128},{144,160},{176,192},{208,224},{3... | collective-permute-start | bytes 196616 | tf_op jit(solution)/shard_map/ppermute | solution.py:409
  19.0 4.2 %collective-permute-start.2 = (f32[2,16,128]{2,1,0:T(8,128)S(1)}, f32[2,16,128]{2,1,0:T(8,128)S(1)}, u32[]{:S(2)}, u32[]{:S(2)}) collective-permute-start(f32[2,16,128]{2,1,0:T(8,128)S(1)} %get-tuple-element.42), channel_id=1, source_target_pairs={{0,1},{2,3},{4,5},{6,7},{8,9},{10,11},{12,13},{14,15},{1,0},{3,2},... | collective-permute-start | bytes 49160 | tf_op jit(solution)/shard_map/ppermute | solution.py:409
  20.6 7.5 %collective-permute-start.3 = (f32[2,16,128]{2,1,0:T(8,128)S(1)}, f32[2,16,128]{2,1,0:T(8,128)S(1)}, u32[]{:S(2)}, u32[]{:S(2)}) collective-permute-start(f32[2,16,128]{2,1,0:T(8,128)S(1)} %get-tuple-element.43), channel_id=1, source_target_pairs={{1,2},{3,4},{5,6},{7,8},{9,10},{11,12},{13,14},{2,1},{4,3},{6,5},{... | collective-permute-start | bytes 49160 | tf_op jit(solution)/shard_map/ppermute | solution.py:409
  33.0 15.3 %all-to-all-start.1 = ((bf16[16,48,128]{2,1,0:T(8,128)(2,1)}), bf16[16,48,128]{2,1,0:T(8,128)(2,1)S(1)}, u32[]{:S(2)}, u32[]{:S(2)}) async-start(bf16[16,48,128]{2,1,0:T(8,128)(2,1)} %get-tuple-element.44), calls=%async_computation.1 | async-start | bytes 393216 | tf_op jit(solution)/shard_map/all_to_all | solution.py:414
  47.8 42.0 %copy-start.8 = (s32[1,16,4]{1,2,0:T(4,128)S(1)}, s32[1,16,4]{1,2,0:T(4,128)}, u32[]{:S(2)}) copy-start(s32[1,16,4]{1,2,0:T(4,128)} %param.29) | copy-start | bytes 772
  47.8 42.1 %copy-start.2 = (f32[1,3,2048]{2,0,1:T(1,128)S(1)}, f32[1,3,2048]{2,0,1:T(1,128)}, u32[]{:S(2)}) copy-start(f32[1,3,2048]{2,0,1:T(1,128)} %param.24) | copy-start | bytes 73732
  47.8 42.1 %copy-start.3 = (f32[1,3,2048]{2,0,1:T(1,128)S(1)}, f32[1,3,2048]{2,0,1:T(1,128)}, u32[]{:S(2)}) copy-start(f32[1,3,2048]{2,0,1:T(1,128)} %param.25) | copy-start | bytes 73732
  47.8 42.1 %copy-start.4 = (s32[2,1,2048]{2,1,0:T(1,128)S(1)}, s32[2,1,2048]{2,1,0:T(1,128)}, u32[]{:S(2)}) copy-start(s32[2,1,2048]{2,1,0:T(1,128)} %param.27) | copy-start | bytes 49156
  47.8 42.1 %copy-start.5 = (f32[1,2048]{1,0:T(1,128)S(1)}, f32[1,2048]{1,0:T(1,128)}, u32[]{:S(2)}) copy-start(f32[1,2048]{1,0:T(1,128)} %param.26) | copy-start | bytes 24580
  48.3 20.8 %all-to-all-start.2 = ((bf16[16,128,128]{2,1,0:T(8,128)(2,1)}), bf16[16,128,128]{2,1,0:T(8,128)(2,1)S(1)}, u32[]{:S(2)}, u32[]{:S(2)}) async-start(bf16[16,128,128]{2,1,0:T(8,128)(2,1)} %get-tuple-element.52), calls=%async_computation.2 | async-start | bytes 1048576 | tf_op jit(solution)/shard_map/all_to_all | solution.py:414
  53.2 13.4 %collective-permute-start.4 = (f32[1,64,128]{2,1,0:T(8,128)S(1)}, f32[1,64,128]{2,1,0:T(8,128)S(1)}, u32[]{:S(2)}, u32[]{:S(2)}) collective-permute-start(f32[1,64,128]{2,1,0:T(8,128)S(1)} %get-tuple-element.56), channel_id=1, source_target_pairs={{0,16},{32,48},{64,80},{96,112},{128,144},{160,176},{192,208},{224... | collective-permute-start | bytes 98312 | tf_op jit(solution)/shard_map/ppermute | solution.py:409
  55.4 11.2 %collective-permute-start.5 = (f32[1,64,128]{2,1,0:T(8,128)S(1)}, f32[1,64,128]{2,1,0:T(8,128)S(1)}, u32[]{:S(2)}, u32[]{:S(2)}) collective-permute-start(f32[1,64,128]{2,1,0:T(8,128)S(1)} %get-tuple-element.57), channel_id=1, source_target_pairs={{16,32},{48,64},{80,96},{112,128},{144,160},{176,192},{208,224},{3... | collective-permute-start | bytes 98312 | tf_op jit(solution)/shard_map/ppermute | solution.py:409
  56.1 4.2 %collective-permute-start.6 = (f32[1,16,128]{2,1,0:T(8,128)S(1)}, f32[1,16,128]{2,1,0:T(8,128)S(1)}, u32[]{:S(2)}, u32[]{:S(2)}) collective-permute-start(f32[1,16,128]{2,1,0:T(8,128)S(1)} %get-tuple-element.58), channel_id=1, source_target_pairs={{0,1},{2,3},{4,5},{6,7},{8,9},{10,11},{12,13},{14,15},{1,0},{3,2},... | collective-permute-start | bytes 24584 | tf_op jit(solution)/shard_map/ppermute | solution.py:409
  57.8 8.8 %collective-permute-start.7 = (f32[1,16,128]{2,1,0:T(8,128)S(1)}, f32[1,16,128]{2,1,0:T(8,128)S(1)}, u32[]{:S(2)}, u32[]{:S(2)}) collective-permute-start(f32[1,16,128]{2,1,0:T(8,128)S(1)} %get-tuple-element.59), channel_id=1, source_target_pairs={{1,2},{3,4},{5,6},{7,8},{9,10},{11,12},{13,14},{2,1},{4,3},{6,5},{... | collective-permute-start | bytes 24584 | tf_op jit(solution)/shard_map/ppermute | solution.py:409
  69.1 28.5 %copy-start.6 = (s32[1,1,16,128]{3,2,1,0:T(8,128)S(1)}, s32[1,1,16,128]{3,2,1,0:T(8,128)}, u32[]{:S(2)}) copy-start(s32[1,1,16,128]{3,2,1,0:T(8,128)} %param.23) | copy-start | bytes 24580
  74.9 22.8 %all-to-all-start.3 = ((bf16[16,128,128]{2,1,0:T(8,128)(2,1)}), bf16[16,128,128]{2,1,0:T(8,128)(2,1)S(1)}, u32[]{:S(2)}, u32[]{:S(2)}) async-start(bf16[16,128,128]{2,1,0:T(8,128)(2,1)} %get-tuple-element.60), calls=%async_computation.3 | async-start | bytes 1048576 | tf_op jit(solution)/shard_map/all_to_all | solution.py:414
  82.3 42.7 %copy-start = (bf16[1,16,4,128,128]{4,3,2,1,0:T(8,128)(2,1)S(1)}, bf16[1,16,4,128,128]{4,3,2,1,0:T(8,128)(2,1)}, u32[]{:S(2)}) copy-start(bf16[1,16,4,128,128]{4,3,2,1,0:T(8,128)(2,1)} %param.28) | copy-start | bytes 6291460
  82.3 14.5 %collective-permute-start.8 = (f32[1,64,128]{2,1,0:T(8,128)S(1)}, f32[1,64,128]{2,1,0:T(8,128)S(1)}, u32[]{:S(2)}, u32[]{:S(2)}) collective-permute-start(f32[1,64,128]{2,1,0:T(8,128)S(1)} %get-tuple-element.62), channel_id=1, source_target_pairs={{0,16},{32,48},{64,80},{96,112},{128,144},{160,176},{192,208},{224... | collective-permute-start | bytes 98312 | tf_op jit(solution)/shard_map/ppermute | solution.py:409
  84.7 12.1 %collective-permute-start.9 = (f32[1,64,128]{2,1,0:T(8,128)S(1)}, f32[1,64,128]{2,1,0:T(8,128)S(1)}, u32[]{:S(2)}, u32[]{:S(2)}) collective-permute-start(f32[1,64,128]{2,1,0:T(8,128)S(1)} %get-tuple-element.63), channel_id=1, source_target_pairs={{16,32},{48,64},{80,96},{112,128},{144,160},{176,192},{208,224},{3... | collective-permute-start | bytes 98312 | tf_op jit(solution)/shard_map/ppermute | solution.py:409
  85.3 8.3 %collective-permute-start.10 = (f32[1,16,128]{2,1,0:T(8,128)S(1)}, f32[1,16,128]{2,1,0:T(8,128)S(1)}, u32[]{:S(2)}, u32[]{:S(2)}) collective-permute-start(f32[1,16,128]{2,1,0:T(8,128)S(1)} %get-tuple-element.64), channel_id=1, source_target_pairs={{0,1},{2,3},{4,5},{6,7},{8,9},{10,11},{12,13},{14,15},{1,0},{3,2},... | collective-permute-start | bytes 24584 | tf_op jit(solution)/shard_map/ppermute | solution.py:409
  87.1 9.7 %collective-permute-start.11 = (f32[1,16,128]{2,1,0:T(8,128)S(1)}, f32[1,16,128]{2,1,0:T(8,128)S(1)}, u32[]{:S(2)}, u32[]{:S(2)}) collective-permute-start(f32[1,16,128]{2,1,0:T(8,128)S(1)} %get-tuple-element.65), channel_id=1, source_target_pairs={{1,2},{3,4},{5,6},{7,8},{9,10},{11,12},{13,14},{2,1},{4,3},{6,5},{... | collective-permute-start | bytes 24584 | tf_op jit(solution)/shard_map/ppermute | solution.py:409
  97.6 39.5 %copy-start.1 = (f32[16,64,128]{2,1,0:T(8,128)S(1)}, f32[16,64,128]{2,1,0:T(8,128)}, u32[]{:S(2)}) copy-start(f32[16,64,128]{2,1,0:T(8,128)} %get-tuple-element.55.diag_hbm.inverse_ref) | copy-start | bytes 1572868

commit v4 on v3

--- a/solution.py
+++ b/solution.py
@@ -9,6 +9,7 @@
 
 ITERS_FLOW = 3
 BIOT = 0.8
+STEPS = (1, 4, 8, 2)
 F32 = jnp.float32
 BF16 = jnp.bfloat16
 NT = (((1,), (1,)), ((), ()))
@@ -101,12 +102,14 @@
     depth, width, _ = field_ref.shape
     swap_z, swap_x = odd("slab"), odd("col")
     head, tail = field_ref[0], field_ref[depth - 1]
-    z_one[0] = jnp.where(swap_z, head, tail)
-    z_two[0] = jnp.where(swap_z, tail, head)
-    for i in range(depth):
-        head, tail = field_ref[i, 0:1, :], field_ref[i, width - 1 : width, :]
-        x_one[0, i : i + 1, :] = jnp.where(swap_x, head, tail)
-        x_two[0, i : i + 1, :] = jnp.where(swap_x, tail, head)
+    z_one[0] = jnp.where(swap_z, head, tail).astype(BF16)
+    z_two[0] = jnp.where(swap_z, tail, head).astype(BF16)
+    heads = jnp.concatenate([field_ref[i, 0:1, :] for i in range(depth)], 0)
+    tails = jnp.concatenate(
+        [field_ref[i, width - 1 : width, :] for i in range(depth)], 0
+    )
+    x_one[0] = jnp.where(swap_x, heads, tails).astype(BF16)
+    x_two[0] = jnp.where(swap_x, tails, heads).astype(BF16)
 
 
 def first_kernel(
@@ -116,7 +119,7 @@
     slip_hbm,
     cell_ref,
     out_hbm,
-    ready_hbm,
+    ready_ref,
     kept_ref,
     z_one,
     z_two,
@@ -125,9 +128,9 @@
     hot_ref,
     field_ref,
     wall_ref,
+    layer_ref,
     slip_ref,
     out_ref,
-    ready_ref,
     sems,
 ):
     depth, width, lateral = field_ref.shape
@@ -135,8 +138,7 @@
         [
             (field_hbm, field_ref),
             (face_x_hbm.at[:, pl.ds(width - 8, 8), :], wall_ref),
-            (face_z_hbm.at[depth - 1], z_one.at[1]),
-            (face_z_hbm.at[depth - 1], z_two.at[1]),
+            (face_z_hbm.at[depth - 1], layer_ref),
             (slip_hbm, slip_ref),
         ],
         sems,
@@ -145,19 +147,22 @@
     fill_hot(hot_ref, cell_ref[...])
     finish(reads)
     gather_lines(hot_ref, field_ref[...].reshape(depth * width, lateral), out_ref)
-    writes = begin([(out_ref, out_hbm)], sems, 5)
+    writes = begin([(out_ref, out_hbm)], sems, 4)
     parts, rows, _ = slip_ref.shape
     for p in range(parts):
         ready_ref[0, p * rows : (p + 1) * rows, :] = slip_ref[p].astype(BF16)
-    mine = ready_ref[0]
-    for o in range(1, ready_ref.shape[0]):
-        ready_ref[o] = mine
-    writes += begin([(ready_ref, ready_hbm)], sems, 6)
     put_edges(field_ref, (z_one, z_two, x_one, x_two))
-    for i in range(depth):
-        x_one[1, i : i + 1, :] = wall_ref[i, 7:8, :]
-        x_two[1, i : i + 1, :] = wall_ref[i, 7:8, :]
+    layer = layer_ref[...].astype(BF16)
+    wall = jnp.concatenate([wall_ref[i, 7:8, :] for i in range(depth)], 0).astype(BF16)
+    z_one[1] = layer
+    z_two[1] = layer
+    x_one[1] = wall
+    x_two[1] = wall
     finish(writes)
+
+
+def pick(choice, one, two):
+    return jnp.where(choice, one.astype(F32), two.astype(F32))
 
 
 def sweep_kernel(
@@ -200,6 +205,8 @@
         sems,
         2,
     )
+    if last:
+        table_reads = begin([(refs[2], refs[4])], sems, 8)
     fill_hot(hot_ref, cell_ref[...])
     finish(linked_reads)
     for q in range(incoming_ref.shape[0]):
@@ -217,7 +224,7 @@
     finish(reads)
     writes = []
     if last:
-        fault_ref, own_ref, new_ref, fault_hot_ref, press_ref = refs
+        fault_ref, own_ref, _, new_ref, fault_hot_ref, press_ref = refs
     elif first:
         new_hbm, out_hbm, turned_out, inverse_out = refs[:4]
         edge_refs = refs[4:]
@@ -226,12 +233,12 @@
         new_hbm, out_hbm = refs[:2]
         edge_refs = refs[2:]
     swap_z, swap_x = odd("slab"), odd("col")
-    below_z = jnp.where(swap_z, z_one[0], z_two[0])
-    above_z = jnp.where(swap_z, z_two[0], z_one[0])
-    edge_z = jnp.where(swap_z, faces[0][1], faces[1][1])
-    behind_x = jnp.where(swap_x, x_one[0], x_two[0])
-    ahead_x = jnp.where(swap_x, x_two[0], x_one[0])
-    edge_x = jnp.where(swap_x, faces[2][1], faces[3][1])
+    below_z = pick(swap_z, z_one[0], z_two[0])
+    above_z = pick(swap_z, z_two[0], z_one[0])
+    edge_z = pick(swap_z, faces[0][1], faces[1][1])
+    behind_x = pick(swap_x, x_one[0], x_two[0])
+    ahead_x = pick(swap_x, x_two[0], x_one[0])
+    edge_x = pick(swap_x, faces[2][1], faces[3][1])
     across = iota((width, lateral), 0)
     along = iota((width, lateral), 1)
     for i in range(depth):
@@ -269,7 +276,7 @@
         new_ref[i] = total * inverse
     lines = new_ref[...].reshape(depth * width, lateral)
     if last:
-        fill_hot(fault_hot_ref, fault_ref[...] >> 7)
+        finish(table_reads)
         high, low = halves(lines.T)
         both = jnp.concatenate([high, low], 0)
         side = iota((lateral, 128), 0)
@@ -321,23 +328,34 @@
 
 def contact_kernel(
     cols_ref,
-    whole_ref,
+    near_ref,
+    far_ref,
     blocks_hbm,
     base_ref,
     slip_ref,
     stiff_ref,
     active_ref,
+    fault_ref,
     own_ref,
+    fault_hot_hbm,
     tiles_ref,
     blocks_ref,
+    fault_hot_ref,
     sems,
 ):
     reads = begin([(blocks_hbm, blocks_ref)], sems)
-    owners = whole_ref.shape[0]
+    fill_hot(fault_hot_ref, fault_ref[...] >> 7)
+    writes = begin([(fault_hot_ref, fault_hot_hbm)], sems, 1)
     rows = base_ref.shape[1]
-    for p in range(3):
-        part = whole_ref[:, p * rows : (p + 1) * rows, :].astype(F32)
-        tiles_ref[p] = part.reshape(owners * rows, 128)
+    me = lax.axis_index("col")
+    held = near_ref.shape[0]
+    for n in range(2 * held):
+        apart = sum(bit for k, bit in enumerate(STEPS) if n >> k & 1)
+        owner = pl.multiple_of((me ^ apart) * rows, rows)
+        for p in range(3):
+            ref = near_ref if n < held else far_ref
+            part = ref[n % held, p * rows : (p + 1) * rows, :].astype(F32)
+            tiles_ref[p, pl.ds(owner, rows), :] = part
     finish(reads)
     coupled = couple(cols_ref, tiles_ref, blocks_ref)
     gain = active_ref[0].astype(F32) / stiff_ref[...]
@@ -346,6 +364,7 @@
         for p in range(3)
     ]
     own_ref[...] = jnp.concatenate([parts[0], -BIOT * gain, parts[1], parts[2]], 0)
+    finish(writes)
 
 
 def tail_kernel(
@@ -408,6 +427,14 @@
         pairs = [(i, i + 1) for i in range(start, count - 1, 2)]
         got.append(lax.ppermute(edge, axis, pairs + [(j, i) for i, j in pairs]))
     return got
+
+
+def paired(block, axis, apart):
+    return lax.ppermute(block, axis, [(i, i ^ apart) for i in range(lax.axis_size(axis))])
+
+
+def double(block, axis, apart):
+    return jnp.concatenate([block, paired(block, axis, apart)], 0)
 
 
 def swap(blocks, axis):
@@ -453,15 +480,15 @@
     block = pltpu.VMEM((depth, width, lateral), F32)
     packet = pltpu.VMEM((slabs, lateral, 128), BF16)
     values = pltpu.VMEM((2 * lateral, slots), BF16)
-    edges = [((1, *layer), F32)] * 2 + [((1, *wall), F32)] * 2
-    doubled = [((2, *layer), F32)] * 2 + [((2, *wall), F32)] * 2
+    edges = [((1, *layer), BF16)] * 2 + [((1, *wall), BF16)] * 2
+    doubled = [((2, *layer), BF16)] * 2 + [((2, *wall), BF16)] * 2
     planes = 7 * rows
 
     outgoing, ready, cells, *sides = call(
         first_kernel,
         [
             ((slabs, lateral, 128), BF16, 0),
-            ((columns, 3 * rows, 128), BF16, 0),
+            ((1, 3 * rows, 128), BF16),
             (cells.shape, jnp.int32),
             *doubled,
         ],
@@ -475,17 +502,17 @@
             table,
             block,
             pltpu.VMEM((depth, 8, lateral), F32),
+            pltpu.VMEM(layer, F32),
             pltpu.VMEM(slip0.shape, F32),
             packet,
-            pltpu.VMEM((columns, 3 * rows, 128), BF16),
-            pltpu.SemaphoreType.DMA((7,)),
+            pltpu.SemaphoreType.DMA((5,)),
         ),
     )
     incoming = swap(outgoing, "slab")
     sides = exchange(sides)
-    ready, incoming, sides = lax.optimization_barrier((ready, incoming, sides))
+    held = double(double(ready, "col", STEPS[0]), "col", STEPS[1])
+    held, incoming, sides = lax.optimization_barrier((held, incoming, sides))
     faces = sides
-    whole = swap(ready, "col")
     turned, diag = nnc_trans[0, 0], accum
     field = pressure
     for sweep in range(ITERS_FLOW):
@@ -493,7 +520,7 @@
         last = sweep == ITERS_FLOW - 1
         extra = [] if first else list(faces)
         if last:
-            extra += [faults, own]
+            extra += [faults, own, fault_hot]
             outs = [
                 (grid[0], F32),
                 ((lines, nodes), BF16),
@@ -518,7 +545,7 @@
             cells,
             *sides,
             *extra,
-            hbm=range(1, 8),
+            hbm=(*range(1, 8), *([19] if last else [])),
             scratch=[
                 *([] if last else [packet, block]),
                 *([values] if first else []),
@@ -535,26 +562,37 @@
         field, outgoing = got[:2]
         if first:
             turned, diag = got[2:4]
-            whole, outgoing = lax.optimization_barrier((whole, outgoing))
+            held, outgoing = lax.optimization_barrier((held, outgoing))
+        else:
+            near, far, outgoing = lax.optimization_barrier((near, far, outgoing))
         incoming = swap(outgoing, "slab")
         sides = exchange(got[-4:])
         if first:
-            (own,) = call(
+            near = double(held, "col", STEPS[2])
+            far = paired(near, "col", STEPS[3])
+            near, far, incoming, sides = lax.optimization_barrier(
+                (near, far, incoming, sides)
+            )
+        else:
+            own, fault_hot = call(
                 contact_kernel,
-                [((4 * rows, 128), F32)],
+                [((4 * rows, 128), F32), ((lines, nodes), BF16, 0)],
                 tile_cols,
-                whole,
+                near,
+                far,
                 blocks,
                 base,
                 slip0,
                 stiff,
                 active,
+                faults,
                 smem=(0,),
-                hbm=(2,),
+                hbm=(3,),
                 scratch=(
                     tiles,
                     pltpu.VMEM(blocks.shape, BF16),
-                    pltpu.SemaphoreType.DMA((1,)),
+                    pltpu.VMEM((lines, nodes), BF16),
+                    pltpu.SemaphoreType.DMA((2,)),
                 ),
             )
     whole = swap(whole, "col")

time: 140 us -> 136 us (0.971)
  blocking collectives: 28.4 us -> 25.5 us
  waiting for transfers between devices: 23 us -> 20.9 us
    ppermute x0 -> x4, starting transfers between devices: none -> 5.57 us  [paired(): lax.ppermute(block, axis, [(i, i ^ apart) for i in range(lax.axis_size(ax...]
    ppermute x12, waiting for transfers between devices: 19.3 us -> 13.8 us  [exchange(): got.append(lax.ppermute(edge, axis, pairs + [(j, i) for i, j in pairs]))]
    all_to_all x4 -> x3, starting transfers between devices: 32.7 us -> 27.9 us  [swap(): return lax.all_to_all(blocks, axis, split_axis=0, concat_axis=0, tiled=True)]
    all_to_all x2, blocking collectives: 28.4 us -> 25.5 us  [swap(): return lax.all_to_all(blocks, axis, split_axis=0, concat_axis=0, tiled=True)]
    ppermute x0 -> x4, waiting for transfers between devices: none -> 2.83 us  [paired(): lax.ppermute(block, axis, [(i, i ^ apart) for i in range(lax.axis_size(ax...]
    all_to_all x4 -> x3, waiting for transfers between devices: 3.74 us -> 4.26 us  [swap(): return lax.all_to_all(blocks, axis, split_axis=0, concat_axis=0, tiled=True)]
  transfers between devices with their start and end apart: 16 -> 19, of which waited for: 7 -> 9; matrix products, arithmetic and copies ran while one was open for 0% -> 0% of each run, Pallas kernels for 7% -> 3%
where the time goes in v4:
time: 136 us; the launch traced here: 135 us
  starting transfers between devices  55.1 us (41%)
  Pallas kernels  31.8 us (23%)
  blocking collectives  25.5 us (19%)
  waiting for transfers between devices  20.9 us (15%)
    pallas_call x7, Pallas kernels, call(): pl.pallas_call(body, in_specs=[pl.BlockSpec(memory_space=space) for space...  31.8 us
    all_to_all x3, starting transfers between devices, swap(): return lax.all_to_all(blocks, axis, split_axis=0, concat_axis=0, tiled=True)  27.9 us
    all_to_all x2, blocking collectives, swap(): return lax.all_to_all(blocks, axis, split_axis=0, concat_axis=0, tiled=True)  25.5 us
    ppermute x12, starting transfers between devices, exchange(): got.append(lax.ppermute(edge, axis, pairs + [(j, i) for i, j in pairs]))  21.7 us
    ppermute x12, waiting for transfers between devices, exchange(): got.append(lax.ppermute(edge, axis, pairs + [(j, i) for i, j in pairs]))  13.8 us
    ppermute x4, starting transfers between devices, paired(): lax.ppermute(block, axis, [(i, i ^ apart) for i in range(lax.axis_size(ax...  5.57 us
    all_to_all x3, waiting for transfers between devices, swap(): return lax.all_to_all(blocks, axis, split_axis=0, concat_axis=0, tiled=True)  4.26 us
    ppermute x4, waiting for transfers between devices, paired(): lax.ppermute(block, axis, [(i, i ^ apart) for i in range(lax.axis_size(ax...  2.83 us
  transfers between devices with their start and end apart: 19, of which 9 were waited for; matrix products, arithmetic and copies ran while one was open for 0% of the time, Pallas kernels for 3%

profile of v4, /device:TPU:1, one launch (start us, length us, event | category | flops | bytes accessed | tf_op | source)
XLA Modules:
  0.0 135.0 jit_solution(6408422162194504329)
XLA Ops:
  0.6 0.0 copy-start.7
  0.6 0.7 copy-done.7
  1.3 2.9 %shard_map.166 = (bf16[16,128,128]{2,1,0:T(8,128)(2,1)}, bf16[1,48,128]{2,1,0:T(8,128)(2,1)S(1)}, s32[16,128]{1,0:T(8,128)S(1)}, bf16[2,64,128]{2,1,0:T(8,128)(2...) custom-call(f32[16,64,128]{2,1,0:T(8,128)} %field_hbm.3, ...), custom_call_target="tpu_custom_call" | custom-call | tf_op jit(solution)/shard_map/pallas_call | solution.py:28
  4.2 11.7 %all-to-all-start = ((bf16[16,128,128]{2,1,0:T(8,128)(2,1)}), bf16[16,128,128]{2,1,0:T(8,128)(2,1)S(1)}, u32[]{:S(2)}, u32[]{:S(2)}) async-start(bf16[16,128,128]{2,1,0:T(8,128)(2,1)} %get-tuple-element.51), calls=%async_computation | async-start | bytes 1048576 | tf_op jit(solution)/shard_map/all_to_all | solution.py:441
  16.0 1.0 collective-permute-start
  17.0 0.8 collective-permute-done
  17.9 1.2 collective-permute-start.1
  19.1 0.6 collective-permute-start.4
  19.7 2.5 %collective-permute-start.5 = (bf16[2,16,128]{2,1,0:T(8,128)(2,1)S(1)}, bf16[2,16,128]{2,1,0:T(8,128)(2,1)S(1)}, u32[]{:S(2)}, u32[]{:S(2)}) collective-permute-start(bf16[2,16,128]{2,1,0:T(8,128)(2,1)S(1)} %get-tuple-element.55), channel_id=1, source_target_pairs={{1,2},{3,4},{5,6},{7,8},{9,10},{11,12},{13,14},{2,1},{4,3},{6,5},{... | collective-permute-start | bytes 24584 | tf_op jit(solution)/shard_map/ppermute | solution.py:428
  22.2 2.5 %collective-permute-start.2 = (bf16[2,64,128]{2,1,0:T(8,128)(2,1)S(1)}, bf16[2,64,128]{2,1,0:T(8,128)(2,1)S(1)}, u32[]{:S(2)}, u32[]{:S(2)}) collective-permute-start(bf16[2,64,128]{2,1,0:T(8,128)(2,1)S(1)} %get-tuple-element.52), channel_id=1, source_target_pairs={{0,16},{32,48},{64,80},{96,112},{128,144},{160,176},{192,208},{224... | collective-permute-start | bytes 98312 | tf_op jit(solution)/shard_map/ppermute | solution.py:428
  24.8 0.7 collective-permute-start.3
  25.4 0.0 collective-permute-done.1
  25.5 0.0 collective-permute-done.4.x_one.refs_2_
  25.5 2.5 %collective-permute-done.5.x_two.refs_3_ = bf16[2,16,128]{2,1,0:T(8,128)(2,1)S(1)} collective-permute-done((bf16[2,16,128]{2,1,0:T(8,128)(2,1)S(1)}, bf16[2,16,128]{2,1,0:T(8,128)(2,1)S(1)}, u32[]{:S(2)}, u32[]{:S(2)}) %collective-permute-start.5) | collective-permute-done | bytes 8224 | tf_op jit(solution)/shard_map/ppermute | solution.py:428
  27.9 3.5 %collective-permute-done.2.z_one.refs_0_ = bf16[2,64,128]{2,1,0:T(8,128)(2,1)S(1)} collective-permute-done((bf16[2,64,128]{2,1,0:T(8,128)(2,1)S(1)}, bf16[2,64,128]{2,1,0:T(8,128)(2,1)S(1)}, u32[]{:S(2)}, u32[]{:S(2)}) %collective-permute-start.2) | collective-permute-done | bytes 32800 | tf_op jit(solution)/shard_map/ppermute | solution.py:428
  31.5 0.0 collective-permute-done.3.z_two.refs_1_
  31.5 1.5 %all-to-all-done.incoming_ref = bf16[16,128,128]{2,1,0:T(8,128)(2,1)S(1)} async-done(((bf16[16,128,128]{2,1,0:T(8,128)(2,1)}), bf16[16,128,128]{2,1,0:T(8,128)(2,1)S(1)}, u32[]{:S(2)}, u32[]{:S(2)}) %all-to-all-start) | async-done | bytes 524320 | tf_op jit(solution)/shard_map/all_to_all | solution.py:441
  32.9 6.1 %shard_map.167 = (f32[16,64,128]{2,1,0:T(8,128)}, bf16[16,128,128]{2,1,0:T(8,128)(2,1)}, f32[16,128,128]{2,1,0:T(8,128)}, f32[16,64,128]{2,1,0:T(8,128)}, bf16[1...) custom-call(bf16[16,128,128]{2,1,0:T(8,128)(2,1)S(1)} %all-to-all-do, ...), custom_call_target="tpu_custom_call" | custom-call | tf_op jit(solution)/shard_map/pallas_call | solution.py:28
  39.0 0.0 copy-start.8
  39.0 0.0 copy-start.2
  39.0 0.0 copy-start.3
  39.1 0.0 copy-start.4
  39.1 0.0 copy-start.5
  39.1 0.0 copy-start.6
  39.1 6.7 %all-to-all-start.1 = ((bf16[16,128,128]{2,1,0:T(8,128)(2,1)}), bf16[16,128,128]{2,1,0:T(8,128)(2,1)S(1)}, u32[]{:S(2)}, u32[]{:S(2)}) async-start(bf16[16,128,128]{2,1,0:T(8,128)(2,1)} %get-tuple-element.65), calls=%async_computation.1 | async-start | bytes 1048576 | tf_op jit(solution)/shard_map/all_to_all | solution.py:441
  45.8 2.5 %collective-permute-start.6 = (bf16[4,48,128]{2,1,0:T(8,128)(2,1)S(1)}, bf16[4,48,128]{2,1,0:T(8,128)(2,1)S(1)}, u32[]{:S(2)}, u32[]{:S(2)}) collective-permute-start(bf16[4,48,128]{2,1,0:T(8,128)(2,1)S(1)} %pad_maximum_fusion), channel_id=1, source_target_pairs={{0,8},{1,9},{2,10},{3,11},{4,12},{5,13},{6,14},{7,15},{8,0},{9,1},... | collective-permute-start | bytes 147464 | tf_op jit(solution)/shard_map/ppermute | solution.py:433
  48.4 2.0 %collective-permute-done.6 = bf16[4,48,128]{2,1,0:T(8,128)(2,1)S(1)} collective-permute-done((bf16[4,48,128]{2,1,0:T(8,128)(2,1)S(1)}, bf16[4,48,128]{2,1,0:T(8,128)(2,1)S(1)}, u32[]{:S(2)}, u32[]{:S(2)}) %collective-permute-start.6) | collective-permute-done | bytes 49184 | tf_op jit(solution)/shard_map/ppermute | solution.py:433
  50.4 0.8 collective-permute-start.7
  51.2 2.2 %collective-permute-start.8 = (bf16[1,64,128]{2,1,0:T(8,128)(2,1)S(1)}, bf16[1,64,128]{2,1,0:T(8,128)(2,1)S(1)}, u32[]{:S(2)}, u32[]{:S(2)}) collective-permute-start(bf16[1,64,128]{2,1,0:T(8,128)(2,1)S(1)} %get-tuple-element.66), channel_id=1, source_target_pairs={{0,16},{32,48},{64,80},{96,112},{128,144},{160,176},{192,208},{224... | collective-permute-start | bytes 49160 | tf_op jit(solution)/shard_map/ppermute | solution.py:428
  53.3 0.7 collective-permute-start.9
  54.0 4.3 %collective-permute-start.10 = (bf16[1,16,128]{2,1,0:T(8,128)(2,1)S(1)}, bf16[1,16,128]{2,1,0:T(8,128)(2,1)S(1)}, u32[]{:S(2)}, u32[]{:S(2)}) collective-permute-start(bf16[1,16,128]{2,1,0:T(8,128)(2,1)S(1)} %get-tuple-element.68), channel_id=1, source_target_pairs={{0,1},{2,3},{4,5},{6,7},{8,9},{10,11},{12,13},{14,15},{1,0},{3,2},... | collective-permute-start | bytes 12296 | tf_op jit(solution)/shard_map/ppermute | solution.py:428
  58.3 2.1 %collective-permute-start.11 = (bf16[1,16,128]{2,1,0:T(8,128)(2,1)S(1)}, bf16[1,16,128]{2,1,0:T(8,128)(2,1)S(1)}, u32[]{:S(2)}, u32[]{:S(2)}) collective-permute-start(bf16[1,16,128]{2,1,0:T(8,128)(2,1)S(1)} %get-tuple-element.69), channel_id=1, source_target_pairs={{1,2},{3,4},{5,6},{7,8},{9,10},{11,12},{13,14},{2,1},{4,3},{6,5},{... | collective-permute-start | bytes 12296 | tf_op jit(solution)/shard_map/ppermute | solution.py:428
  60.4 0.0 collective-permute-done.10.x_one
  60.4 3.1 %collective-permute-done.11.x_two = bf16[1,16,128]{2,1,0:T(8,128)(2,1)S(1)} collective-permute-done((bf16[1,16,128]{2,1,0:T(8,128)(2,1)S(1)}, bf16[1,16,128]{2,1,0:T(8,128)(2,1)S(1)}, u32[]{:S(2)}, u32[]{:S(2)}) %collective-permute-start.11) | collective-permute-done | bytes 4128 | tf_op jit(solution)/shard_map/ppermute | solution.py:428
  63.5 0.0 collective-permute-done.8.z_one
  63.5 0.0 collective-permute-done.9.z_two
  63.5 0.0 collective-permute-done.7.far_ref
  63.5 0.0 all-to-all-done.1.incoming_ref
  63.6 5.8 %shard_map.168 = (f32[16,64,128]{2,1,0:T(8,128)}, bf16[16,128,128]{2,1,0:T(8,128)(2,1)}, bf16[1,64,128]{2,1,0:T(8,128)(2,1)S(1)}, bf16[1,64,128]{2,1,0:T(8,128)(...) custom-call(bf16[16,128,128]{2,1,0:T(8,128)(2,1)S(1)} %all-to-all-done.1.incoming_ref, ...), custom_call_target="tpu_custom_call" | custom-call | tf_op jit(solution)/shard_map/pallas_call | solution.py:28
  69.3 9.4 %all-to-all-start.2 = ((bf16[16,128,128]{2,1,0:T(8,128)(2,1)}), bf16[16,128,128]{2,1,0:T(8,128)(2,1)S(1)}, u32[]{:S(2)}, u32[]{:S(2)}) async-start(bf16[16,128,128]{2,1,0:T(8,128)(2,1)} %get-tuple-element.81), calls=%async_computation.2 | async-start | bytes 1048576 | tf_op jit(solution)/shard_map/all_to_all | solution.py:441
  78.7 2.3 %collective-permute-start.12 = (bf16[1,64,128]{2,1,0:T(8,128)(2,1)S(1)}, bf16[1,64,128]{2,1,0:T(8,128)(2,1)S(1)}, u32[]{:S(2)}, u32[]{:S(2)}) collective-permute-start(bf16[1,64,128]{2,1,0:T(8,128)(2,1)S(1)} %get-tuple-element.83), channel_id=1, source_target_pairs={{0,16},{32,48},{64,80},{96,112},{128,144},{160,176},{192,208},{224... | collective-permute-start | bytes 49160 | tf_op jit(solution)/shard_map/ppermute | solution.py:428
  81.0 0.7 collective-permute-start.13
  81.6 1.3 collective-permute-start.14
  82.9 1.9 %collective-permute-start.15 = (bf16[1,16,128]{2,1,0:T(8,128)(2,1)S(1)}, bf16[1,16,128]{2,1,0:T(8,128)(2,1)S(1)}, u32[]{:S(2)}, u32[]{:S(2)}) collective-permute-start(bf16[1,16,128]{2,1,0:T(8,128)(2,1)S(1)} %get-tuple-element.86), channel_id=1, source_target_pairs={{1,2},{3,4},{5,6},{7,8},{9,10},{11,12},{13,14},{2,1},{4,3},{6,5},{... | collective-permute-start | bytes 12296 | tf_op jit(solution)/shard_map/ppermute | solution.py:428
  84.9 0.0 copy-done.8
  84.9 0.1 copy.27.cols_ref
  84.9 0.0 copy-done.2
  84.9 0.0 copy-done.3
  85.0 0.0 copy-done.4
  85.0 0.0 copy-done.5
  85.0 0.0 copy-done.6
  85.0 3.9 %shard_map.169 = (f32[64,128]{1,0:T(8,128)S(1)}, bf16[1024,2048]{1,0:T(8,128)(2,1)}) custom-call(s32[16,4]{1,0:T(8,128)S(1)} %copy.27.cols_ref, bf16[8,48,128]{2,1,0:T(8,128)(2,1)S(1)} %constant_dynamic-update-slice_fusion.near_ref, bf16[8,48,128]{2,1,0:T(8,128)(2,1)S(1)} %collective-permute-done.7.far_ref, bf16[16,4,128,128]{3,2,1,0:T(8,128)(2,1)} %bitcast.15, ...), custom_call_target="tpu_custom_call" | custom-call | tf_op jit(solution)/shard_map/pallas_call | solution.py:28
  88.9 0.0 collective-permute-done.14.x_one
  88.9 0.5 collective-permute-done.15.x_two
  89.4 4.2 %collective-permute-done.12.z_one = bf16[1,64,128]{2,1,0:T(8,128)(2,1)S(1)} collective-permute-done((bf16[1,64,128]{2,1,0:T(8,128)(2,1)S(1)}, bf16[1,64,128]{2,1,0:T(8,128)(2,1)S(1)}, u32[]{:S(2)}, u32[]{:S(2)}) %collective-permute-start.12) | collective-permute-done | bytes 16416 | tf_op jit(solution)/shard_map/ppermute | solution.py:428
  93.5 0.0 collective-permute-done.13.z_two
  93.5 2.8 %all-to-all-done.2.incoming_ref = bf16[16,128,128]{2,1,0:T(8,128)(2,1)S(1)} async-done(((bf16[16,128,128]{2,1,0:T(8,128)(2,1)}), bf16[16,128,128]{2,1,0:T(8,128)(2,1)S(1)}, u32[]{:S(2)}, u32[]{:S(2)}) %all-to-all-start.2) | async-done | bytes 524320 | tf_op jit(solution)/shard_map/all_to_all | solution.py:441
  96.4 8.1 %shard_map.170 = (f32[16,64,128]{2,1,0:T(8,128)S(1)}, bf16[1024,2048]{1,0:T(8,128)(2,1)S(1)}, bf16[16,112,128]{2,1,0:T(8,128)(2,1)S(1)}) custom-call(bf16[16,128,128]{2,1,0:T(8,128)(2,1)S(1)} %all-to-all-done.2.incoming_ref, f32[16,128,128]{2,1,0:T(8,128)} %get-tuple-element.73.turned_hbm, f32[16,64,128]{2,1,0:T(8,128)} %get-tuple-element.82.field_hbm, ...), custom_call_target="tpu_custom_call" | custom-call | tf_op jit(solution)/shard_map/pallas_call | solution.py:28
  104.4 16.3 %all_to_all.25.whole_ref = bf16[16,112,128]{2,1,0:T(8,128)(2,1)S(1)} all-to-all(bf16[16,112,128]{2,1,0:T(8,128)(2,1)S(1)} %get-tuple-element.91), channel_id=1, replica_groups=mesh['slab'=16,'col'=16] {'col'}, dimensions={0} | all-to-all | bytes 917504 | tf_op jit(solution)/shard_map/all_to_all | solution.py:441
  120.7 0.0 copy-done
  120.7 2.8 %shard_map.171 = (f32[16,128]{1,0:T(8,128)S(1)}, f32[3,16,128]{2,1,0:T(8,128)}, f32[3,16,128]{2,1,0:T(8,128)}) custom-call(s32[16,4]{1,0:T(8,128)S(1)} %copy.27.cols_ref, bf16[16,112,128]{2,1,0:T(8,128)(2,1)S(1)} %all_to_all.25.whole_ref, bf16[16,4,128,128]{3,2,1,0:T(8,128)(2,1)S(1)} %bitcast.16, f32[3,16,128]{2,1,0:T(8,128)S(1)} %bitcast.18, ...), custom_call_target="tpu_custom_call" | custom-call | tf_op jit(solution)/shard_map/pallas_call | solution.py:28
  123.6 9.2 %all_to_all.26 = f32[16,1,128]{2,1,0:T(1,128)S(1)} all-to-all(f32[16,1,128]{2,1,0:T(1,128)S(1)} %bitcast.30), channel_id=1, replica_groups=mesh['slab'=16,'col'=16] {'col'}, dimensions={0} | all-to-all | bytes 16384 | tf_op jit(solution)/shard_map/all_to_all | solution.py:441
  132.8 0.0 copy-done.1
  132.8 2.2 %shard_map.172 = f32[16,64,128]{2,1,0:T(8,128)} custom-call(f32[16,128]{1,0:T(8,128)S(1)} %bitcast.28, s32[16,128]{1,0:T(8,128)S(1)} %bitcast.23, bf16[1024,2048]{1,0:T(8,128)(2,1)S(1)} %get-tuple-element.93.fault_hot_ref, f32[16,64,128]{2,1,0:T(8,128)S(1)} %get-tuple-element.94.field_ref, f32[16,64,128]{2,1,0:T(8,128)S(1)} %copy-done.1), custom_call_target="tpu_custom_call" | custom-call | tf_op jit(solution)/shard_map/pallas_call | solution.py:28
  (6 shorter events, 0.0 us)
Async XLA Ops:
  0.6 0.7 copy-start.7
  4.2 28.7 %all-to-all-start = ((bf16[16,128,128]{2,1,0:T(8,128)(2,1)}), bf16[16,128,128]{2,1,0:T(8,128)(2,1)S(1)}, u32[]{:S(2)}, u32[]{:S(2)}) async-start(bf16[16,128,128]{2,1,0:T(8,128)(2,1)} %get-tuple-element.51), calls=%async_computation | async-start | bytes 1048576 | tf_op jit(solution)/shard_map/all_to_all | solution.py:441
  16.0 1.9 %collective-permute-start = (bf16[1,48,128]{2,1,0:T(8,128)(2,1)S(1)}, bf16[1,48,128]{2,1,0:T(8,128)(2,1)S(1)}, u32[]{:S(2)}, u32[]{:S(2)}) collective-permute-start(bf16[1,48,128]{2,1,0:T(8,128)(2,1)S(1)} %get-tuple-element.50), channel_id=1, source_target_pairs={{0,1},{1,0},{2,3},{3,2},{4,5},{5,4},{6,7},{7,6},{8,9},{9,8},{10,11... | collective-permute-start | bytes 36872 | tf_op jit(solution)/shard_map/ppermute | solution.py:433
  17.9 7.6 %collective-permute-start.1 = (bf16[2,48,128]{2,1,0:T(8,128)(2,1)S(1)}, bf16[2,48,128]{2,1,0:T(8,128)(2,1)S(1)}, u32[]{:S(2)}, u32[]{:S(2)}) collective-permute-start(bf16[2,48,128]{2,1,0:T(8,128)(2,1)S(1)} %pad_maximum_fusion.1), channel_id=1, source_target_pairs={{0,4},{1,5},{2,6},{3,7},{4,0},{5,1},{6,2},{7,3},{8,12},{9,13},{10,... | collective-permute-start | bytes 73736 | tf_op jit(solution)/shard_map/ppermute | solution.py:433
  19.1 6.4 %collective-permute-start.4 = (bf16[2,16,128]{2,1,0:T(8,128)(2,1)S(1)}, bf16[2,16,128]{2,1,0:T(8,128)(2,1)S(1)}, u32[]{:S(2)}, u32[]{:S(2)}) collective-permute-start(bf16[2,16,128]{2,1,0:T(8,128)(2,1)S(1)} %get-tuple-element.54), channel_id=1, source_target_pairs={{0,1},{2,3},{4,5},{6,7},{8,9},{10,11},{12,13},{14,15},{1,0},{3,2},... | collective-permute-start | bytes 24584 | tf_op jit(solution)/shard_map/ppermute | solution.py:428
  19.7 8.2 %collective-permute-start.5 = (bf16[2,16,128]{2,1,0:T(8,128)(2,1)S(1)}, bf16[2,16,128]{2,1,0:T(8,128)(2,1)S(1)}, u32[]{:S(2)}, u32[]{:S(2)}) collective-permute-start(bf16[2,16,128]{2,1,0:T(8,128)(2,1)S(1)} %get-tuple-element.55), channel_id=1, source_target_pairs={{1,2},{3,4},{5,6},{7,8},{9,10},{11,12},{13,14},{2,1},{4,3},{6,5},{... | collective-permute-start | bytes 24584 | tf_op jit(solution)/shard_map/ppermute | solution.py:428
  22.2 9.2 %collective-permute-start.2 = (bf16[2,64,128]{2,1,0:T(8,128)(2,1)S(1)}, bf16[2,64,128]{2,1,0:T(8,128)(2,1)S(1)}, u32[]{:S(2)}, u32[]{:S(2)}) collective-permute-start(bf16[2,64,128]{2,1,0:T(8,128)(2,1)S(1)} %get-tuple-element.52), channel_id=1, source_target_pairs={{0,16},{32,48},{64,80},{96,112},{128,144},{160,176},{192,208},{224... | collective-permute-start | bytes 98312 | tf_op jit(solution)/shard_map/ppermute | solution.py:428
  24.8 6.7 %collective-permute-start.3 = (bf16[2,64,128]{2,1,0:T(8,128)(2,1)S(1)}, bf16[2,64,128]{2,1,0:T(8,128)(2,1)S(1)}, u32[]{:S(2)}, u32[]{:S(2)}) collective-permute-start(bf16[2,64,128]{2,1,0:T(8,128)(2,1)S(1)} %get-tuple-element.53), channel_id=1, source_target_pairs={{16,32},{48,64},{80,96},{112,128},{144,160},{176,192},{208,224},{3... | collective-permute-start | bytes 98312 | tf_op jit(solution)/shard_map/ppermute | solution.py:428
  39.0 45.8 %copy-start.8 = (s32[1,16,4]{1,2,0:T(4,128)S(1)}, s32[1,16,4]{1,2,0:T(4,128)}, u32[]{:S(2)}) copy-start(s32[1,16,4]{1,2,0:T(4,128)} %param.29) | copy-start | bytes 772
  39.0 45.9 %copy-start.2 = (f32[1,3,2048]{2,0,1:T(1,128)S(1)}, f32[1,3,2048]{2,0,1:T(1,128)}, u32[]{:S(2)}) copy-start(f32[1,3,2048]{2,0,1:T(1,128)} %param.24) | copy-start | bytes 73732
  39.0 45.9 %copy-start.3 = (f32[1,3,2048]{2,0,1:T(1,128)S(1)}, f32[1,3,2048]{2,0,1:T(1,128)}, u32[]{:S(2)}) copy-start(f32[1,3,2048]{2,0,1:T(1,128)} %param.25) | copy-start | bytes 73732
  39.1 45.9 %copy-start.4 = (s32[1,1,16,128]{3,2,1,0:T(8,128)S(1)}, s32[1,1,16,128]{3,2,1,0:T(8,128)}, u32[]{:S(2)}) copy-start(s32[1,1,16,128]{3,2,1,0:T(8,128)} %param.23) | copy-start | bytes 24580
  39.1 45.9 %copy-start.5 = (s32[2,1,2048]{2,1,0:T(1,128)S(1)}, s32[2,1,2048]{2,1,0:T(1,128)}, u32[]{:S(2)}) copy-start(s32[2,1,2048]{2,1,0:T(1,128)} %param.27) | copy-start | bytes 49156
  39.1 45.9 %copy-start.6 = (f32[1,2048]{1,0:T(1,128)S(1)}, f32[1,2048]{1,0:T(1,128)}, u32[]{:S(2)}) copy-start(f32[1,2048]{1,0:T(1,128)} %param.26) | copy-start | bytes 24580
  39.1 24.5 %all-to-all-start.1 = ((bf16[16,128,128]{2,1,0:T(8,128)(2,1)}), bf16[16,128,128]{2,1,0:T(8,128)(2,1)S(1)}, u32[]{:S(2)}, u32[]{:S(2)}) async-start(bf16[16,128,128]{2,1,0:T(8,128)(2,1)} %get-tuple-element.65), calls=%async_computation.1 | async-start | bytes 1048576 | tf_op jit(solution)/shard_map/all_to_all | solution.py:441
  45.8 4.5 %collective-permute-start.6 = (bf16[4,48,128]{2,1,0:T(8,128)(2,1)S(1)}, bf16[4,48,128]{2,1,0:T(8,128)(2,1)S(1)}, u32[]{:S(2)}, u32[]{:S(2)}) collective-permute-start(bf16[4,48,128]{2,1,0:T(8,128)(2,1)S(1)} %pad_maximum_fusion), channel_id=1, source_target_pairs={{0,8},{1,9},{2,10},{3,11},{4,12},{5,13},{6,14},{7,15},{8,0},{9,1},... | collective-permute-start | bytes 147464 | tf_op jit(solution)/shard_map/ppermute | solution.py:433
  50.4 13.2 %collective-permute-start.7 = (bf16[8,48,128]{2,1,0:T(8,128)(2,1)S(1)}, bf16[8,48,128]{2,1,0:T(8,128)(2,1)S(1)}, u32[]{:S(2)}, u32[]{:S(2)}) collective-permute-start(bf16[8,48,128]{2,1,0:T(8,128)(2,1)S(1)} %constant_dynamic-update-slice_fusion.near_ref), channel_id=1, source_target_pairs={{0,2},{1,3},{2,0},{3,1},{4,6},{5,7},{6,4},{7,5},{8,10},{9,11},{10,... | collective-permute-start | bytes 294920 | tf_op jit(solution)/shard_map/ppermute | solution.py:433
  51.2 12.4 %collective-permute-start.8 = (bf16[1,64,128]{2,1,0:T(8,128)(2,1)S(1)}, bf16[1,64,128]{2,1,0:T(8,128)(2,1)S(1)}, u32[]{:S(2)}, u32[]{:S(2)}) collective-permute-start(bf16[1,64,128]{2,1,0:T(8,128)(2,1)S(1)} %get-tuple-element.66), channel_id=1, source_target_pairs={{0,16},{32,48},{64,80},{96,112},{128,144},{160,176},{192,208},{224... | collective-permute-start | bytes 49160 | tf_op jit(solution)/shard_map/ppermute | solution.py:428
  53.3 10.2 %collective-permute-start.9 = (bf16[1,64,128]{2,1,0:T(8,128)(2,1)S(1)}, bf16[1,64,128]{2,1,0:T(8,128)(2,1)S(1)}, u32[]{:S(2)}, u32[]{:S(2)}) collective-permute-start(bf16[1,64,128]{2,1,0:T(8,128)(2,1)S(1)} %get-tuple-element.67), channel_id=1, source_target_pairs={{16,32},{48,64},{80,96},{112,128},{144,160},{176,192},{208,224},{3... | collective-permute-start | bytes 49160 | tf_op jit(solution)/shard_map/ppermute | solution.py:428
  54.0 6.4 %collective-permute-start.10 = (bf16[1,16,128]{2,1,0:T(8,128)(2,1)S(1)}, bf16[1,16,128]{2,1,0:T(8,128)(2,1)S(1)}, u32[]{:S(2)}, u32[]{:S(2)}) collective-permute-start(bf16[1,16,128]{2,1,0:T(8,128)(2,1)S(1)} %get-tuple-element.68), channel_id=1, source_target_pairs={{0,1},{2,3},{4,5},{6,7},{8,9},{10,11},{12,13},{14,15},{1,0},{3,2},... | collective-permute-start | bytes 12296 | tf_op jit(solution)/shard_map/ppermute | solution.py:428
  58.3 5.2 %collective-permute-start.11 = (bf16[1,16,128]{2,1,0:T(8,128)(2,1)S(1)}, bf16[1,16,128]{2,1,0:T(8,128)(2,1)S(1)}, u32[]{:S(2)}, u32[]{:S(2)}) collective-permute-start(bf16[1,16,128]{2,1,0:T(8,128)(2,1)S(1)} %get-tuple-element.69), channel_id=1, source_target_pairs={{1,2},{3,4},{5,6},{7,8},{9,10},{11,12},{13,14},{2,1},{4,3},{6,5},{... | collective-permute-start | bytes 12296 | tf_op jit(solution)/shard_map/ppermute | solution.py:428
  69.3 27.0 %all-to-all-start.2 = ((bf16[16,128,128]{2,1,0:T(8,128)(2,1)}), bf16[16,128,128]{2,1,0:T(8,128)(2,1)S(1)}, u32[]{:S(2)}, u32[]{:S(2)}) async-start(bf16[16,128,128]{2,1,0:T(8,128)(2,1)} %get-tuple-element.81), calls=%async_computation.2 | async-start | bytes 1048576 | tf_op jit(solution)/shard_map/all_to_all | solution.py:441
  78.7 14.8 %collective-permute-start.12 = (bf16[1,64,128]{2,1,0:T(8,128)(2,1)S(1)}, bf16[1,64,128]{2,1,0:T(8,128)(2,1)S(1)}, u32[]{:S(2)}, u32[]{:S(2)}) collective-permute-start(bf16[1,64,128]{2,1,0:T(8,128)(2,1)S(1)} %get-tuple-element.83), channel_id=1, source_target_pairs={{0,16},{32,48},{64,80},{96,112},{128,144},{160,176},{192,208},{224... | collective-permute-start | bytes 49160 | tf_op jit(solution)/shard_map/ppermute | solution.py:428
  81.0 12.6 %collective-permute-start.13 = (bf16[1,64,128]{2,1,0:T(8,128)(2,1)S(1)}, bf16[1,64,128]{2,1,0:T(8,128)(2,1)S(1)}, u32[]{:S(2)}, u32[]{:S(2)}) collective-permute-start(bf16[1,64,128]{2,1,0:T(8,128)(2,1)S(1)} %get-tuple-element.84), channel_id=1, source_target_pairs={{16,32},{48,64},{80,96},{112,128},{144,160},{176,192},{208,224},{3... | collective-permute-start | bytes 49160 | tf_op jit(solution)/shard_map/ppermute | solution.py:428
  81.6 7.2 %collective-permute-start.14 = (bf16[1,16,128]{2,1,0:T(8,128)(2,1)S(1)}, bf16[1,16,128]{2,1,0:T(8,128)(2,1)S(1)}, u32[]{:S(2)}, u32[]{:S(2)}) collective-permute-start(bf16[1,16,128]{2,1,0:T(8,128)(2,1)S(1)} %get-tuple-element.85), channel_id=1, source_target_pairs={{0,1},{2,3},{4,5},{6,7},{8,9},{10,11},{12,13},{14,15},{1,0},{3,2},... | collective-permute-start | bytes 12296 | tf_op jit(solution)/shard_map/ppermute | solution.py:428
  82.9 6.4 %collective-permute-start.15 = (bf16[1,16,128]{2,1,0:T(8,128)(2,1)S(1)}, bf16[1,16,128]{2,1,0:T(8,128)(2,1)S(1)}, u32[]{:S(2)}, u32[]{:S(2)}) collective-permute-start(bf16[1,16,128]{2,1,0:T(8,128)(2,1)S(1)} %get-tuple-element.86), channel_id=1, source_target_pairs={{1,2},{3,4},{5,6},{7,8},{9,10},{11,12},{13,14},{2,1},{4,3},{6,5},{... | collective-permute-start | bytes 12296 | tf_op jit(solution)/shard_map/ppermute | solution.py:428
  96.4 24.4 %copy-start = (bf16[1,16,4,128,128]{4,3,2,1,0:T(8,128)(2,1)S(1)}, bf16[1,16,4,128,128]{4,3,2,1,0:T(8,128)(2,1)}, u32[]{:S(2)}) copy-start(bf16[1,16,4,128,128]{4,3,2,1,0:T(8,128)(2,1)} %param.28) | copy-start | bytes 6291460
  96.4 36.4 %copy-start.1 = (f32[16,64,128]{2,1,0:T(8,128)S(1)}, f32[16,64,128]{2,1,0:T(8,128)}, u32[]{:S(2)}) copy-start(f32[16,64,128]{2,1,0:T(8,128)} %get-tuple-element.75.diag_hbm.inverse_ref) | copy-start | bytes 1572868

commit v5 on v4

--- a/solution.py
+++ b/solution.py
@@ -9,7 +9,7 @@
 
 ITERS_FLOW = 3
 BIOT = 0.8
-STEPS = (1, 4, 8, 2)
+STEPS = (1, 2, 8, 4)
 F32 = jnp.float32
 BF16 = jnp.bfloat16
 NT = (((1,), (1,)), ((), ()))
@@ -64,12 +64,19 @@
     return high, (x - high.astype(F32)).astype(BF16)
 
 
-def fill_hot(hot_ref, lines):
-    rows = hot_ref.shape[0]
-    ids = iota((rows, 128), 0)
+def fill_hot(hot_ref, lines, width):
+    depth = hot_ref.shape[0] // width
+    shift = width.bit_length() - 1
     for q in range(lines.shape[0]):
-        hit = ids == lines[q : q + 1, :]
-        hot_ref[:, q * 128 : (q + 1) * 128] = jnp.where(hit, 1.0, 0.0).astype(BF16)
+        line = lines[q : q + 1, :]
+        layer = jnp.broadcast_to(line >> shift, (16, 128))
+        place = jnp.where(iota((width, 128), 0) == line & (width - 1), 1.0, 0.0).astype(BF16)
+        for i in range(depth):
+            here = jnp.where(layer == i, 1.0, 0.0).astype(BF16)
+            for j in range(0, width, 16):
+                hot_ref[i * width + j : i * width + j + 16, q * 128 : (q + 1) * 128] = (
+                    place[j : j + 16] * here
+                )
 
 
 def gather_lines(hot_ref, field, out_ref):
@@ -144,7 +151,7 @@
         sems,
     )
     kept_ref[...] = cell_ref[...]
-    fill_hot(hot_ref, cell_ref[...])
+    fill_hot(hot_ref, cell_ref[...], width)
     finish(reads)
     gather_lines(hot_ref, field_ref[...].reshape(depth * width, lateral), out_ref)
     writes = begin([(out_ref, out_hbm)], sems, 4)
@@ -207,7 +214,7 @@
     )
     if last:
         table_reads = begin([(refs[2], refs[4])], sems, 8)
-    fill_hot(hot_ref, cell_ref[...])
+    fill_hot(hot_ref, cell_ref[...], width)
     finish(linked_reads)
     for q in range(incoming_ref.shape[0]):
         turned = turned_ref[q]
@@ -280,14 +287,16 @@
         high, low = halves(lines.T)
         both = jnp.concatenate([high, low], 0)
         side = iota((lateral, 128), 0)
-        for q in range(fault_ref.shape[0]):
-            got = jnp.dot(
-                both, fault_hot_ref[:, q * 128 : (q + 1) * 128], preferred_element_type=F32
+        for q in range(0, fault_ref.shape[0], 2):
+            pair = jnp.dot(
+                both, fault_hot_ref[:, q * 128 : (q + 2) * 128], preferred_element_type=F32
             )
-            got = got[:lateral] + got[lateral:]
-            lane = fault_ref[q : q + 1, :] & 127
-            got = jnp.sum(jnp.where(side == lane, got, 0.0), 0, keepdims=True)
-            face_x_ref[0, q : q + 1, :] = got
+            pair = pair[:lateral] + pair[lateral:]
+            for n in (0, 1):
+                lane = fault_ref[q + n : q + n + 1, :] & 127
+                got = pair[:, n * 128 : (n + 1) * 128]
+                got = jnp.sum(jnp.where(side == lane, got, 0.0), 0, keepdims=True)
+                face_x_ref[0, q + n : q + n + 1, :] = got
         rows = fault_ref.shape[0]
         planes = [
             *halves(face_x_ref[0, :rows, :]),
@@ -327,6 +336,7 @@
 
 
 def contact_kernel(
+    width,
     cols_ref,
     near_ref,
     far_ref,
@@ -344,7 +354,7 @@
     sems,
 ):
     reads = begin([(blocks_hbm, blocks_ref)], sems)
-    fill_hot(fault_hot_ref, fault_ref[...] >> 7)
+    fill_hot(fault_hot_ref, fault_ref[...] >> 7, width)
     writes = begin([(fault_hot_ref, fault_hot_hbm)], sems, 1)
     rows = base_ref.shape[1]
     me = lax.axis_index("col")
@@ -564,18 +574,17 @@
             turned, diag = got[2:4]
             held, outgoing = lax.optimization_barrier((held, outgoing))
         else:
-            near, far, outgoing = lax.optimization_barrier((near, far, outgoing))
+            held, other, outgoing = lax.optimization_barrier((held, other, outgoing))
         incoming = swap(outgoing, "slab")
         sides = exchange(got[-4:])
         if first:
-            near = double(held, "col", STEPS[2])
+            other = paired(held, "col", STEPS[2])
+            other, incoming, sides = lax.optimization_barrier((other, incoming, sides))
+        else:
+            near = jnp.concatenate([held, other], 0)
             far = paired(near, "col", STEPS[3])
-            near, far, incoming, sides = lax.optimization_barrier(
-                (near, far, incoming, sides)
-            )
-        else:
             own, fault_hot = call(
-                contact_kernel,
+                functools.partial(contact_kernel, width),
                 [((4 * rows, 128), F32), ((lines, nodes), BF16, 0)],
                 tile_cols,
                 near,

time: 136 us -> 130 us (0.956)
  waiting for transfers between devices: 20.9 us -> 16.6 us
  blocking collectives: 25.5 us -> 27.3 us
  Pallas kernels: 31.8 us -> 30.2 us
    ppermute x12, waiting for transfers between devices: 13.8 us -> 7.92 us  [exchange(): got.append(lax.ppermute(edge, axis, pairs + [(j, i) for i, j in pairs]))]
    all_to_all x2, blocking collectives: 25.5 us -> 27.3 us  [swap(): return lax.all_to_all(blocks, axis, split_axis=0, concat_axis=0, tiled=True)]
    pallas_call x7, Pallas kernels: 31.8 us -> 30.2 us  [call(): pl.pallas_call(body, in_specs=[pl.BlockSpec(memory_space=space) for space...]
    all_to_all x3, starting transfers between devices: 27.9 us -> 26.4 us  [swap(): return lax.all_to_all(blocks, axis, split_axis=0, concat_axis=0, tiled=True)]
where the time goes in v5:
time: 130 us
  starting transfers between devices  53.8 us (41%)
  Pallas kernels  30.2 us (23%)
  blocking collectives  27.3 us (21%)
  waiting for transfers between devices  16.6 us (13%)
    pallas_call x7, Pallas kernels, call(): pl.pallas_call(body, in_specs=[pl.BlockSpec(memory_space=space) for space...  30.2 us
    all_to_all x2, blocking collectives, swap(): return lax.all_to_all(blocks, axis, split_axis=0, concat_axis=0, tiled=True)  27.3 us
    all_to_all x3, starting transfers between devices, swap(): return lax.all_to_all(blocks, axis, split_axis=0, concat_axis=0, tiled=True)  26.4 us
    ppermute x12, starting transfers between devices, exchange(): got.append(lax.ppermute(edge, axis, pairs + [(j, i) for i, j in pairs]))  22.4 us
    ppermute x12, waiting for transfers between devices, exchange(): got.append(lax.ppermute(edge, axis, pairs + [(j, i) for i, j in pairs]))  7.92 us
    all_to_all x3, waiting for transfers between devices, swap(): return lax.all_to_all(blocks, axis, split_axis=0, concat_axis=0, tiled=True)  5.39 us
    ppermute x4, starting transfers between devices, paired(): lax.ppermute(block, axis, [(i, i ^ apart) for i in range(lax.axis_size(ax...  5.08 us
    ppermute x4, waiting for transfers between devices, paired(): lax.ppermute(block, axis, [(i, i ^ apart) for i in range(lax.axis_size(ax...  3.26 us
  transfers between devices with their start and end apart: 19, of which 9 were waited for; matrix products, arithmetic and copies ran while one was open for 0% of the time, Pallas kernels for 3%

profile of v5, /device:TPU:1, one launch (start us, length us, event | category | flops | bytes accessed | tf_op | source)
XLA Modules:
  0.0 129.7 jit_solution(12492886191062959215)
XLA Ops:
  0.6 0.0 copy-start.7
  0.6 0.7 copy-done.7
  1.3 2.7 %shard_map.166 = (bf16[16,128,128]{2,1,0:T(8,128)(2,1)}, bf16[1,48,128]{2,1,0:T(8,128)(2,1)S(1)}, s32[16,128]{1,0:T(8,128)S(1)}, bf16[2,64,128]{2,1,0:T(8,128)(2...) custom-call(f32[16,64,128]{2,1,0:T(8,128)} %field_hbm.3, ...), custom_call_target="tpu_custom_call" | custom-call | tf_op jit(solution)/shard_map/pallas_call | solution.py:28
  4.1 11.7 %all-to-all-start = ((bf16[16,128,128]{2,1,0:T(8,128)(2,1)}), bf16[16,128,128]{2,1,0:T(8,128)(2,1)S(1)}, u32[]{:S(2)}, u32[]{:S(2)}) async-start(bf16[16,128,128]{2,1,0:T(8,128)(2,1)} %get-tuple-element.50), calls=%async_computation | async-start | bytes 1048576 | tf_op jit(solution)/shard_map/all_to_all | solution.py:451
  15.8 1.0 collective-permute-start
  16.9 0.8 collective-permute-done
  17.7 0.7 collective-permute-start.1
  18.4 0.6 collective-permute-start.4
  19.1 2.5 %collective-permute-start.5 = (bf16[2,16,128]{2,1,0:T(8,128)(2,1)S(1)}, bf16[2,16,128]{2,1,0:T(8,128)(2,1)S(1)}, u32[]{:S(2)}, u32[]{:S(2)}) collective-permute-start(bf16[2,16,128]{2,1,0:T(8,128)(2,1)S(1)} %get-tuple-element.54), channel_id=1, source_target_pairs={{1,2},{3,4},{5,6},{7,8},{9,10},{11,12},{13,14},{2,1},{4,3},{6,5},{... | collective-permute-start | bytes 24584 | tf_op jit(solution)/shard_map/ppermute | solution.py:438
  21.6 2.5 %collective-permute-start.2 = (bf16[2,64,128]{2,1,0:T(8,128)(2,1)S(1)}, bf16[2,64,128]{2,1,0:T(8,128)(2,1)S(1)}, u32[]{:S(2)}, u32[]{:S(2)}) collective-permute-start(bf16[2,64,128]{2,1,0:T(8,128)(2,1)S(1)} %get-tuple-element.51), channel_id=1, source_target_pairs={{0,16},{32,48},{64,80},{96,112},{128,144},{160,176},{192,208},{224... | collective-permute-start | bytes 98312 | tf_op jit(solution)/shard_map/ppermute | solution.py:438
  24.1 0.7 collective-permute-start.3
  24.8 2.4 %collective-permute-done.1 = bf16[2,48,128]{2,1,0:T(8,128)(2,1)S(1)} collective-permute-done((bf16[2,48,128]{2,1,0:T(8,128)(2,1)S(1)}, bf16[2,48,128]{2,1,0:T(8,128)(2,1)S(1)}, u32[]{:S(2)}, u32[]{:S(2)}) %collective-permute-start.1) | collective-permute-done | bytes 24608 | tf_op jit(solution)/shard_map/ppermute | solution.py:443
  27.2 0.0 collective-permute-done.4.x_one.refs_2_
  27.2 1.8 %collective-permute-done.5.x_two.refs_3_ = bf16[2,16,128]{2,1,0:T(8,128)(2,1)S(1)} collective-permute-done((bf16[2,16,128]{2,1,0:T(8,128)(2,1)S(1)}, bf16[2,16,128]{2,1,0:T(8,128)(2,1)S(1)}, u32[]{:S(2)}, u32[]{:S(2)}) %collective-permute-start.5) | collective-permute-done | bytes 8224 | tf_op jit(solution)/shard_map/ppermute | solution.py:438
  29.0 2.0 %collective-permute-done.2.z_one.refs_0_ = bf16[2,64,128]{2,1,0:T(8,128)(2,1)S(1)} collective-permute-done((bf16[2,64,128]{2,1,0:T(8,128)(2,1)S(1)}, bf16[2,64,128]{2,1,0:T(8,128)(2,1)S(1)}, u32[]{:S(2)}, u32[]{:S(2)}) %collective-permute-start.2) | collective-permute-done | bytes 32800 | tf_op jit(solution)/shard_map/ppermute | solution.py:438
  31.0 0.0 collective-permute-done.3.z_two.refs_1_
  31.0 2.1 %all-to-all-done.incoming_ref = bf16[16,128,128]{2,1,0:T(8,128)(2,1)S(1)} async-done(((bf16[16,128,128]{2,1,0:T(8,128)(2,1)}), bf16[16,128,128]{2,1,0:T(8,128)(2,1)S(1)}, u32[]{:S(2)}, u32[]{:S(2)}) %all-to-all-start) | async-done | bytes 524320 | tf_op jit(solution)/shard_map/all_to_all | solution.py:451
  33.0 6.1 %shard_map.167 = (f32[16,64,128]{2,1,0:T(8,128)}, bf16[16,128,128]{2,1,0:T(8,128)(2,1)}, f32[16,128,128]{2,1,0:T(8,128)}, f32[16,64,128]{2,1,0:T(8,128)}, bf16[1...) custom-call(bf16[16,128,128]{2,1,0:T(8,128)(2,1)S(1)} %all-to-all-do, ...), custom_call_target="tpu_custom_call" | custom-call | tf_op jit(solution)/shard_map/pallas_call | solution.py:28
  39.1 0.0 copy-start.8
  39.1 0.0 copy-start.2
  39.1 0.0 copy-start.3
  39.1 0.0 copy-start.4
  39.1 0.0 copy-start.5
  39.2 0.0 copy-start.6
  39.2 6.7 %all-to-all-start.1 = ((bf16[16,128,128]{2,1,0:T(8,128)(2,1)}), bf16[16,128,128]{2,1,0:T(8,128)(2,1)S(1)}, u32[]{:S(2)}, u32[]{:S(2)}) async-start(bf16[16,128,128]{2,1,0:T(8,128)(2,1)} %get-tuple-element.64), calls=%async_computation.1 | async-start | bytes 1048576 | tf_op jit(solution)/shard_map/all_to_all | solution.py:451
  45.8 2.8 %collective-permute-start.6 = (bf16[4,48,128]{2,1,0:T(8,128)(2,1)S(1)}, bf16[4,48,128]{2,1,0:T(8,128)(2,1)S(1)}, u32[]{:S(2)}, u32[]{:S(2)}) collective-permute-start(bf16[4,48,128]{2,1,0:T(8,128)(2,1)S(1)} %pad_maximum_fusion), channel_id=1, source_target_pairs={{0,8},{1,9},{2,10},{3,11},{4,12},{5,13},{6,14},{7,15},{8,0},{9,1},... | collective-permute-start | bytes 147464 | tf_op jit(solution)/shard_map/ppermute | solution.py:443
  48.7 2.2 %collective-permute-start.7 = (bf16[1,64,128]{2,1,0:T(8,128)(2,1)S(1)}, bf16[1,64,128]{2,1,0:T(8,128)(2,1)S(1)}, u32[]{:S(2)}, u32[]{:S(2)}) collective-permute-start(bf16[1,64,128]{2,1,0:T(8,128)(2,1)S(1)} %get-tuple-element.65), channel_id=1, source_target_pairs={{0,16},{32,48},{64,80},{96,112},{128,144},{160,176},{192,208},{224... | collective-permute-start | bytes 49160 | tf_op jit(solution)/shard_map/ppermute | solution.py:438
  50.9 0.7 collective-permute-start.8
  51.5 3.0 %collective-permute-start.9 = (bf16[1,16,128]{2,1,0:T(8,128)(2,1)S(1)}, bf16[1,16,128]{2,1,0:T(8,128)(2,1)S(1)}, u32[]{:S(2)}, u32[]{:S(2)}) collective-permute-start(bf16[1,16,128]{2,1,0:T(8,128)(2,1)S(1)} %get-tuple-element.67), channel_id=1, source_target_pairs={{0,1},{2,3},{4,5},{6,7},{8,9},{10,11},{12,13},{14,15},{1,0},{3,2},... | collective-permute-start | bytes 12296 | tf_op jit(solution)/shard_map/ppermute | solution.py:438
  54.5 2.2 %collective-permute-start.10 = (bf16[1,16,128]{2,1,0:T(8,128)(2,1)S(1)}, bf16[1,16,128]{2,1,0:T(8,128)(2,1)S(1)}, u32[]{:S(2)}, u32[]{:S(2)}) collective-permute-start(bf16[1,16,128]{2,1,0:T(8,128)(2,1)S(1)} %get-tuple-element.68), channel_id=1, source_target_pairs={{1,2},{3,4},{5,6},{7,8},{9,10},{11,12},{13,14},{2,1},{4,3},{6,5},{... | collective-permute-start | bytes 12296 | tf_op jit(solution)/shard_map/ppermute | solution.py:438
  56.7 0.0 collective-permute-done.9.x_one
  56.7 3.0 %collective-permute-done.10.x_two = bf16[1,16,128]{2,1,0:T(8,128)(2,1)S(1)} collective-permute-done((bf16[1,16,128]{2,1,0:T(8,128)(2,1)S(1)}, bf16[1,16,128]{2,1,0:T(8,128)(2,1)S(1)}, u32[]{:S(2)}, u32[]{:S(2)}) %collective-permute-start.10) | collective-permute-done | bytes 4128 | tf_op jit(solution)/shard_map/ppermute | solution.py:438
  59.7 0.0 collective-permute-done.7.z_one
  59.7 0.0 collective-permute-done.8.z_two
  59.7 0.0 collective-permute-done.6
  59.8 1.6 %all-to-all-done.1.incoming_ref = bf16[16,128,128]{2,1,0:T(8,128)(2,1)S(1)} async-done(((bf16[16,128,128]{2,1,0:T(8,128)(2,1)}), bf16[16,128,128]{2,1,0:T(8,128)(2,1)S(1)}, u32[]{:S(2)}, u32[]{:S(2)}) %all-to-all-start.1) | async-done | bytes 524320 | tf_op jit(solution)/shard_map/all_to_all | solution.py:451
  61.3 5.7 %shard_map.168 = (f32[16,64,128]{2,1,0:T(8,128)}, bf16[16,128,128]{2,1,0:T(8,128)(2,1)}, bf16[1,64,128]{2,1,0:T(8,128)(2,1)S(1)}, bf16[1,64,128]{2,1,0:T(8,128)(...) custom-call(bf16[16,128,128]{2,1,0:T(8,128)(2,1)S(1)} %all-to-all-done.1.incoming_ref, ...), custom_call_target="tpu_custom_call" | custom-call | tf_op jit(solution)/shard_map/pallas_call | solution.py:28
  67.1 8.0 %all-to-all-start.2 = ((bf16[16,128,128]{2,1,0:T(8,128)(2,1)}), bf16[16,128,128]{2,1,0:T(8,128)(2,1)S(1)}, u32[]{:S(2)}, u32[]{:S(2)}) async-start(bf16[16,128,128]{2,1,0:T(8,128)(2,1)} %get-tuple-element.79), calls=%async_computation.2 | async-start | bytes 1048576 | tf_op jit(solution)/shard_map/all_to_all | solution.py:451
  75.1 0.5 collective-permute-start.15
  75.5 2.3 %collective-permute-start.11 = (bf16[1,64,128]{2,1,0:T(8,128)(2,1)S(1)}, bf16[1,64,128]{2,1,0:T(8,128)(2,1)S(1)}, u32[]{:S(2)}, u32[]{:S(2)}) collective-permute-start(bf16[1,64,128]{2,1,0:T(8,128)(2,1)S(1)} %get-tuple-element.81), channel_id=1, source_target_pairs={{0,16},{32,48},{64,80},{96,112},{128,144},{160,176},{192,208},{224... | collective-permute-start | bytes 49160 | tf_op jit(solution)/shard_map/ppermute | solution.py:438
  77.8 0.7 collective-permute-start.12
  78.5 1.9 %collective-permute-start.13 = (bf16[1,16,128]{2,1,0:T(8,128)(2,1)S(1)}, bf16[1,16,128]{2,1,0:T(8,128)(2,1)S(1)}, u32[]{:S(2)}, u32[]{:S(2)}) collective-permute-start(bf16[1,16,128]{2,1,0:T(8,128)(2,1)S(1)} %get-tuple-element.83), channel_id=1, source_target_pairs={{0,1},{2,3},{4,5},{6,7},{8,9},{10,11},{12,13},{14,15},{1,0},{3,2},... | collective-permute-start | bytes 12296 | tf_op jit(solution)/shard_map/ppermute | solution.py:438
  80.3 3.2 %collective-permute-start.14 = (bf16[1,16,128]{2,1,0:T(8,128)(2,1)S(1)}, bf16[1,16,128]{2,1,0:T(8,128)(2,1)S(1)}, u32[]{:S(2)}, u32[]{:S(2)}) collective-permute-start(bf16[1,16,128]{2,1,0:T(8,128)(2,1)S(1)} %get-tuple-element.84), channel_id=1, source_target_pairs={{1,2},{3,4},{5,6},{7,8},{9,10},{11,12},{13,14},{2,1},{4,3},{6,5},{... | collective-permute-start | bytes 12296 | tf_op jit(solution)/shard_map/ppermute | solution.py:438
  83.6 0.0 copy-done.8
  83.6 0.1 copy.27.cols_ref
  83.7 0.0 collective-permute-done.15.far_ref
  83.7 0.0 copy-done.2
  83.7 0.0 copy-done.3
  83.7 0.0 copy-done.4
  83.7 0.0 copy-done.5
  83.7 0.0 copy-done.6
  83.7 3.8 %shard_map.169 = (f32[64,128]{1,0:T(8,128)S(1)}, bf16[1024,2048]{1,0:T(8,128)(2,1)}) custom-call(s32[16,4]{1,0:T(8,128)S(1)} %copy.27.cols_ref, bf16[8,48,128]{2,1,0:T(8,128)(2,1)S(1)} %constant_dynamic-update-slice_fusion.near_ref, bf16[8,48,128]{2,1,0:T(8,128)(2,1)S(1)} %collective-permute-done.15.far_ref, bf16[16,4,128,128]{3,2,1,0:T(8,128)(2,1)} %bitcast.15, ...), custom_call_target="tpu_custom_call" | custom-call | tf_op jit(solution)/shard_map/pallas_call | solution.py:28
  87.5 0.0 collective-permute-done.13.x_one
  87.5 1.2 collective-permute-done.14.x_two
  88.7 0.0 collective-permute-done.11.z_one
  88.7 0.0 collective-permute-done.12.z_two
  88.7 1.8 %all-to-all-done.2.incoming_ref = bf16[16,128,128]{2,1,0:T(8,128)(2,1)S(1)} async-done(((bf16[16,128,128]{2,1,0:T(8,128)(2,1)}), bf16[16,128,128]{2,1,0:T(8,128)(2,1)S(1)}, u32[]{:S(2)}, u32[]{:S(2)}) %all-to-all-start.2) | async-done | bytes 524320 | tf_op jit(solution)/shard_map/all_to_all | solution.py:451
  90.4 6.8 %shard_map.170 = (f32[16,64,128]{2,1,0:T(8,128)S(1)}, bf16[1024,2048]{1,0:T(8,128)(2,1)S(1)}, bf16[16,112,128]{2,1,0:T(8,128)(2,1)S(1)}) custom-call(bf16[16,128,128]{2,1,0:T(8,128)(2,1)S(1)} %all-to-all-done.2.incoming_ref, f32[16,128,128]{2,1,0:T(8,128)} %get-tuple-element.71.turned_hbm, f32[16,64,128]{2,1,0:T(8,128)} %get-tuple-element.80.field_hbm, ...), custom_call_target="tpu_custom_call" | custom-call | tf_op jit(solution)/shard_map/pallas_call | solution.py:28
  97.3 18.1 %all_to_all.25.whole_ref = bf16[16,112,128]{2,1,0:T(8,128)(2,1)S(1)} all-to-all(bf16[16,112,128]{2,1,0:T(8,128)(2,1)S(1)} %get-tuple-element.89), channel_id=1, replica_groups=mesh['slab'=16,'col'=16] {'col'}, dimensions={0} | all-to-all | bytes 917504 | tf_op jit(solution)/shard_map/all_to_all | solution.py:451
  115.4 0.0 copy-done
  115.4 2.8 %shard_map.171 = (f32[16,128]{1,0:T(8,128)S(1)}, f32[3,16,128]{2,1,0:T(8,128)}, f32[3,16,128]{2,1,0:T(8,128)}) custom-call(s32[16,4]{1,0:T(8,128)S(1)} %copy.27.cols_ref, bf16[16,112,128]{2,1,0:T(8,128)(2,1)S(1)} %all_to_all.25.whole_ref, bf16[16,4,128,128]{3,2,1,0:T(8,128)(2,1)S(1)} %bitcast.16, f32[3,16,128]{2,1,0:T(8,128)S(1)} %bitcast.18, ...), custom_call_target="tpu_custom_call" | custom-call | tf_op jit(solution)/shard_map/pallas_call | solution.py:28
  118.2 9.2 %all_to_all.26 = f32[16,1,128]{2,1,0:T(1,128)S(1)} all-to-all(f32[16,1,128]{2,1,0:T(1,128)S(1)} %bitcast.30), channel_id=1, replica_groups=mesh['slab'=16,'col'=16] {'col'}, dimensions={0} | all-to-all | bytes 16384 | tf_op jit(solution)/shard_map/all_to_all | solution.py:451
  127.4 0.0 copy-done.1
  127.4 2.2 %shard_map.172 = f32[16,64,128]{2,1,0:T(8,128)} custom-call(f32[16,128]{1,0:T(8,128)S(1)} %bitcast.28, s32[16,128]{1,0:T(8,128)S(1)} %bitcast.23, bf16[1024,2048]{1,0:T(8,128)(2,1)S(1)} %get-tuple-element.91.fault_hot_ref, f32[16,64,128]{2,1,0:T(8,128)S(1)} %get-tuple-element.92.field_ref, f32[16,64,128]{2,1,0:T(8,128)S(1)} %copy-done.1), custom_call_target="tpu_custom_call" | custom-call | tf_op jit(solution)/shard_map/pallas_call | solution.py:28
  (6 shorter events, 0.0 us)
Async XLA Ops:
  0.6 0.7 copy-start.7
  4.1 29.0 %all-to-all-start = ((bf16[16,128,128]{2,1,0:T(8,128)(2,1)}), bf16[16,128,128]{2,1,0:T(8,128)(2,1)S(1)}, u32[]{:S(2)}, u32[]{:S(2)}) async-start(bf16[16,128,128]{2,1,0:T(8,128)(2,1)} %get-tuple-element.50), calls=%async_computation | async-start | bytes 1048576 | tf_op jit(solution)/shard_map/all_to_all | solution.py:451
  15.8 1.9 %collective-permute-start = (bf16[1,48,128]{2,1,0:T(8,128)(2,1)S(1)}, bf16[1,48,128]{2,1,0:T(8,128)(2,1)S(1)}, u32[]{:S(2)}, u32[]{:S(2)}) collective-permute-start(bf16[1,48,128]{2,1,0:T(8,128)(2,1)S(1)} %get-tuple-element.49), channel_id=1, source_target_pairs={{0,1},{1,0},{2,3},{3,2},{4,5},{5,4},{6,7},{7,6},{8,9},{9,8},{10,11... | collective-permute-start | bytes 36872 | tf_op jit(solution)/shard_map/ppermute | solution.py:443
  17.7 9.5 %collective-permute-start.1 = (bf16[2,48,128]{2,1,0:T(8,128)(2,1)S(1)}, bf16[2,48,128]{2,1,0:T(8,128)(2,1)S(1)}, u32[]{:S(2)}, u32[]{:S(2)}) collective-permute-start(bf16[2,48,128]{2,1,0:T(8,128)(2,1)S(1)} %pad_maximum_fusion.1), channel_id=1, source_target_pairs={{0,2},{1,3},{2,0},{3,1},{4,6},{5,7},{6,4},{7,5},{8,10},{9,11},{10,... | collective-permute-start | bytes 73736 | tf_op jit(solution)/shard_map/ppermute | solution.py:443
  18.4 8.8 %collective-permute-start.4 = (bf16[2,16,128]{2,1,0:T(8,128)(2,1)S(1)}, bf16[2,16,128]{2,1,0:T(8,128)(2,1)S(1)}, u32[]{:S(2)}, u32[]{:S(2)}) collective-permute-start(bf16[2,16,128]{2,1,0:T(8,128)(2,1)S(1)} %get-tuple-element.53), channel_id=1, source_target_pairs={{0,1},{2,3},{4,5},{6,7},{8,9},{10,11},{12,13},{14,15},{1,0},{3,2},... | collective-permute-start | bytes 24584 | tf_op jit(solution)/shard_map/ppermute | solution.py:438
  19.1 9.9 %collective-permute-start.5 = (bf16[2,16,128]{2,1,0:T(8,128)(2,1)S(1)}, bf16[2,16,128]{2,1,0:T(8,128)(2,1)S(1)}, u32[]{:S(2)}, u32[]{:S(2)}) collective-permute-start(bf16[2,16,128]{2,1,0:T(8,128)(2,1)S(1)} %get-tuple-element.54), channel_id=1, source_target_pairs={{1,2},{3,4},{5,6},{7,8},{9,10},{11,12},{13,14},{2,1},{4,3},{6,5},{... | collective-permute-start | bytes 24584 | tf_op jit(solution)/shard_map/ppermute | solution.py:438
  21.6 9.4 %collective-permute-start.2 = (bf16[2,64,128]{2,1,0:T(8,128)(2,1)S(1)}, bf16[2,64,128]{2,1,0:T(8,128)(2,1)S(1)}, u32[]{:S(2)}, u32[]{:S(2)}) collective-permute-start(bf16[2,64,128]{2,1,0:T(8,128)(2,1)S(1)} %get-tuple-element.51), channel_id=1, source_target_pairs={{0,16},{32,48},{64,80},{96,112},{128,144},{160,176},{192,208},{224... | collective-permute-start | bytes 98312 | tf_op jit(solution)/shard_map/ppermute | solution.py:438
  24.1 6.8 %collective-permute-start.3 = (bf16[2,64,128]{2,1,0:T(8,128)(2,1)S(1)}, bf16[2,64,128]{2,1,0:T(8,128)(2,1)S(1)}, u32[]{:S(2)}, u32[]{:S(2)}) collective-permute-start(bf16[2,64,128]{2,1,0:T(8,128)(2,1)S(1)} %get-tuple-element.52), channel_id=1, source_target_pairs={{16,32},{48,64},{80,96},{112,128},{144,160},{176,192},{208,224},{3... | collective-permute-start | bytes 98312 | tf_op jit(solution)/shard_map/ppermute | solution.py:438
  39.1 44.5 %copy-start.8 = (s32[1,16,4]{1,2,0:T(4,128)S(1)}, s32[1,16,4]{1,2,0:T(4,128)}, u32[]{:S(2)}) copy-start(s32[1,16,4]{1,2,0:T(4,128)} %param.29) | copy-start | bytes 772
  39.1 44.6 %copy-start.2 = (f32[1,3,2048]{2,0,1:T(1,128)S(1)}, f32[1,3,2048]{2,0,1:T(1,128)}, u32[]{:S(2)}) copy-start(f32[1,3,2048]{2,0,1:T(1,128)} %param.24) | copy-start | bytes 73732
  39.1 44.5 %copy-start.3 = (f32[1,3,2048]{2,0,1:T(1,128)S(1)}, f32[1,3,2048]{2,0,1:T(1,128)}, u32[]{:S(2)}) copy-start(f32[1,3,2048]{2,0,1:T(1,128)} %param.25) | copy-start | bytes 73732
  39.1 44.5 %copy-start.4 = (s32[1,1,16,128]{3,2,1,0:T(8,128)S(1)}, s32[1,1,16,128]{3,2,1,0:T(8,128)}, u32[]{:S(2)}) copy-start(s32[1,1,16,128]{3,2,1,0:T(8,128)} %param.23) | copy-start | bytes 24580
  39.1 44.5 %copy-start.5 = (s32[2,1,2048]{2,1,0:T(1,128)S(1)}, s32[2,1,2048]{2,1,0:T(1,128)}, u32[]{:S(2)}) copy-start(s32[2,1,2048]{2,1,0:T(1,128)} %param.27) | copy-start | bytes 49156
  39.2 44.5 %copy-start.6 = (f32[1,2048]{1,0:T(1,128)S(1)}, f32[1,2048]{1,0:T(1,128)}, u32[]{:S(2)}) copy-start(f32[1,2048]{1,0:T(1,128)} %param.26) | copy-start | bytes 24580
  39.2 22.1 %all-to-all-start.1 = ((bf16[16,128,128]{2,1,0:T(8,128)(2,1)}), bf16[16,128,128]{2,1,0:T(8,128)(2,1)S(1)}, u32[]{:S(2)}, u32[]{:S(2)}) async-start(bf16[16,128,128]{2,1,0:T(8,128)(2,1)} %get-tuple-element.64), calls=%async_computation.1 | async-start | bytes 1048576 | tf_op jit(solution)/shard_map/all_to_all | solution.py:451
  45.8 13.9 %collective-permute-start.6 = (bf16[4,48,128]{2,1,0:T(8,128)(2,1)S(1)}, bf16[4,48,128]{2,1,0:T(8,128)(2,1)S(1)}, u32[]{:S(2)}, u32[]{:S(2)}) collective-permute-start(bf16[4,48,128]{2,1,0:T(8,128)(2,1)S(1)} %pad_maximum_fusion), channel_id=1, source_target_pairs={{0,8},{1,9},{2,10},{3,11},{4,12},{5,13},{6,14},{7,15},{8,0},{9,1},... | collective-permute-start | bytes 147464 | tf_op jit(solution)/shard_map/ppermute | solution.py:443
  48.7 11.1 %collective-permute-start.7 = (bf16[1,64,128]{2,1,0:T(8,128)(2,1)S(1)}, bf16[1,64,128]{2,1,0:T(8,128)(2,1)S(1)}, u32[]{:S(2)}, u32[]{:S(2)}) collective-permute-start(bf16[1,64,128]{2,1,0:T(8,128)(2,1)S(1)} %get-tuple-element.65), channel_id=1, source_target_pairs={{0,16},{32,48},{64,80},{96,112},{128,144},{160,176},{192,208},{224... | collective-permute-start | bytes 49160 | tf_op jit(solution)/shard_map/ppermute | solution.py:438
  50.9 8.9 %collective-permute-start.8 = (bf16[1,64,128]{2,1,0:T(8,128)(2,1)S(1)}, bf16[1,64,128]{2,1,0:T(8,128)(2,1)S(1)}, u32[]{:S(2)}, u32[]{:S(2)}) collective-permute-start(bf16[1,64,128]{2,1,0:T(8,128)(2,1)S(1)} %get-tuple-element.66), channel_id=1, source_target_pairs={{16,32},{48,64},{80,96},{112,128},{144,160},{176,192},{208,224},{3... | collective-permute-start | bytes 49160 | tf_op jit(solution)/shard_map/ppermute | solution.py:438
  51.5 5.2 %collective-permute-start.9 = (bf16[1,16,128]{2,1,0:T(8,128)(2,1)S(1)}, bf16[1,16,128]{2,1,0:T(8,128)(2,1)S(1)}, u32[]{:S(2)}, u32[]{:S(2)}) collective-permute-start(bf16[1,16,128]{2,1,0:T(8,128)(2,1)S(1)} %get-tuple-element.67), channel_id=1, source_target_pairs={{0,1},{2,3},{4,5},{6,7},{8,9},{10,11},{12,13},{14,15},{1,0},{3,2},... | collective-permute-start | bytes 12296 | tf_op jit(solution)/shard_map/ppermute | solution.py:438
  54.5 5.2 %collective-permute-start.10 = (bf16[1,16,128]{2,1,0:T(8,128)(2,1)S(1)}, bf16[1,16,128]{2,1,0:T(8,128)(2,1)S(1)}, u32[]{:S(2)}, u32[]{:S(2)}) collective-permute-start(bf16[1,16,128]{2,1,0:T(8,128)(2,1)S(1)} %get-tuple-element.68), channel_id=1, source_target_pairs={{1,2},{3,4},{5,6},{7,8},{9,10},{11,12},{13,14},{2,1},{4,3},{6,5},{... | collective-permute-start | bytes 12296 | tf_op jit(solution)/shard_map/ppermute | solution.py:438
  67.1 23.4 %all-to-all-start.2 = ((bf16[16,128,128]{2,1,0:T(8,128)(2,1)}), bf16[16,128,128]{2,1,0:T(8,128)(2,1)S(1)}, u32[]{:S(2)}, u32[]{:S(2)}) async-start(bf16[16,128,128]{2,1,0:T(8,128)(2,1)} %get-tuple-element.79), calls=%async_computation.2 | async-start | bytes 1048576 | tf_op jit(solution)/shard_map/all_to_all | solution.py:451
  75.1 8.6 %collective-permute-start.15 = (bf16[8,48,128]{2,1,0:T(8,128)(2,1)S(1)}, bf16[8,48,128]{2,1,0:T(8,128)(2,1)S(1)}, u32[]{:S(2)}, u32[]{:S(2)}) collective-permute-start(bf16[8,48,128]{2,1,0:T(8,128)(2,1)S(1)} %constant_dynamic-update-slice_fusion.near_ref), channel_id=1, source_target_pairs={{0,4},{1,5},{2,6},{3,7},{4,0},{5,1},{6,2},{7,3},{8,12},{9,13},{10,... | collective-permute-start | bytes 294920 | tf_op jit(solution)/shard_map/ppermute | solution.py:443
  75.5 13.1 %collective-permute-start.11 = (bf16[1,64,128]{2,1,0:T(8,128)(2,1)S(1)}, bf16[1,64,128]{2,1,0:T(8,128)(2,1)S(1)}, u32[]{:S(2)}, u32[]{:S(2)}) collective-permute-start(bf16[1,64,128]{2,1,0:T(8,128)(2,1)S(1)} %get-tuple-element.81), channel_id=1, source_target_pairs={{0,16},{32,48},{64,80},{96,112},{128,144},{160,176},{192,208},{224... | collective-permute-start | bytes 49160 | tf_op jit(solution)/shard_map/ppermute | solution.py:438
  77.8 10.9 %collective-permute-start.12 = (bf16[1,64,128]{2,1,0:T(8,128)(2,1)S(1)}, bf16[1,64,128]{2,1,0:T(8,128)(2,1)S(1)}, u32[]{:S(2)}, u32[]{:S(2)}) collective-permute-start(bf16[1,64,128]{2,1,0:T(8,128)(2,1)S(1)} %get-tuple-element.82), channel_id=1, source_target_pairs={{16,32},{48,64},{80,96},{112,128},{144,160},{176,192},{208,224},{3... | collective-permute-start | bytes 49160 | tf_op jit(solution)/shard_map/ppermute | solution.py:438
  78.5 9.0 %collective-permute-start.13 = (bf16[1,16,128]{2,1,0:T(8,128)(2,1)S(1)}, bf16[1,16,128]{2,1,0:T(8,128)(2,1)S(1)}, u32[]{:S(2)}, u32[]{:S(2)}) collective-permute-start(bf16[1,16,128]{2,1,0:T(8,128)(2,1)S(1)} %get-tuple-element.83), channel_id=1, source_target_pairs={{0,1},{2,3},{4,5},{6,7},{8,9},{10,11},{12,13},{14,15},{1,0},{3,2},... | collective-permute-start | bytes 12296 | tf_op jit(solution)/shard_map/ppermute | solution.py:438
  80.3 8.3 %collective-permute-start.14 = (bf16[1,16,128]{2,1,0:T(8,128)(2,1)S(1)}, bf16[1,16,128]{2,1,0:T(8,128)(2,1)S(1)}, u32[]{:S(2)}, u32[]{:S(2)}) collective-permute-start(bf16[1,16,128]{2,1,0:T(8,128)(2,1)S(1)} %get-tuple-element.84), channel_id=1, source_target_pairs={{1,2},{3,4},{5,6},{7,8},{9,10},{11,12},{13,14},{2,1},{4,3},{6,5},{... | collective-permute-start | bytes 12296 | tf_op jit(solution)/shard_map/ppermute | solution.py:438
  90.4 24.9 %copy-start = (bf16[1,16,4,128,128]{4,3,2,1,0:T(8,128)(2,1)S(1)}, bf16[1,16,4,128,128]{4,3,2,1,0:T(8,128)(2,1)}, u32[]{:S(2)}) copy-start(bf16[1,16,4,128,128]{4,3,2,1,0:T(8,128)(2,1)} %param.28) | copy-start | bytes 6291460
  90.4 37.0 %copy-start.1 = (f32[16,64,128]{2,1,0:T(8,128)S(1)}, f32[16,64,128]{2,1,0:T(8,128)}, u32[]{:S(2)}) copy-start(f32[16,64,128]{2,1,0:T(8,128)} %get-tuple-element.73.diag_hbm.inverse_ref) | copy-start | bytes 1572868

commit v6 on v5

--- a/solution.py
+++ b/solution.py
@@ -79,14 +79,18 @@
                 )
 
 
-def gather_lines(hot_ref, field, out_ref):
+def gather_lines(hot_ref, field, out_ref, out_hbm, sems, at):
     turned = field.T.astype(BF16)
+    copies = []
     for q in range(0, out_ref.shape[0], 2):
         got = jnp.dot(
             turned, hot_ref[:, q * 128 : (q + 2) * 128], preferred_element_type=F32
         ).astype(BF16)
         out_ref[q] = got[:, :128]
         out_ref[q + 1] = got[:, 128:]
+        pair = pl.ds(q, 2)
+        copies += begin([(out_ref.at[pair], out_hbm.at[pair])], sems, at + q // 2)
+    return copies
 
 
 def scatter_lines(hot_ref, values_ref):
@@ -153,8 +157,8 @@
     kept_ref[...] = cell_ref[...]
     fill_hot(hot_ref, cell_ref[...], width)
     finish(reads)
-    gather_lines(hot_ref, field_ref[...].reshape(depth * width, lateral), out_ref)
-    writes = begin([(out_ref, out_hbm)], sems, 4)
+    lines = field_ref[...].reshape(depth * width, lateral)
+    writes = gather_lines(hot_ref, lines, out_ref, out_hbm, sems, 4)
     parts, rows, _ = slip_ref.shape
     for p in range(parts):
         ready_ref[0, p * rows : (p + 1) * rows, :] = slip_ref[p].astype(BF16)
@@ -202,6 +206,8 @@
         new_ref, out_ref = refs.pop(), refs.pop()
     faces = [z_one, z_two, x_one, x_two] if first else [refs.pop(0) for _ in range(4)]
     linked_reads = begin([(turned_hbm, turned_ref)], sems)
+    fill_hot(hot_ref, cell_ref[...], width)
+    finish(linked_reads)
     reads = begin(
         list(
             zip(
@@ -214,8 +220,6 @@
     )
     if last:
         table_reads = begin([(refs[2], refs[4])], sems, 8)
-    fill_hot(hot_ref, cell_ref[...], width)
-    finish(linked_reads)
     for q in range(incoming_ref.shape[0]):
         turned = turned_ref[q]
         if first:
@@ -312,8 +316,7 @@
         writes += begin([(new_ref, new_hbm)], sems, 9)
         if first:
             writes += begin([(diag_ref, inverse_out)], sems, 10)
-        gather_lines(hot_ref, lines, out_ref)
-        writes += begin([(out_ref, out_hbm)], sems, 11)
+        writes += gather_lines(hot_ref, lines, out_ref, out_hbm, sems, 11)
         put_edges(new_ref, edge_refs)
     finish(writes)
 
@@ -515,7 +518,7 @@
             pltpu.VMEM(layer, F32),
             pltpu.VMEM(slip0.shape, F32),
             packet,
-            pltpu.SemaphoreType.DMA((5,)),
+            pltpu.SemaphoreType.DMA((4 + slabs // 2,)),
         ),
     )
     incoming = swap(outgoing, "slab")
@@ -563,7 +566,7 @@
                 pltpu.VMEM((slabs, lateral, 128), F32),
                 values,
                 table,
-                pltpu.SemaphoreType.DMA((12,)),
+                pltpu.SemaphoreType.DMA((11 + slabs // 2,)),
             ],
         )
         if last:

time: 130 us -> 135 us (1.038)
  Pallas kernels: 30.2 us -> 34.4 us
    pallas_call x7, Pallas kernels: 30.2 us -> 34.4 us  [call(): pl.pallas_call(body, in_specs=[pl.BlockSpec(memory_space=space) for space...]
where the time goes in v6:
time: 135 us; the launch traced here: 134 us
  starting transfers between devices  53.8 us (40%)
  Pallas kernels  34.4 us (25%)
  blocking collectives  27.3 us (20%)
  waiting for transfers between devices  16.6 us (12%)
    pallas_call x7, Pallas kernels, call(): pl.pallas_call(body, in_specs=[pl.BlockSpec(memory_space=space) for space...  34.4 us
    all_to_all x2, blocking collectives, swap(): return lax.all_to_all(blocks, axis, split_axis=0, concat_axis=0, tiled=True)  27.3 us
    all_to_all x3, starting transfers between devices, swap(): return lax.all_to_all(blocks, axis, split_axis=0, concat_axis=0, tiled=True)  26.4 us
    ppermute x12, starting transfers between devices, exchange(): got.append(lax.ppermute(edge, axis, pairs + [(j, i) for i, j in pairs]))  22.4 us
    ppermute x12, waiting for transfers between devices, exchange(): got.append(lax.ppermute(edge, axis, pairs + [(j, i) for i, j in pairs]))  7.94 us
    all_to_all x3, waiting for transfers between devices, swap(): return lax.all_to_all(blocks, axis, split_axis=0, concat_axis=0, tiled=True)  5.39 us
    ppermute x4, starting transfers between devices, paired(): lax.ppermute(block, axis, [(i, i ^ apart) for i in range(lax.axis_size(ax...  5.08 us
    ppermute x4, waiting for transfers between devices, paired(): lax.ppermute(block, axis, [(i, i ^ apart) for i in range(lax.axis_size(ax...  3.26 us
  transfers between devices with their start and end apart: 19, of which 9 were waited for; matrix products, arithmetic and copies ran while one was open for 0% of the time, Pallas kernels for 3%

profile of v6, /device:TPU:1, one launch (start us, length us, event | category | flops | bytes accessed | tf_op | source)
XLA Modules:
  0.0 133.8 jit_solution(8429152491419176083)
XLA Ops:
  0.6 0.0 copy-start.7
  0.6 0.7 copy-done.7
  1.3 2.6 %shard_map.166 = (bf16[16,128,128]{2,1,0:T(8,128)(2,1)}, bf16[1,48,128]{2,1,0:T(8,128)(2,1)S(1)}, s32[16,128]{1,0:T(8,128)S(1)}, bf16[2,64,128]{2,1,0:T(8,128)(2...) custom-call(f32[16,64,128]{2,1,0:T(8,128)} %field_hbm.3, ...), custom_call_target="tpu_custom_call" | custom-call | tf_op jit(solution)/shard_map/pallas_call | solution.py:28
  4.0 11.7 %all-to-all-start = ((bf16[16,128,128]{2,1,0:T(8,128)(2,1)}), bf16[16,128,128]{2,1,0:T(8,128)(2,1)S(1)}, u32[]{:S(2)}, u32[]{:S(2)}) async-start(bf16[16,128,128]{2,1,0:T(8,128)(2,1)} %get-tuple-element.50), calls=%async_computation | async-start | bytes 1048576 | tf_op jit(solution)/shard_map/all_to_all | solution.py:454
  15.7 1.0 collective-permute-start
  16.8 0.8 collective-permute-done
  17.6 0.7 collective-permute-start.1
  18.4 0.6 collective-permute-start.4
  19.0 2.5 %collective-permute-start.5 = (bf16[2,16,128]{2,1,0:T(8,128)(2,1)S(1)}, bf16[2,16,128]{2,1,0:T(8,128)(2,1)S(1)}, u32[]{:S(2)}, u32[]{:S(2)}) collective-permute-start(bf16[2,16,128]{2,1,0:T(8,128)(2,1)S(1)} %get-tuple-element.54), channel_id=1, source_target_pairs={{1,2},{3,4},{5,6},{7,8},{9,10},{11,12},{13,14},{2,1},{4,3},{6,5},{... | collective-permute-start | bytes 24584 | tf_op jit(solution)/shard_map/ppermute | solution.py:441
  21.5 2.5 %collective-permute-start.2 = (bf16[2,64,128]{2,1,0:T(8,128)(2,1)S(1)}, bf16[2,64,128]{2,1,0:T(8,128)(2,1)S(1)}, u32[]{:S(2)}, u32[]{:S(2)}) collective-permute-start(bf16[2,64,128]{2,1,0:T(8,128)(2,1)S(1)} %get-tuple-element.51), channel_id=1, source_target_pairs={{0,16},{32,48},{64,80},{96,112},{128,144},{160,176},{192,208},{224... | collective-permute-start | bytes 98312 | tf_op jit(solution)/shard_map/ppermute | solution.py:441
  24.0 0.7 collective-permute-start.3
  24.7 2.4 %collective-permute-done.1 = bf16[2,48,128]{2,1,0:T(8,128)(2,1)S(1)} collective-permute-done((bf16[2,48,128]{2,1,0:T(8,128)(2,1)S(1)}, bf16[2,48,128]{2,1,0:T(8,128)(2,1)S(1)}, u32[]{:S(2)}, u32[]{:S(2)}) %collective-permute-start.1) | collective-permute-done | bytes 24608 | tf_op jit(solution)/shard_map/ppermute | solution.py:446
  27.1 0.0 collective-permute-done.4.x_one.refs_2_
  27.2 1.8 %collective-permute-done.5.x_two.refs_3_ = bf16[2,16,128]{2,1,0:T(8,128)(2,1)S(1)} collective-permute-done((bf16[2,16,128]{2,1,0:T(8,128)(2,1)S(1)}, bf16[2,16,128]{2,1,0:T(8,128)(2,1)S(1)}, u32[]{:S(2)}, u32[]{:S(2)}) %collective-permute-start.5) | collective-permute-done | bytes 8224 | tf_op jit(solution)/shard_map/ppermute | solution.py:441
  28.9 2.0 %collective-permute-done.2.z_one.refs_0_ = bf16[2,64,128]{2,1,0:T(8,128)(2,1)S(1)} collective-permute-done((bf16[2,64,128]{2,1,0:T(8,128)(2,1)S(1)}, bf16[2,64,128]{2,1,0:T(8,128)(2,1)S(1)}, u32[]{:S(2)}, u32[]{:S(2)}) %collective-permute-start.2) | collective-permute-done | bytes 32800 | tf_op jit(solution)/shard_map/ppermute | solution.py:441
  30.9 0.0 collective-permute-done.3.z_two.refs_1_
  30.9 2.1 %all-to-all-done.incoming_ref = bf16[16,128,128]{2,1,0:T(8,128)(2,1)S(1)} async-done(((bf16[16,128,128]{2,1,0:T(8,128)(2,1)}), bf16[16,128,128]{2,1,0:T(8,128)(2,1)S(1)}, u32[]{:S(2)}, u32[]{:S(2)}) %all-to-all-start) | async-done | bytes 524320 | tf_op jit(solution)/shard_map/all_to_all | solution.py:454
  32.9 7.1 %shard_map.167 = (f32[16,64,128]{2,1,0:T(8,128)}, bf16[16,128,128]{2,1,0:T(8,128)(2,1)}, f32[16,128,128]{2,1,0:T(8,128)}, f32[16,64,128]{2,1,0:T(8,128)}, bf16[1...) custom-call(bf16[16,128,128]{2,1,0:T(8,128)(2,1)S(1)} %all-to-all-do, ...), custom_call_target="tpu_custom_call" | custom-call | tf_op jit(solution)/shard_map/pallas_call | solution.py:28
  40.1 0.0 copy-start.8
  40.1 0.0 copy-start.2
  40.1 0.0 copy-start.3
  40.1 0.0 copy-start.4
  40.1 0.0 copy-start.5
  40.1 0.0 copy-start.6
  40.1 6.7 %all-to-all-start.1 = ((bf16[16,128,128]{2,1,0:T(8,128)(2,1)}), bf16[16,128,128]{2,1,0:T(8,128)(2,1)S(1)}, u32[]{:S(2)}, u32[]{:S(2)}) async-start(bf16[16,128,128]{2,1,0:T(8,128)(2,1)} %get-tuple-element.64), calls=%async_computation.1 | async-start | bytes 1048576 | tf_op jit(solution)/shard_map/all_to_all | solution.py:454
  46.8 2.8 %collective-permute-start.6 = (bf16[4,48,128]{2,1,0:T(8,128)(2,1)S(1)}, bf16[4,48,128]{2,1,0:T(8,128)(2,1)S(1)}, u32[]{:S(2)}, u32[]{:S(2)}) collective-permute-start(bf16[4,48,128]{2,1,0:T(8,128)(2,1)S(1)} %pad_maximum_fusion), channel_id=1, source_target_pairs={{0,8},{1,9},{2,10},{3,11},{4,12},{5,13},{6,14},{7,15},{8,0},{9,1},... | collective-permute-start | bytes 147464 | tf_op jit(solution)/shard_map/ppermute | solution.py:446
  49.6 2.2 %collective-permute-start.7 = (bf16[1,64,128]{2,1,0:T(8,128)(2,1)S(1)}, bf16[1,64,128]{2,1,0:T(8,128)(2,1)S(1)}, u32[]{:S(2)}, u32[]{:S(2)}) collective-permute-start(bf16[1,64,128]{2,1,0:T(8,128)(2,1)S(1)} %get-tuple-element.65), channel_id=1, source_target_pairs={{0,16},{32,48},{64,80},{96,112},{128,144},{160,176},{192,208},{224... | collective-permute-start | bytes 49160 | tf_op jit(solution)/shard_map/ppermute | solution.py:441
  51.8 0.7 collective-permute-start.8
  52.5 3.0 %collective-permute-start.9 = (bf16[1,16,128]{2,1,0:T(8,128)(2,1)S(1)}, bf16[1,16,128]{2,1,0:T(8,128)(2,1)S(1)}, u32[]{:S(2)}, u32[]{:S(2)}) collective-permute-start(bf16[1,16,128]{2,1,0:T(8,128)(2,1)S(1)} %get-tuple-element.67), channel_id=1, source_target_pairs={{0,1},{2,3},{4,5},{6,7},{8,9},{10,11},{12,13},{14,15},{1,0},{3,2},... | collective-permute-start | bytes 12296 | tf_op jit(solution)/shard_map/ppermute | solution.py:441
  55.5 2.2 %collective-permute-start.10 = (bf16[1,16,128]{2,1,0:T(8,128)(2,1)S(1)}, bf16[1,16,128]{2,1,0:T(8,128)(2,1)S(1)}, u32[]{:S(2)}, u32[]{:S(2)}) collective-permute-start(bf16[1,16,128]{2,1,0:T(8,128)(2,1)S(1)} %get-tuple-element.68), channel_id=1, source_target_pairs={{1,2},{3,4},{5,6},{7,8},{9,10},{11,12},{13,14},{2,1},{4,3},{6,5},{... | collective-permute-start | bytes 12296 | tf_op jit(solution)/shard_map/ppermute | solution.py:441
  57.7 0.0 collective-permute-done.9.x_one
  57.7 3.0 %collective-permute-done.10.x_two = bf16[1,16,128]{2,1,0:T(8,128)(2,1)S(1)} collective-permute-done((bf16[1,16,128]{2,1,0:T(8,128)(2,1)S(1)}, bf16[1,16,128]{2,1,0:T(8,128)(2,1)S(1)}, u32[]{:S(2)}, u32[]{:S(2)}) %collective-permute-start.10) | collective-permute-done | bytes 4128 | tf_op jit(solution)/shard_map/ppermute | solution.py:441
  60.7 0.0 collective-permute-done.7.z_one
  60.7 0.0 collective-permute-done.8.z_two
  60.7 0.0 collective-permute-done.6
  60.7 1.6 %all-to-all-done.1.incoming_ref = bf16[16,128,128]{2,1,0:T(8,128)(2,1)S(1)} async-done(((bf16[16,128,128]{2,1,0:T(8,128)(2,1)}), bf16[16,128,128]{2,1,0:T(8,128)(2,1)S(1)}, u32[]{:S(2)}, u32[]{:S(2)}) %all-to-all-start.1) | async-done | bytes 524320 | tf_op jit(solution)/shard_map/all_to_all | solution.py:454
  62.3 6.8 %shard_map.168 = (f32[16,64,128]{2,1,0:T(8,128)}, bf16[16,128,128]{2,1,0:T(8,128)(2,1)}, bf16[1,64,128]{2,1,0:T(8,128)(2,1)S(1)}, bf16[1,64,128]{2,1,0:T(8,128)(...) custom-call(bf16[16,128,128]{2,1,0:T(8,128)(2,1)S(1)} %all-to-all-done.1.incoming_ref, ...), custom_call_target="tpu_custom_call" | custom-call | tf_op jit(solution)/shard_map/pallas_call | solution.py:28
  69.1 8.0 %all-to-all-start.2 = ((bf16[16,128,128]{2,1,0:T(8,128)(2,1)}), bf16[16,128,128]{2,1,0:T(8,128)(2,1)S(1)}, u32[]{:S(2)}, u32[]{:S(2)}) async-start(bf16[16,128,128]{2,1,0:T(8,128)(2,1)} %get-tuple-element.79), calls=%async_computation.2 | async-start | bytes 1048576 | tf_op jit(solution)/shard_map/all_to_all | solution.py:454
  77.1 0.5 collective-permute-start.15
  77.6 2.3 %collective-permute-start.11 = (bf16[1,64,128]{2,1,0:T(8,128)(2,1)S(1)}, bf16[1,64,128]{2,1,0:T(8,128)(2,1)S(1)}, u32[]{:S(2)}, u32[]{:S(2)}) collective-permute-start(bf16[1,64,128]{2,1,0:T(8,128)(2,1)S(1)} %get-tuple-element.81), channel_id=1, source_target_pairs={{0,16},{32,48},{64,80},{96,112},{128,144},{160,176},{192,208},{224... | collective-permute-start | bytes 49160 | tf_op jit(solution)/shard_map/ppermute | solution.py:441
  79.8 0.7 collective-permute-start.12
  80.5 1.8 %collective-permute-start.13 = (bf16[1,16,128]{2,1,0:T(8,128)(2,1)S(1)}, bf16[1,16,128]{2,1,0:T(8,128)(2,1)S(1)}, u32[]{:S(2)}, u32[]{:S(2)}) collective-permute-start(bf16[1,16,128]{2,1,0:T(8,128)(2,1)S(1)} %get-tuple-element.83), channel_id=1, source_target_pairs={{0,1},{2,3},{4,5},{6,7},{8,9},{10,11},{12,13},{14,15},{1,0},{3,2},... | collective-permute-start | bytes 12296 | tf_op jit(solution)/shard_map/ppermute | solution.py:441
  82.3 3.3 %collective-permute-start.14 = (bf16[1,16,128]{2,1,0:T(8,128)(2,1)S(1)}, bf16[1,16,128]{2,1,0:T(8,128)(2,1)S(1)}, u32[]{:S(2)}, u32[]{:S(2)}) collective-permute-start(bf16[1,16,128]{2,1,0:T(8,128)(2,1)S(1)} %get-tuple-element.84), channel_id=1, source_target_pairs={{1,2},{3,4},{5,6},{7,8},{9,10},{11,12},{13,14},{2,1},{4,3},{6,5},{... | collective-permute-start | bytes 12296 | tf_op jit(solution)/shard_map/ppermute | solution.py:441
  85.6 0.0 copy-done.8
  85.6 0.1 copy.27.cols_ref
  85.7 0.0 collective-permute-done.15.far_ref
  85.7 0.0 copy-done.2
  85.7 0.0 copy-done.3
  85.7 0.0 copy-done.4
  85.7 0.0 copy-done.5
  85.7 0.0 copy-done.6
  85.7 3.8 %shard_map.169 = (f32[64,128]{1,0:T(8,128)S(1)}, bf16[1024,2048]{1,0:T(8,128)(2,1)}) custom-call(s32[16,4]{1,0:T(8,128)S(1)} %copy.27.cols_ref, bf16[8,48,128]{2,1,0:T(8,128)(2,1)S(1)} %constant_dynamic-update-slice_fusion.near_ref, bf16[8,48,128]{2,1,0:T(8,128)(2,1)S(1)} %collective-permute-done.15.far_ref, bf16[16,4,128,128]{3,2,1,0:T(8,128)(2,1)} %bitcast.15, ...), custom_call_target="tpu_custom_call" | custom-call | tf_op jit(solution)/shard_map/pallas_call | solution.py:28
  89.5 0.0 collective-permute-done.13.x_one
  89.5 1.2 collective-permute-done.14.x_two
  90.7 0.0 collective-permute-done.11.z_one
  90.7 0.0 collective-permute-done.12.z_two
  90.7 1.8 %all-to-all-done.2.incoming_ref = bf16[16,128,128]{2,1,0:T(8,128)(2,1)S(1)} async-done(((bf16[16,128,128]{2,1,0:T(8,128)(2,1)}), bf16[16,128,128]{2,1,0:T(8,128)(2,1)S(1)}, u32[]{:S(2)}, u32[]{:S(2)}) %all-to-all-start.2) | async-done | bytes 524320 | tf_op jit(solution)/shard_map/all_to_all | solution.py:454
  92.5 9.0 %shard_map.170 = (f32[16,64,128]{2,1,0:T(8,128)S(1)}, bf16[1024,2048]{1,0:T(8,128)(2,1)S(1)}, bf16[16,112,128]{2,1,0:T(8,128)(2,1)S(1)}) custom-call(bf16[16,128,128]{2,1,0:T(8,128)(2,1)S(1)} %all-to-all-done.2.incoming_ref, f32[16,128,128]{2,1,0:T(8,128)} %get-tuple-element.71.turned_hbm, f32[16,64,128]{2,1,0:T(8,128)} %get-tuple-element.80.field_hbm, ...), custom_call_target="tpu_custom_call" | custom-call | tf_op jit(solution)/shard_map/pallas_call | solution.py:28
  101.5 18.1 %all_to_all.25.whole_ref = bf16[16,112,128]{2,1,0:T(8,128)(2,1)S(1)} all-to-all(bf16[16,112,128]{2,1,0:T(8,128)(2,1)S(1)} %get-tuple-element.89), channel_id=1, replica_groups=mesh['slab'=16,'col'=16] {'col'}, dimensions={0} | all-to-all | bytes 917504 | tf_op jit(solution)/shard_map/all_to_all | solution.py:454
  119.6 0.0 copy-done
  119.6 2.8 %shard_map.171 = (f32[16,128]{1,0:T(8,128)S(1)}, f32[3,16,128]{2,1,0:T(8,128)}, f32[3,16,128]{2,1,0:T(8,128)}) custom-call(s32[16,4]{1,0:T(8,128)S(1)} %copy.27.cols_ref, bf16[16,112,128]{2,1,0:T(8,128)(2,1)S(1)} %all_to_all.25.whole_ref, bf16[16,4,128,128]{3,2,1,0:T(8,128)(2,1)S(1)} %bitcast.16, f32[3,16,128]{2,1,0:T(8,128)S(1)} %bitcast.18, ...), custom_call_target="tpu_custom_call" | custom-call | tf_op jit(solution)/shard_map/pallas_call | solution.py:28
  122.4 9.2 %all_to_all.26 = f32[16,1,128]{2,1,0:T(1,128)S(1)} all-to-all(f32[16,1,128]{2,1,0:T(1,128)S(1)} %bitcast.30), channel_id=1, replica_groups=mesh['slab'=16,'col'=16] {'col'}, dimensions={0} | all-to-all | bytes 16384 | tf_op jit(solution)/shard_map/all_to_all | solution.py:454
  131.6 0.0 copy-done.1
  131.6 2.2 %shard_map.172 = f32[16,64,128]{2,1,0:T(8,128)} custom-call(f32[16,128]{1,0:T(8,128)S(1)} %bitcast.28, s32[16,128]{1,0:T(8,128)S(1)} %bitcast.23, bf16[1024,2048]{1,0:T(8,128)(2,1)S(1)} %get-tuple-element.91.fault_hot_ref, f32[16,64,128]{2,1,0:T(8,128)S(1)} %get-tuple-element.92.field_ref, f32[16,64,128]{2,1,0:T(8,128)S(1)} %copy-done.1), custom_call_target="tpu_custom_call" | custom-call | tf_op jit(solution)/shard_map/pallas_call | solution.py:28
  (6 shorter events, 0.0 us)
Async XLA Ops:
  0.6 0.7 copy-start.7
  4.0 29.0 %all-to-all-start = ((bf16[16,128,128]{2,1,0:T(8,128)(2,1)}), bf16[16,128,128]{2,1,0:T(8,128)(2,1)S(1)}, u32[]{:S(2)}, u32[]{:S(2)}) async-start(bf16[16,128,128]{2,1,0:T(8,128)(2,1)} %get-tuple-element.50), calls=%async_computation | async-start | bytes 1048576 | tf_op jit(solution)/shard_map/all_to_all | solution.py:454
  15.7 1.9 %collective-permute-start = (bf16[1,48,128]{2,1,0:T(8,128)(2,1)S(1)}, bf16[1,48,128]{2,1,0:T(8,128)(2,1)S(1)}, u32[]{:S(2)}, u32[]{:S(2)}) collective-permute-start(bf16[1,48,128]{2,1,0:T(8,128)(2,1)S(1)} %get-tuple-element.49), channel_id=1, source_target_pairs={{0,1},{1,0},{2,3},{3,2},{4,5},{5,4},{6,7},{7,6},{8,9},{9,8},{10,11... | collective-permute-start | bytes 36872 | tf_op jit(solution)/shard_map/ppermute | solution.py:446
  17.6 9.5 %collective-permute-start.1 = (bf16[2,48,128]{2,1,0:T(8,128)(2,1)S(1)}, bf16[2,48,128]{2,1,0:T(8,128)(2,1)S(1)}, u32[]{:S(2)}, u32[]{:S(2)}) collective-permute-start(bf16[2,48,128]{2,1,0:T(8,128)(2,1)S(1)} %pad_maximum_fusion.1), channel_id=1, source_target_pairs={{0,2},{1,3},{2,0},{3,1},{4,6},{5,7},{6,4},{7,5},{8,10},{9,11},{10,... | collective-permute-start | bytes 73736 | tf_op jit(solution)/shard_map/ppermute | solution.py:446
  18.4 8.8 %collective-permute-start.4 = (bf16[2,16,128]{2,1,0:T(8,128)(2,1)S(1)}, bf16[2,16,128]{2,1,0:T(8,128)(2,1)S(1)}, u32[]{:S(2)}, u32[]{:S(2)}) collective-permute-start(bf16[2,16,128]{2,1,0:T(8,128)(2,1)S(1)} %get-tuple-element.53), channel_id=1, source_target_pairs={{0,1},{2,3},{4,5},{6,7},{8,9},{10,11},{12,13},{14,15},{1,0},{3,2},... | collective-permute-start | bytes 24584 | tf_op jit(solution)/shard_map/ppermute | solution.py:441
  19.0 9.9 %collective-permute-start.5 = (bf16[2,16,128]{2,1,0:T(8,128)(2,1)S(1)}, bf16[2,16,128]{2,1,0:T(8,128)(2,1)S(1)}, u32[]{:S(2)}, u32[]{:S(2)}) collective-permute-start(bf16[2,16,128]{2,1,0:T(8,128)(2,1)S(1)} %get-tuple-element.54), channel_id=1, source_target_pairs={{1,2},{3,4},{5,6},{7,8},{9,10},{11,12},{13,14},{2,1},{4,3},{6,5},{... | collective-permute-start | bytes 24584 | tf_op jit(solution)/shard_map/ppermute | solution.py:441
  21.5 9.4 %collective-permute-start.2 = (bf16[2,64,128]{2,1,0:T(8,128)(2,1)S(1)}, bf16[2,64,128]{2,1,0:T(8,128)(2,1)S(1)}, u32[]{:S(2)}, u32[]{:S(2)}) collective-permute-start(bf16[2,64,128]{2,1,0:T(8,128)(2,1)S(1)} %get-tuple-element.51), channel_id=1, source_target_pairs={{0,16},{32,48},{64,80},{96,112},{128,144},{160,176},{192,208},{224... | collective-permute-start | bytes 98312 | tf_op jit(solution)/shard_map/ppermute | solution.py:441
  24.0 6.8 %collective-permute-start.3 = (bf16[2,64,128]{2,1,0:T(8,128)(2,1)S(1)}, bf16[2,64,128]{2,1,0:T(8,128)(2,1)S(1)}, u32[]{:S(2)}, u32[]{:S(2)}) collective-permute-start(bf16[2,64,128]{2,1,0:T(8,128)(2,1)S(1)} %get-tuple-element.52), channel_id=1, source_target_pairs={{16,32},{48,64},{80,96},{112,128},{144,160},{176,192},{208,224},{3... | collective-permute-start | bytes 98312 | tf_op jit(solution)/shard_map/ppermute | solution.py:441
  40.1 45.5 %copy-start.8 = (s32[1,16,4]{1,2,0:T(4,128)S(1)}, s32[1,16,4]{1,2,0:T(4,128)}, u32[]{:S(2)}) copy-start(s32[1,16,4]{1,2,0:T(4,128)} %param.29) | copy-start | bytes 772
  40.1 45.6 %copy-start.2 = (f32[1,3,2048]{2,0,1:T(1,128)S(1)}, f32[1,3,2048]{2,0,1:T(1,128)}, u32[]{:S(2)}) copy-start(f32[1,3,2048]{2,0,1:T(1,128)} %param.24) | copy-start | bytes 73732
  40.1 45.6 %copy-start.3 = (f32[1,3,2048]{2,0,1:T(1,128)S(1)}, f32[1,3,2048]{2,0,1:T(1,128)}, u32[]{:S(2)}) copy-start(f32[1,3,2048]{2,0,1:T(1,128)} %param.25) | copy-start | bytes 73732
  40.1 45.6 %copy-start.4 = (s32[1,1,16,128]{3,2,1,0:T(8,128)S(1)}, s32[1,1,16,128]{3,2,1,0:T(8,128)}, u32[]{:S(2)}) copy-start(s32[1,1,16,128]{3,2,1,0:T(8,128)} %param.23) | copy-start | bytes 24580
  40.1 45.6 %copy-start.5 = (s32[2,1,2048]{2,1,0:T(1,128)S(1)}, s32[2,1,2048]{2,1,0:T(1,128)}, u32[]{:S(2)}) copy-start(s32[2,1,2048]{2,1,0:T(1,128)} %param.27) | copy-start | bytes 49156
  40.1 45.6 %copy-start.6 = (f32[1,2048]{1,0:T(1,128)S(1)}, f32[1,2048]{1,0:T(1,128)}, u32[]{:S(2)}) copy-start(f32[1,2048]{1,0:T(1,128)} %param.26) | copy-start | bytes 24580
  40.1 22.1 %all-to-all-start.1 = ((bf16[16,128,128]{2,1,0:T(8,128)(2,1)}), bf16[16,128,128]{2,1,0:T(8,128)(2,1)S(1)}, u32[]{:S(2)}, u32[]{:S(2)}) async-start(bf16[16,128,128]{2,1,0:T(8,128)(2,1)} %get-tuple-element.64), calls=%async_computation.1 | async-start | bytes 1048576 | tf_op jit(solution)/shard_map/all_to_all | solution.py:454
  46.8 13.9 %collective-permute-start.6 = (bf16[4,48,128]{2,1,0:T(8,128)(2,1)S(1)}, bf16[4,48,128]{2,1,0:T(8,128)(2,1)S(1)}, u32[]{:S(2)}, u32[]{:S(2)}) collective-permute-start(bf16[4,48,128]{2,1,0:T(8,128)(2,1)S(1)} %pad_maximum_fusion), channel_id=1, source_target_pairs={{0,8},{1,9},{2,10},{3,11},{4,12},{5,13},{6,14},{7,15},{8,0},{9,1},... | collective-permute-start | bytes 147464 | tf_op jit(solution)/shard_map/ppermute | solution.py:446
  49.6 11.1 %collective-permute-start.7 = (bf16[1,64,128]{2,1,0:T(8,128)(2,1)S(1)}, bf16[1,64,128]{2,1,0:T(8,128)(2,1)S(1)}, u32[]{:S(2)}, u32[]{:S(2)}) collective-permute-start(bf16[1,64,128]{2,1,0:T(8,128)(2,1)S(1)} %get-tuple-element.65), channel_id=1, source_target_pairs={{0,16},{32,48},{64,80},{96,112},{128,144},{160,176},{192,208},{224... | collective-permute-start | bytes 49160 | tf_op jit(solution)/shard_map/ppermute | solution.py:441
  51.8 8.9 %collective-permute-start.8 = (bf16[1,64,128]{2,1,0:T(8,128)(2,1)S(1)}, bf16[1,64,128]{2,1,0:T(8,128)(2,1)S(1)}, u32[]{:S(2)}, u32[]{:S(2)}) collective-permute-start(bf16[1,64,128]{2,1,0:T(8,128)(2,1)S(1)} %get-tuple-element.66), channel_id=1, source_target_pairs={{16,32},{48,64},{80,96},{112,128},{144,160},{176,192},{208,224},{3... | collective-permute-start | bytes 49160 | tf_op jit(solution)/shard_map/ppermute | solution.py:441
  52.5 5.2 %collective-permute-start.9 = (bf16[1,16,128]{2,1,0:T(8,128)(2,1)S(1)}, bf16[1,16,128]{2,1,0:T(8,128)(2,1)S(1)}, u32[]{:S(2)}, u32[]{:S(2)}) collective-permute-start(bf16[1,16,128]{2,1,0:T(8,128)(2,1)S(1)} %get-tuple-element.67), channel_id=1, source_target_pairs={{0,1},{2,3},{4,5},{6,7},{8,9},{10,11},{12,13},{14,15},{1,0},{3,2},... | collective-permute-start | bytes 12296 | tf_op jit(solution)/shard_map/ppermute | solution.py:441
  55.5 5.2 %collective-permute-start.10 = (bf16[1,16,128]{2,1,0:T(8,128)(2,1)S(1)}, bf16[1,16,128]{2,1,0:T(8,128)(2,1)S(1)}, u32[]{:S(2)}, u32[]{:S(2)}) collective-permute-start(bf16[1,16,128]{2,1,0:T(8,128)(2,1)S(1)} %get-tuple-element.68), channel_id=1, source_target_pairs={{1,2},{3,4},{5,6},{7,8},{9,10},{11,12},{13,14},{2,1},{4,3},{6,5},{... | collective-permute-start | bytes 12296 | tf_op jit(solution)/shard_map/ppermute | solution.py:441
  69.1 23.4 %all-to-all-start.2 = ((bf16[16,128,128]{2,1,0:T(8,128)(2,1)}), bf16[16,128,128]{2,1,0:T(8,128)(2,1)S(1)}, u32[]{:S(2)}, u32[]{:S(2)}) async-start(bf16[16,128,128]{2,1,0:T(8,128)(2,1)} %get-tuple-element.79), calls=%async_computation.2 | async-start | bytes 1048576 | tf_op jit(solution)/shard_map/all_to_all | solution.py:454
  77.1 8.6 %collective-permute-start.15 = (bf16[8,48,128]{2,1,0:T(8,128)(2,1)S(1)}, bf16[8,48,128]{2,1,0:T(8,128)(2,1)S(1)}, u32[]{:S(2)}, u32[]{:S(2)}) collective-permute-start(bf16[8,48,128]{2,1,0:T(8,128)(2,1)S(1)} %constant_dynamic-update-slice_fusion.near_ref), channel_id=1, source_target_pairs={{0,4},{1,5},{2,6},{3,7},{4,0},{5,1},{6,2},{7,3},{8,12},{9,13},{10,... | collective-permute-start | bytes 294920 | tf_op jit(solution)/shard_map/ppermute | solution.py:446
  77.6 13.1 %collective-permute-start.11 = (bf16[1,64,128]{2,1,0:T(8,128)(2,1)S(1)}, bf16[1,64,128]{2,1,0:T(8,128)(2,1)S(1)}, u32[]{:S(2)}, u32[]{:S(2)}) collective-permute-start(bf16[1,64,128]{2,1,0:T(8,128)(2,1)S(1)} %get-tuple-element.81), channel_id=1, source_target_pairs={{0,16},{32,48},{64,80},{96,112},{128,144},{160,176},{192,208},{224... | collective-permute-start | bytes 49160 | tf_op jit(solution)/shard_map/ppermute | solution.py:441
  79.8 10.9 %collective-permute-start.12 = (bf16[1,64,128]{2,1,0:T(8,128)(2,1)S(1)}, bf16[1,64,128]{2,1,0:T(8,128)(2,1)S(1)}, u32[]{:S(2)}, u32[]{:S(2)}) collective-permute-start(bf16[1,64,128]{2,1,0:T(8,128)(2,1)S(1)} %get-tuple-element.82), channel_id=1, source_target_pairs={{16,32},{48,64},{80,96},{112,128},{144,160},{176,192},{208,224},{3... | collective-permute-start | bytes 49160 | tf_op jit(solution)/shard_map/ppermute | solution.py:441
  80.5 9.0 %collective-permute-start.13 = (bf16[1,16,128]{2,1,0:T(8,128)(2,1)S(1)}, bf16[1,16,128]{2,1,0:T(8,128)(2,1)S(1)}, u32[]{:S(2)}, u32[]{:S(2)}) collective-permute-start(bf16[1,16,128]{2,1,0:T(8,128)(2,1)S(1)} %get-tuple-element.83), channel_id=1, source_target_pairs={{0,1},{2,3},{4,5},{6,7},{8,9},{10,11},{12,13},{14,15},{1,0},{3,2},... | collective-permute-start | bytes 12296 | tf_op jit(solution)/shard_map/ppermute | solution.py:441
  82.3 8.4 %collective-permute-start.14 = (bf16[1,16,128]{2,1,0:T(8,128)(2,1)S(1)}, bf16[1,16,128]{2,1,0:T(8,128)(2,1)S(1)}, u32[]{:S(2)}, u32[]{:S(2)}) collective-permute-start(bf16[1,16,128]{2,1,0:T(8,128)(2,1)S(1)} %get-tuple-element.84), channel_id=1, source_target_pairs={{1,2},{3,4},{5,6},{7,8},{9,10},{11,12},{13,14},{2,1},{4,3},{6,5},{... | collective-permute-start | bytes 12296 | tf_op jit(solution)/shard_map/ppermute | solution.py:441
  92.5 27.1 %copy-start = (bf16[1,16,4,128,128]{4,3,2,1,0:T(8,128)(2,1)S(1)}, bf16[1,16,4,128,128]{4,3,2,1,0:T(8,128)(2,1)}, u32[]{:S(2)}) copy-start(bf16[1,16,4,128,128]{4,3,2,1,0:T(8,128)(2,1)} %param.28) | copy-start | bytes 6291460
  92.5 39.1 %copy-start.1 = (f32[16,64,128]{2,1,0:T(8,128)S(1)}, f32[16,64,128]{2,1,0:T(8,128)}, u32[]{:S(2)}) copy-start(f32[16,64,128]{2,1,0:T(8,128)} %get-tuple-element.73.diag_hbm.inverse_ref) | copy-start | bytes 1572868
